TPU v7x, 32 devices: a whole 2x2x4 slice. The times are simulated.
32 devices in a mesh: dp: 8 (over z, x), mp: 4 (over y, core).
Axes of the slice: x: 2, y: 2, z: 4, core: 2. Of those that a mesh axis runs over, the one named last changes fastest.
Arguments:
- block_input: bfloat16 [2, 8192, 512], P(None, 'dp'), may hold values from -6 to 6
- out_cotangent: bfloat16 [2, 8192, 512], P(None, 'dp'), may hold values from -6 to 6
- early_up: bfloat16 [512, 2048], P('dp', 'mp'), may hold values from -0.25 to 0.25
- early_down: bfloat16 [2048, 512], P('mp', 'dp'), may hold values from -0.125 to 0.125
- attention_in: bfloat16 [3, 512, 512], P(None, 'dp', 'mp'), may hold values from -0.25 to 0.25
- attention_out: bfloat16 [512, 512], P('mp', 'dp'), may hold values from -6 to 6
- relative_bias: bfloat16 [8, 4096], P('mp', 'dp'), may hold values from -6 to 300
- pointwise_in: bfloat16 [2, 512, 512], P(None, 'dp', 'mp'), may hold values from -0.25 to 0.25
- depthwise: bfloat16 [512, 31], P(('mp', 'dp')), may hold values from -1 to 1
- batch_norm: bfloat16 [2, 512], P(None, ('mp', 'dp')), may hold values from 0.5 to 1.5
- pointwise_out: bfloat16 [512, 512], P('mp', 'dp'), may hold values from -0.25 to 0.25
- late_up: bfloat16 [512, 2048], P('dp', 'mp'), may hold values from -0.25 to 0.25
- late_down: bfloat16 [2048, 512], P('mp', 'dp'), may hold values from -0.125 to 0.125
- norm_gains: bfloat16 [5, 512], P(None, 'dp'), may hold values from 0.5 to 1.5
Outputs:
- block_output: bfloat16 [2, 8192, 512], P(None, ('dp', 'mp'))
- input_grad: float32 [2, 8192, 512], P(None, ('dp', 'mp'))
- early_up_grad: float32 [512, 2048], P('dp', 'mp')
- early_down_grad: float32 [2048, 512], P('mp', 'dp')
- attention_in_grad: float32 [3, 512, 512], P(None, 'dp', 'mp')
- attention_out_grad: float32 [512, 512], P('mp', 'dp')
- relative_bias_grad: float32 [8, 4096], P('mp', 'dp')
- pointwise_in_grad: float32 [2, 512, 512], P(None, 'dp', 'mp')
- depthwise_grad: float32 [512, 31], P(('mp', 'dp'))
- batch_norm_grad: float32 [2, 512], P(None, ('mp', 'dp'))
- pointwise_out_grad: float32 [512, 512], P('mp', 'dp')
- late_up_grad: float32 [512, 2048], P('dp', 'mp')
- late_down_grad: float32 [2048, 512], P('mp', 'dp')
- norm_gains_grad: float32 [5, 512], P(None, 'dp')
All inputs are finite; a program needn't handle non-finite values.
Results may differ from a plain program's by a relative error of at most 0.035.
Values may be sent and summed in bfloat16 or wider, within the bound.
No kernel may reach another device: no remote copies, remote signals or barrier semaphores. Data moves between devices by JAX's collectives and lax.ppermute only.
A program may use at most 320 MiB of HBM per device.

v0:
```python
import functools

import jax
import jax.numpy as jnp
from jax import lax
from jax.experimental import pallas as pl
from jax.experimental.pallas import tpu as pltpu
from jax.sharding import PartitionSpec as P


EPS = 1e-05
BF16 = jnp.bfloat16
F32 = jnp.float32
SUB = 128
NT = (((1,), (1,)), ((), ()))


def flip_pair(value, axis, bit):
    return lax.ppermute(value, axis, [(i, i ^ 1 << bit) for i in range(lax.axis_size(axis))])


def bits_of(axis):
    return (lax.axis_size(axis) - 1).bit_length()


def own_bit(axis, bit):
    return lax.shift_right_logical(lax.axis_index(axis), bit) & 1


def full_order():
    dp_bits, mp_bits = bits_of("dp"), bits_of("mp")
    dp_high = [("dp", bit) for bit in range(dp_bits - 1, 0, -1)]
    mp_high = [("mp", bit) for bit in range(mp_bits - 1, 0, -1)]
    first = dp_high + [("dp", 0)] + mp_high + [("mp", 0)]
    second = dp_high + mp_high + [("dp", 0)] + [("mp", 0)]
    return (first, second)


def tied(value, other):
    return lax.optimization_barrier((value, other))[0]


def gather_groups(shard, order):
    held = {0: shard}
    for axis, bit in order:
        for delta in list(held):
            own = held[delta]
            other = flip_pair(own, axis, bit)
            if axis == "mp":
                held[delta ^ 1 << bit] = other
            else:
                held[delta] = jnp.concatenate([own, other], axis=0)
    return held


def scatter_groups(parts, order, marks=None):
    parts = dict(parts)
    total = None
    for axis, bit in reversed(order):
        if axis == "mp":
            for delta in [d for d in parts if d >> bit & 1]:
                other = flip_pair(parts.pop(delta), axis, bit)
                home = delta ^ 1 << bit
                parts[home] = (parts[home].astype(F32) + other.astype(F32)).astype(BF16)
        else:
            for delta in parts:
                half = parts[delta].shape[0] // 2
                keep, send = parts[delta][:half], parts[delta][half:]
                other = flip_pair(send, axis, bit)
                total = keep.astype(F32) + other.astype(F32)
                parts[delta] = total.astype(BF16)
        if marks is not None:
            marks.append(dict(parts))
    return total


def reversed_blocks(count):
    bits = (count - 1).bit_length()
    return [int(format(i, "b").zfill(bits)[::-1], 2) if bits else 0 for i in range(count)]


def block_choice(features, count, dtype):
    row = lax.broadcasted_iota(jnp.int32, (features, features), 0)
    col = lax.broadcasted_iota(jnp.int32, (features, features), 1)
    size = features // count
    block, image = col // size, jnp.zeros_like(col)
    for bit in range((count - 1).bit_length()):
        image = image * 2 + (block >> bit & 1)
    image = image ^ lax.axis_index("dp")
    return (row == image * size + col % size).astype(dtype)


def lane_flip(dtype):
    row = lax.broadcasted_iota(jnp.int32, (SUB, SUB), 0)
    col = lax.broadcasted_iota(jnp.int32, (SUB, SUB), 1)
    return (row + col == SUB - 1).astype(dtype)


def regroup(parts, widths, count):
    if count == 1:
        return parts
    joined = []
    for start in range(0, len(parts), count):
        pieces, at = [], 0
        for width in widths:
            pieces += [part[:, at : at + width] for part in parts[start : start + count]]
            at += width
        joined.append(jnp.concatenate(pieces, axis=1))
    return joined


def ungroup(parts, widths, count):
    if count == 1:
        return parts
    split = []
    for part in parts:
        for i in range(count):
            pieces, at = [], 0
            for width in widths:
                pieces.append(part[:, at + i * width : at + (i + 1) * width])
                at += width * count
            split.append(jnp.concatenate(pieces, axis=1))
    return split


def swap_groups(value, groups, delta):
    width = value.shape[-1] // groups
    parts = [value[..., (g ^ delta) * width : ((g ^ delta) + 1) * width] for g in range(groups)]
    return jnp.concatenate(parts, axis=-1)


def absolute_groups(value, groups):
    for bit in range((groups - 1).bit_length()):
        value = jnp.where(own_bit("mp", bit) == 0, value, swap_groups(value, groups, 1 << bit))
    return value


def channel_total(sums):
    groups = lax.axis_size("mp")
    for bit in range(bits_of("mp")):
        sums = sums + swap_groups(flip_pair(sums, "mp", bit), groups, 1 << bit)
    for bit in range(1, bits_of("dp")):
        sums = sums + flip_pair(sums, "dp", bit)
    return sums


def edge_rows(first_rows, last_rows, half_of_slot):
    groups = lax.axis_size("mp")
    place = lax.axis_index("mp")
    up = [(i, (i + 1) % groups) for i in range(groups)]
    down = [(i, (i - 1) % groups) for i in range(groups)]
    before = lax.ppermute(absolute_groups(last_rows, groups), "mp", up)
    after = lax.ppermute(absolute_groups(first_rows, groups), "mp", down)
    before = absolute_groups(before, groups)
    after = absolute_groups(after, groups)
    second = half_of_slot[:, None, None] == 1
    nothing = jnp.zeros_like(before)
    before = jnp.where(place == 0, jnp.where(second, before[::-1], nothing), before)
    after = jnp.where(place == groups - 1, jnp.where(second, nothing, after[::-1]), after)
    return (before, after)


def swish_grad(value):
    logistic = jax.nn.sigmoid(value)
    return logistic * (1.0 + value * (1.0 - logistic))


def normed_of(value):
    centred = value - jnp.mean(value, axis=-1, keepdims=True)
    inverse = lax.rsqrt(jnp.mean(centred * centred, axis=-1, keepdims=True) + EPS)
    return (centred * inverse, inverse)


def norm_back(normed, inverse, gain, upstream):
    scaled = upstream * gain
    inner = (
        scaled
        - jnp.mean(scaled, axis=-1, keepdims=True)
        - normed * jnp.mean(scaled * normed, axis=-1, keepdims=True)
    )
    return (inverse * inner, jnp.sum(upstream * normed, axis=0, keepdims=True))


def mm(left, right):
    return jnp.dot(left, right, preferred_element_type=F32)


def mm_nt(left, right):
    return lax.dot_general(left, right, NT, preferred_element_type=F32)


def call_kernel(kernel, outs, *inputs):
    return pl.pallas_call(
        kernel, out_shape=[jax.ShapeDtypeStruct(shape, dtype) for shape, dtype in outs]
    )(*inputs)


def column_join(refs, index):
    return jnp.concatenate([ref[:, index * SUB : (index + 1) * SUB] for ref in refs], axis=1)


def ffn_forward_kernel(groups, v_ref, gain_ref, *refs):
    ups, downs, out_ref = refs[:groups], refs[groups : 2 * groups], refs[-1]
    value = v_ref[...]
    normed, _ = normed_of(value)
    active = (normed * gain_ref[...]).astype(BF16)
    total = jnp.zeros_like(value)
    for up_ref, down_ref in zip(ups, downs):
        pre = mm(active, up_ref[...])
        hidden = (pre * jax.nn.sigmoid(pre)).astype(BF16)
        total += mm_nt(hidden, down_ref[...])
    out_ref[...] = value + 0.5 * total


def ffn_backward_kernel(groups, v_ref, d_ref, gain_ref, one_ref, two_ref, last_ref, *refs):
    ups, downs = refs[:groups], refs[groups : 2 * groups]
    out_ref = refs[2 * groups]
    gus, gds = refs[2 * groups + 1 : 3 * groups + 1], refs[3 * groups + 1 :]
    part = ups[0].shape[1]
    normed, inverse = normed_of(v_ref[...])
    upstream = d_ref[...]
    active = (normed * gain_ref[...]).astype(BF16)
    error = (0.5 * upstream).astype(BF16)
    active_t = active.T
    error_t = error.T
    total = jnp.zeros_like(upstream)
    for up_ref, down_ref, gu_ref, gd_ref in zip(ups, downs, gus, gds):
        pre = mm(active, up_ref[...])
        logistic = jax.nn.sigmoid(pre)
        hidden = (pre * logistic).astype(BF16)
        gd_ref[:, :part] = mm(error_t, hidden).astype(BF16)
        d_hidden = mm(error, down_ref[...])
        d_pre = (d_hidden * (logistic * (1.0 + pre * (1.0 - logistic)))).astype(BF16)
        gu_ref[...] = mm(active_t, d_pre).astype(BF16)
        total += mm_nt(d_pre, up_ref[...])
    back, grad_gain = norm_back(normed, inverse, gain_ref[...], total)
    out_ref[...] = upstream + back
    known = [grad_gain, one_ref[...], two_ref[...], last_ref[...]]
    count = sum(value.shape[0] for value in known)
    known.append(jnp.zeros((SUB - count, upstream.shape[1]), F32))
    columns = jnp.concatenate(known, axis=0).T.astype(BF16)
    for gd_ref in gds:
        gd_ref[:, part:] = columns


def project_kernel(groups, v_ref, gain_ref, *refs):
    weights, q_ref = refs[:groups], refs[groups]
    pair_refs = refs[groups + 1 :]
    normed, _ = normed_of(v_ref[...])
    active = (normed * gain_ref[...]).astype(BF16)
    q_ref[...] = mm(active, column_join(weights, 0)).astype(BF16)
    width = q_ref.shape[1] // len(pair_refs)
    for i in (0, 1):
        projected = mm(active, column_join(weights, i + 1)).astype(BF16)
        for h, pair_ref in enumerate(pair_refs):
            pair_ref[i] = projected[:, h * width : (h + 1) * width]


def project_backward_kernel(groups, halves, v_ref, d_ref, gain_ref, *refs):
    weights, smalls = refs[:groups], refs[groups : 2 * groups]
    dqs = refs[2 * groups : 2 * groups + halves]
    pairs = refs[2 * groups + halves : 2 * groups + 2 * halves]
    out_ref, gg_ref = refs[2 * groups + 2 * halves : 2 * groups + 2 * halves + 2]
    grads = refs[2 * groups + 2 * halves + 2 :]
    normed, inverse = normed_of(v_ref[...])
    active_t = (normed * gain_ref[...]).astype(BF16).T
    total = jnp.zeros_like(d_ref[...])
    for i in range(3):
        parts = [ref[...] for ref in dqs] if i == 0 else [ref[i - 1] for ref in pairs]
        error = jnp.concatenate(parts, axis=1) if halves > 1 else parts[0]
        total += mm_nt(error, column_join(weights, i))
        grad = mm(active_t, error).astype(BF16)
        for g, grad_ref in enumerate(grads):
            grad_ref[:, i * SUB : (i + 1) * SUB] = grad[:, g * SUB : (g + 1) * SUB]
    for small_ref, grad_ref in zip(smalls, grads):
        grad_ref[:, 3 * SUB :] = small_ref[...]
    back, grad_gain = norm_back(normed, inverse, gain_ref[...], total)
    out_ref[...] = d_ref[...] + back
    gg_ref[...] = grad_gain


def middle_kernel(groups, halves, v_ref, gain_ref, *refs):
    weights, contexts = refs[:groups], refs[groups : groups + halves]
    out_ref, lin_ref, sig_ref, glu_ref = refs[groups + halves :]
    parts = [ref[...] for ref in contexts]
    context = jnp.concatenate(parts, axis=1) if halves > 1 else parts[0]
    value = v_ref[...] + mm_nt(context, column_join(weights, 0))
    out_ref[...] = value
    normed, _ = normed_of(value)
    active = (normed * gain_ref[...]).astype(BF16)
    lin = mm(active, column_join(weights, 1))
    gate = jax.nn.sigmoid(mm(active, column_join(weights, 2)))
    lin_ref[...] = lin
    sig_ref[...] = gate
    glu_ref[...] = (lin * gate).astype(BF16)


def middle_backward_kernel(groups, halves, dglu_ref, lin_ref, sig_ref, v_ref, d_ref, gain_ref, *refs):
    weights, contexts = refs[:groups], refs[groups : groups + halves]
    out_ref, gg_ref, dctx_ref = refs[groups + halves : groups + halves + 3]
    grads = refs[groups + halves + 3 :]
    d_glu, lin, gate = dglu_ref[...], lin_ref[...], sig_ref[...]
    d_lin = (d_glu * gate).astype(BF16)
    d_gate = (d_glu * lin * gate * (1.0 - gate)).astype(BF16)
    normed, inverse = normed_of(v_ref[...])
    active_t = (normed * gain_ref[...]).astype(BF16).T
    total = mm_nt(d_lin, column_join(weights, 1)) + mm_nt(d_gate, column_join(weights, 2))
    back, grad_gain = norm_back(normed, inverse, gain_ref[...], total)
    value = d_ref[...] + back
    out_ref[...] = value
    gg_ref[...] = grad_gain
    error = value.astype(BF16)
    dctx_ref[...] = mm(error, column_join(weights, 0)).astype(BF16)
    parts = [ref[...] for ref in contexts]
    context = jnp.concatenate(parts, axis=1) if halves > 1 else parts[0]
    for i, grad in enumerate((mm(error.T, context), mm(active_t, d_lin), mm(active_t, d_gate))):
        rounded = grad.astype(BF16)
        for g, grad_ref in enumerate(grads):
            grad_ref[:, i * SUB : (i + 1) * SUB] = rounded[:, g * SUB : (g + 1) * SUB]


def turn_kernel(groups, batch_rows, conv_ref, stat_ref, bn_ref, v_ref, up_ref, gains_ref, *refs):
    weights = refs[:groups]
    final_ref, out_ref, dpre_ref, gg_ref, sums_ref = refs[groups : groups + 5]
    grads, pres = refs[groups + 5 : -1], refs[-1]
    part = pres.shape[2]
    top, bottom = slice(4 * SUB, 4 * SUB + part), slice(4 * SUB + part, 4 * SUB + 2 * part)
    gain_three, gain_four = gains_ref[3:4], gains_ref[4:5]
    mean = stat_ref[0:1] / batch_rows
    white = (conv_ref[...] - mean) * lax.rsqrt(stat_ref[1:2] / batch_rows - mean * mean + EPS)
    bn_pre = bn_ref[0:1] * white + bn_ref[1:2]
    activated = (bn_pre * jax.nn.sigmoid(bn_pre)).astype(BF16)
    outward = column_join(weights, 3)
    third = v_ref[...] + mm_nt(activated, outward)
    normed, inverse = normed_of(third)
    active = (normed * gain_three).astype(BF16)
    total = jnp.zeros_like(third)
    for g, weight in enumerate(weights):
        pre = mm(active, weight[:, top])
        pres[g] = pre
        total += mm_nt((pre * jax.nn.sigmoid(pre)).astype(BF16), weight[:, bottom])
    last_normed, last_inverse = normed_of(third + 0.5 * total)
    final_ref[...] = (last_normed * gain_four).astype(BF16)
    fourth, grad_four = norm_back(last_normed, last_inverse, gain_four, up_ref[...])
    error = (0.5 * fourth).astype(BF16)
    active_t = active.T
    error_t = error.T
    total = jnp.zeros_like(third)
    for g, (weight, grad_ref) in enumerate(zip(weights, grads)):
        pre = pres[g]
        logistic = jax.nn.sigmoid(pre)
        hidden = (pre * logistic).astype(BF16)
        grad_ref[:, SUB + part :] = mm(error_t, hidden).astype(BF16)
        d_hidden = mm(error, weight[:, bottom])
        d_pre = (d_hidden * (logistic * (1.0 + pre * (1.0 - logistic)))).astype(BF16)
        grad_ref[:, SUB : SUB + part] = mm(active_t, d_pre).astype(BF16)
        total += mm_nt(d_pre, weight[:, top])
    back, grad_three = norm_back(normed, inverse, gain_three, total)
    value = fourth + back
    out_ref[...] = value
    gg_ref[0:1] = grad_three
    gg_ref[1:2] = grad_four
    error = value.astype(BF16)
    grad = mm(error.T, activated).astype(BF16)
    for g, grad_ref in enumerate(grads):
        grad_ref[:, :SUB] = grad[:, g * SUB : (g + 1) * SUB]
    d_pre = mm(error, outward) * swish_grad(bn_pre)
    dpre_ref[...] = d_pre
    sums_ref[0:1] = jnp.sum(d_pre, axis=0, keepdims=True)
    sums_ref[1:2] = jnp.sum(d_pre * white, axis=0, keepdims=True)


def build_skew(line_ref, skew, heads, chunks):
    for h in range(heads):
        for c in range(chunks):
            window = jnp.concatenate(
                [line_ref[0, h, c + 1 : c + 2, :], line_ref[0, h, c : c + 1, :]], axis=1
            )
            window = jnp.broadcast_to(window, (SUB, 2 * SUB))
            rolled = pltpu.roll(window, 1, 1, stride=1, stride_axis=0)
            skew[h, SUB * c : SUB * (c + 1), :] = rolled[:, SUB:]


def stack_heads(rows, heads, factor):
    lane = lax.broadcasted_iota(jnp.int32, rows.shape, 1)
    size = rows.shape[1] // heads
    return jnp.concatenate(
        [
            rows * jnp.where((lane >= h * size) & (lane < (h + 1) * size), factor, 0.0).astype(BF16)
            for h in range(heads)
        ],
        axis=0,
    )


def diagonal_heads(value, heads):
    size, columns = value.shape[0] // heads, value.shape[1] // heads
    parts = [
        value[h * size : (h + 1) * size, h * columns : (h + 1) * columns] for h in range(heads)
    ]
    return jnp.concatenate(parts, axis=0)


def tile_bias(skew, columns, block, offset_of):
    parts = [
        skew[h, pl.ds(pl.multiple_of(offset_of(qb), SUB), block), :] for h, qb in columns
    ]
    return jnp.concatenate(parts, axis=1)


def column_tiles(heads, steps):
    columns = [(h, qb) for h in range(heads) for qb in range(steps)]
    return [columns[i : i + 2] for i in range(0, len(columns), 2)]


def attend_forward_kernel(pieces, heads, qpos, kpos, q_ref, line_ref, *refs):
    k_refs = refs[:pieces]
    v_refs = refs[pieces : 2 * pieces]
    ctx_ref, lse_ref, ctx32_ref, skew, query, scores, probs, v_t = refs[2 * pieces :]
    rows, width = q_ref.shape
    block = rows // 2
    chunks = skew.shape[1] // SUB
    middle = skew.shape[1] // 2
    tiles = column_tiles(heads, rows // SUB)
    span = 2 * SUB
    build_skew(line_ref, skew, heads, chunks)
    for p in range(pieces):
        v_t[:width, p * rows : (p + 1) * rows] = v_refs[p][0].T
    v_t[width:, :] = jnp.ones_like(v_t[width:, :])
    query[...] = stack_heads(q_ref[...], heads, (width // heads) ** (-0.5))
    tops = [jnp.full((8, span), -jnp.inf, F32) for _ in tiles]
    for c in range(2 * pieces):
        keys = k_refs[c // 2][0, (c % 2) * block : (c % 2 + 1) * block, :]
        for t, tile in enumerate(tiles):
            raw = mm_nt(keys, query[t * span : (t + 1) * span, :])
            raw = raw + tile_bias(skew, tile, block, lambda qb: kpos[c] - qpos[qb] + middle)
            scores[c * block : (c + 1) * block, t * span : (t + 1) * span] = raw
            tops[t] = jnp.maximum(tops[t], jnp.max(raw.reshape(block // 8, 8, span), axis=0))
    tops = [jnp.max(top, axis=0, keepdims=True) for top in tops]
    for c in range(2 * pieces):
        for t in range(len(tiles)):
            part = (slice(c * block, (c + 1) * block), slice(t * span, (t + 1) * span))
            probs[part] = jnp.exp(scores[part] - tops[t]).astype(BF16)
    out_t = mm(v_t[...], probs[...])
    total = out_t[width : width + 1, :]
    out_t = out_t[:width, :] / total
    out = diagonal_heads(out_t, heads).T
    ctx_ref[...] = out.astype(BF16)
    ctx32_ref[...] = out
    lse_ref[0] = jnp.concatenate(tops, axis=1) + jnp.log(total)


def attend_backward_kernel(pieces, heads, qpos, kpos, q_ref, d_ref, ctx_ref, lse_ref, line_ref, *refs):
    k_refs = refs[:pieces]
    v_refs = refs[pieces : 2 * pieces]
    dq_ref = refs[2 * pieces]
    dkv_refs = refs[2 * pieces + 1 : 3 * pieces + 1]
    line_grad, skew, skew_grad, query, error, probs, d_scores, k_t = refs[3 * pieces + 1 :]
    rows, width = q_ref.shape
    block = rows // 2
    chunks = skew.shape[1] // SUB
    middle = skew.shape[1] // 2
    scale = (width // heads) ** (-0.5)
    size = width // heads
    tiles = column_tiles(heads, rows // SUB)
    span = 2 * SUB
    build_skew(line_ref, skew, heads, chunks)
    skew_grad[...] = jnp.zeros_like(skew_grad)
    for p in range(pieces):
        k_t[:, p * rows : (p + 1) * rows] = k_refs[p][0].T
    query[...] = stack_heads(q_ref[...], heads, scale)
    error[...] = stack_heads(d_ref[...], heads, 1.0)
    weighed = (d_ref[...].astype(F32) * ctx_ref[...]).T
    dot_sum = jnp.concatenate(
        [jnp.sum(weighed[h * size : (h + 1) * size], axis=0, keepdims=True) for h in range(heads)],
        axis=1,
    )
    lse = lse_ref[0]
    for c in range(2 * pieces):
        part = slice((c % 2) * block, (c % 2 + 1) * block)
        here = slice(c * block, (c + 1) * block)
        keys = k_refs[c // 2][0, part, :]
        values = v_refs[c // 2][0, part, :]
        for t, tile in enumerate(tiles):
            cols = slice(t * span, (t + 1) * span)
            raw = mm_nt(keys, query[cols, :])
            bias = tile_bias(skew, tile, block, lambda qb: kpos[c] - qpos[qb] + middle)
            prob = jnp.exp(raw + bias - lse[:, cols])
            d_score = prob * (mm_nt(values, error[cols, :]) - dot_sum[:, cols])
            probs[c % 2, :, cols] = prob.astype(BF16)
            d_scores[here, cols] = d_score.astype(BF16)
            for i, (h, qb) in enumerate(tile):
                offset = pl.multiple_of(kpos[c] - qpos[qb] + middle, SUB)
                skew_grad[h, pl.ds(offset, block), :] += d_score[:, i * SUB : (i + 1) * SUB]
        dkv_refs[c // 2][0, part, :] = mm(d_scores[here, :], query[...]).astype(BF16)
        dkv_refs[c // 2][1, part, :] = mm(probs[c % 2], error[...]).astype(BF16)
    dq_t = mm(k_t[...], d_scores[...])
    dq_ref[...] = (diagonal_heads(dq_t, heads).T * scale).astype(BF16)
    line_grad[...] = jnp.zeros_like(line_grad)
    for h in range(heads):
        for c in range(chunks):
            block_grad = skew_grad[h, SUB * c : SUB * (c + 1), :]
            value = jnp.concatenate([jnp.zeros_like(block_grad), block_grad], axis=1)
            half = SUB // 2
            while half >= 1:
                value = value[:half] + pltpu.roll(value[half:], 2 * SUB - half, 1)
                half //= 2
            value = pltpu.roll(value, 2 * SUB - 1, 1)
            line_grad[0, h, c + 1 : c + 2, :] += value[:, :SUB]
            line_grad[0, h, c : c + 1, :] += value[:, SUB:]


def attention_specs(rows, first, pieces, shifts, line_shape):
    whole_q = pl.BlockSpec((rows, SUB), lambda j, *_: (0, j + first))
    own = pl.BlockSpec((rows, SUB), lambda j, *_: (0, j))
    line = pl.BlockSpec((1,) + line_shape[1:], lambda j, *_: (j + first, 0, 0, 0))
    keys, values = [], []
    for p in range(pieces):
        keys.append(pl.BlockSpec((1, rows, SUB), lambda j, *_, d=shifts[p]: (0, 0, j ^ d)))
        values.append(pl.BlockSpec((1, rows, SUB), lambda j, *_, d=shifts[p]: (1, 0, j ^ d)))
    return (whole_q, own, line, keys, values)


def attend_forward(query, pairs, shifts, line, first, qpos, kpos):
    rows = query.shape[0]
    heads = line.shape[1]
    groups = pairs[0].shape[2] // SUB
    pieces = len(pairs)
    table = (line.shape[2] - 1) * SUB
    whole_q, own, line_spec, keys, values = attention_specs(rows, first, pieces, shifts, line.shape)
    return pl.pallas_call(
        functools.partial(attend_forward_kernel, pieces, heads),
        out_shape=(
            jax.ShapeDtypeStruct((rows, groups * SUB), BF16),
            jax.ShapeDtypeStruct((groups, 1, heads * rows), F32),
            jax.ShapeDtypeStruct((rows, groups * SUB), F32),
        ),
        grid_spec=pltpu.PrefetchScalarGridSpec(
            num_scalar_prefetch=2,
            grid=(groups,),
            in_specs=[whole_q, line_spec] + keys + values,
            out_specs=(
                own,
                pl.BlockSpec((1, 1, heads * rows), lambda j, *_: (j, 0, 0)),
                own,
            ),
            scratch_shapes=[
                pltpu.VMEM((heads, table, SUB), F32),
                pltpu.VMEM((heads * rows, SUB), BF16),
                pltpu.VMEM((pieces * rows, heads * rows), F32),
                pltpu.VMEM((pieces * rows, heads * rows), BF16),
                pltpu.VMEM((SUB + 16, pieces * rows), BF16),
            ],
        ),
        name="attend_forward",
    )(qpos, kpos, query, line, *pairs, *pairs)


def attend_backward(query, d_context, lse, context, pairs, shifts, line, first, qpos, kpos):
    rows = query.shape[0]
    heads = line.shape[1]
    groups = pairs[0].shape[2] // SUB
    pieces = len(pairs)
    table = (line.shape[2] - 1) * SUB
    whole_q, own, line_spec, keys, values = attention_specs(rows, first, pieces, shifts, line.shape)
    lse_spec = pl.BlockSpec((1, 1, heads * rows), lambda j, *_: (j, 0, 0))
    pair_specs = [
        pl.BlockSpec((2, rows, SUB), lambda j, *_, d=shifts[p]: (0, 0, j ^ d))
        for p in range(pieces)
    ]
    return pl.pallas_call(
        functools.partial(attend_backward_kernel, pieces, heads),
        out_shape=(
            (jax.ShapeDtypeStruct((rows, groups * SUB), BF16),)
            + tuple(jax.ShapeDtypeStruct(pairs[0].shape, BF16) for _ in range(pieces))
            + (jax.ShapeDtypeStruct((groups,) + line.shape[1:], F32),)
        ),
        grid_spec=pltpu.PrefetchScalarGridSpec(
            num_scalar_prefetch=2,
            grid=(groups,),
            in_specs=[whole_q, whole_q, own, lse_spec, line_spec] + keys + values,
            out_specs=(
                (own,)
                + tuple(pair_specs)
                + (pl.BlockSpec((1,) + line.shape[1:], lambda j, *_: (j, 0, 0, 0)),)
            ),
            scratch_shapes=[
                pltpu.VMEM((heads, table, SUB), F32),
                pltpu.VMEM((heads, table, SUB), F32),
                pltpu.VMEM((heads * rows, SUB), BF16),
                pltpu.VMEM((heads * rows, SUB), BF16),
                pltpu.VMEM((2, rows // 2, heads * rows), BF16),
                pltpu.VMEM((pieces * rows, heads * rows), BF16),
                pltpu.VMEM((SUB, pieces * rows), BF16),
            ],
        ),
        name="attend_backward",
    )(qpos, kpos, query, d_context, context, lse, line, *pairs, *pairs)


def block_step(
    block_input,
    out_cotangent,
    early_up,
    early_down,
    attention_in,
    attention_out,
    relative_bias,
    pointwise_in,
    depthwise,
    batch_norm,
    pointwise_out,
    late_up,
    late_down,
    norm_gains,
):
    dp_n, mp_n = lax.axis_size("dp"), lax.axis_size("mp")
    held_rows, features = block_input.shape[1:]
    block = held_rows // mp_n
    rows = 2 * block
    batch_rows = held_rows * dp_n
    batch = lax.axis_index("dp") % 2
    place = lax.axis_index("mp")
    shard_rows, part = early_up.shape
    heads, table_part = relative_bias.shape
    channel_part, kernel = depthwise.shape
    head_width = attention_out.shape[0]
    channels = mp_n * head_width
    margin = (kernel - 1) // 2
    order_a, order_b = full_order()
    fold = max(1, SUB // head_width)
    groups = mp_n // fold
    blocks = jnp.array(reversed_blocks(dp_n), jnp.int32)
    to_natural = blocks[jnp.arange(dp_n, dtype=jnp.int32) ^ lax.axis_index("dp")]
    to_held = blocks ^ lax.axis_index("dp")
    choice = block_choice(features, dp_n, BF16)

    def exchanged(value):
        mine = lax.dynamic_slice_in_dim(value, place * block, block, 1)
        own = lax.dynamic_index_in_dim(mine, batch, 0, keepdims=False)
        away = lax.dynamic_index_in_dim(mine, 1 - batch, 0, keepdims=False)
        other = flip_pair(away, "dp", 0)
        return mm(jnp.concatenate([own, other], axis=0), choice)

    def listed(parts, widths):
        return regroup([parts[delta] for delta in range(mp_n)], widths, fold)

    def unlisted(parts, widths):
        return dict(enumerate(ungroup(list(parts), widths, fold)))

    bias_rows = heads * table_part // SUB
    tap_n = kernel + 2
    gain_row = bias_rows + channel_part
    small_rows = gain_row + norm_gains.shape[0]
    small = jnp.concatenate(
        [
            relative_bias.reshape(bias_rows, SUB),
            jnp.pad(jnp.concatenate([depthwise, batch_norm.T], axis=1), ((0, 0), (0, SUB - tap_n))),
            jnp.pad(norm_gains, ((0, shard_rows - small_rows), (0, SUB - shard_rows))),
        ],
        axis=0,
    )
    early_u = gather_groups(early_up, order_a)
    early_d = gather_groups(early_down.T, order_b)
    start = exchanged(block_input)
    pair_widths = [head_width] * 3
    att_shard = jnp.concatenate([attention_in[0], attention_in[1], attention_in[2], small], axis=1)
    att_held = gather_groups(att_shard, order_b)
    rest_widths = [head_width] * 4 + [part] * 2
    rest_shard = jnp.concatenate(
        [
            attention_out.T,
            pointwise_in[0],
            pointwise_in[1],
            pointwise_out.T,
            late_up,
            late_down.T,
        ],
        axis=1,
    )
    rest = listed(gather_groups(rest_shard, order_b), rest_widths)
    if fold == 1:
        att = [att_held[delta] for delta in range(mp_n)]
    else:
        att = listed({d: value[:, : 3 * head_width] for d, value in att_held.items()}, pair_widths)
    gains = (
        att_held[0]
        .reshape(dp_n, shard_rows, -1)[:, gain_row:small_rows, 3 * head_width : 3 * head_width + shard_rows]
        .transpose(1, 0, 2)
        .reshape(5, features)
        .astype(F32)
    )
    gain = [gains[i : i + 1] for i in range(5)]
    tiny = jnp.stack([att_held[delta][:, 3 * head_width :] for delta in range(mp_n)])
    tiny = tiny.reshape(mp_n, dp_n, shard_rows, SUB)[:, to_natural]
    line = (
        tiny[:, :, :bias_rows]
        .reshape(mp_n, dp_n, heads, table_part // SUB, SUB)
        .transpose(0, 2, 1, 3, 4)
        .reshape(mp_n, heads, dp_n * table_part // SUB, SUB)
    )
    line = jnp.einsum("ghcl,lk->ghck", line, lane_flip(BF16), preferred_element_type=F32)
    line = jnp.pad(line, ((0, 0), (0, 0), (1, 0), (0, 0)))
    line = line.reshape(groups, heads * fold, line.shape[2], SUB)
    taps = (
        tiny[:, :, bias_rows : bias_rows + channel_part, :tap_n].reshape(channels, tap_n).T.astype(F32)
    )

    half_of_slot = jnp.stack([batch, 1 - batch]).astype(jnp.int32)
    kept = [0]
    for bit in range(bits_of("mp") - 1, -1, -1):
        kept = kept + [delta ^ 1 << bit for delta in kept]
    qpos = (
        half_of_slot[:, None] * held_rows
        + place * block
        + SUB * jnp.arange(block // SUB, dtype=jnp.int32)[None, :]
    ).reshape(-1)
    kpos = jnp.stack(
        [half_of_slot[r] * held_rows + (place ^ delta) * block for delta in kept for r in (0, 1)]
    )
    wide = (rows, channels)
    halves = 2 if fold == 1 and mp_n >= 4 else 1
    local = groups // halves
    up_list = [early_u[delta] for delta in range(mp_n)]
    down_list = [early_d[delta] for delta in range(mp_n)]
    (after_first,) = call_kernel(
        functools.partial(ffn_forward_kernel, mp_n),
        [((rows, features), F32)],
        start,
        gain[0],
        *up_list,
        *down_list,
    )
    query, *pair_halves = call_kernel(
        functools.partial(project_kernel, groups),
        [(wide, BF16)] + [((2, rows, local * SUB), BF16)] * halves,
        after_first,
        gain[1],
        *att,
    )
    top_bit = bits_of("mp") - 1
    held_pairs = []
    for h in range(halves):
        pieces = [pair_halves[h]]
        away = pair_halves[halves - 1 - h]
        if h > 0:
            away = tied(away, held_pairs[h - 1][1])
        pieces.append(flip_pair(away, "mp", top_bit))
        for bit in range(top_bit - 1, -1, -1):
            pieces = pieces + [flip_pair(piece, "mp", bit) for piece in pieces]
        if fold > 1:
            pieces = [swap_groups(piece, mp_n, delta) for piece, delta in zip(pieces, kept)]
        held_pairs.append(pieces)
    shifts = [delta & (local - 1) if fold == 1 else 0 for delta in kept]
    attended = []
    for h in range(halves):
        attended.append(attend_forward(query, held_pairs[h], shifts, line, h * local, qpos, kpos))
    contexts = [item[0] for item in attended]
    after_second, lin, gate_sig, glu = call_kernel(
        functools.partial(middle_kernel, groups, halves),
        [((rows, features), F32), (wide, F32), (wide, F32), (wide, BF16)],
        after_first,
        gain[2],
        *rest,
        *contexts,
    )
    cotangent = exchanged(out_cotangent)
    glu = tied(glu, cotangent).reshape(2, block, channels)
    edge = margin + 1
    before, after = edge_rows(glu[:, :edge], glu[:, block - edge :], half_of_slot)
    extended = jnp.concatenate([before[:, 1:], glu, after[:, :margin]], axis=1).astype(F32)
    conv = jnp.zeros((2, block, channels), F32)
    for tap in range(kernel):
        conv = conv + taps[tap] * extended[:, tap : tap + block]
    conv = conv.reshape(rows, channels)
    sums = channel_total(jnp.stack([jnp.sum(conv, axis=0), jnp.sum(conv * conv, axis=0)]))
    bmean = sums[0:1] / batch_rows
    binv = lax.rsqrt(sums[1:2] / batch_rows - bmean * bmean + EPS)
    bn_rows = taps[kernel:]

    wide_part = part * fold
    turn_widths = [head_width, part, part]
    final_rows, d_third, d_pre, gg_last, local_sums, *turn_grads = pl.pallas_call(
        functools.partial(turn_kernel, groups, batch_rows),
        out_shape=[
            jax.ShapeDtypeStruct((rows, features), BF16),
            jax.ShapeDtypeStruct((rows, features), F32),
            jax.ShapeDtypeStruct(wide, F32),
            jax.ShapeDtypeStruct((2, features), F32),
            jax.ShapeDtypeStruct((2, channels), F32),
        ]
        + [jax.ShapeDtypeStruct((features, SUB + 2 * wide_part), BF16)] * groups,
        scratch_shapes=[pltpu.VMEM((groups, rows, wide_part), F32)],
        name="turn",
    )(conv, sums, bn_rows, after_second, cotangent, gains, *rest)
    turn_marks = []
    own_turn = scatter_groups(unlisted(turn_grads, turn_widths), order_a, turn_marks)

    sums = channel_total(local_sums)
    white = (conv - bmean) * binv
    d_conv = (
        binv * bn_rows[0:1] * (d_pre - sums[0:1] / batch_rows - white * sums[1:2] / batch_rows)
    ).reshape(2, block, channels)
    before, after = edge_rows(d_conv[:, :edge], d_conv[:, block - edge :], half_of_slot)
    d_extended = jnp.concatenate([before[:, 1:], d_conv, after[:, :margin]], axis=1)
    d_glu = jnp.zeros((2, block, channels), F32)
    tap_grads = []
    for tap in range(kernel):
        d_glu = d_glu + taps[tap] * d_extended[:, kernel - 1 - tap : kernel - 1 - tap + block]
        tap_grads.append(jnp.sum(extended[:, tap : tap + block] * d_conv, axis=(0, 1)))
    tap_grads = jnp.stack(tap_grads + [local_sums[1], local_sums[0]])
    d_second, gain_two, d_context, *middle_grads = call_kernel(
        functools.partial(middle_backward_kernel, groups, halves),
        [((rows, features), F32), (gain[2].shape, F32), (wide, BF16)]
        + [((features, 3 * SUB), BF16)] * groups,
        tied(d_glu.reshape(rows, channels), turn_marks[0][1 << top_bit]),
        lin,
        gate_sig,
        after_second,
        d_third,
        gain[2],
        *rest,
        *contexts,
    )
    own_middle = scatter_groups(unlisted(middle_grads, pair_widths), order_b)
    d_queries, kept_pairs, sent_pairs, line_grads = [], [], [], []
    for h in range(halves):
        grads = attend_backward(
            query, d_context, attended[h][1], attended[h][2], held_pairs[h], shifts, line,
            h * local, qpos, kpos,
        )
        d_queries.append(grads[0])
        line_grads.append(grads[-1])
        pieces = dict(zip(kept, grads[1:-1]))
        if fold > 1:
            pieces = {delta: swap_groups(value, mp_n, delta) for delta, value in pieces.items()}
        for bit in range(top_bit):
            for delta in [d for d in pieces if d >> bit & 1]:
                other = flip_pair(pieces.pop(delta), "mp", bit)
                home = delta ^ 1 << bit
                pieces[home] = (pieces[home].astype(F32) + other.astype(F32)).astype(BF16)
        kept_pairs.append(pieces[0])
        sent_pairs.append(flip_pair(pieces[1 << top_bit], "mp", top_bit))
    d_pairs = [
        (kept_pairs[h].astype(F32) + sent_pairs[halves - 1 - h].astype(F32)).astype(BF16)
        for h in range(halves)
    ]
    line_grad = jnp.concatenate(line_grads, axis=0)[:, :, 1:].reshape(mp_n, heads, -1, SUB)
    line_grad = jnp.einsum(
        "ghcl,lk->ghck", line_grad, lane_flip(F32), precision=lax.Precision.HIGHEST
    )
    tiny = jnp.concatenate(
        [
            line_grad.reshape(mp_n, heads, dp_n, table_part // SUB, SUB)
            .transpose(0, 2, 1, 3, 4)
            .reshape(mp_n, dp_n, bias_rows, SUB)[:, to_held],
            jnp.pad(
                tap_grads.T.reshape(mp_n, dp_n, channel_part, tap_n)[:, to_held],
                (
                    (0, 0),
                    (0, 0),
                    (0, shard_rows - bias_rows - channel_part),
                    (0, SUB - tap_n),
                ),
            ),
        ],
        axis=2,
    ).astype(BF16)
    tiny = tiny.reshape(mp_n, features, SUB)
    smalls = [tiny[g] for g in range(groups)]
    d_first, gain_one, *att_grads = call_kernel(
        functools.partial(project_backward_kernel, groups, halves),
        [((rows, features), F32), (gain[1].shape, F32)] + [((features, 4 * SUB), BF16)] * groups,
        after_first,
        d_second,
        gain[1],
        *att,
        *smalls,
        *d_queries,
        *d_pairs,
    )
    if fold > 1:
        att_grads = ungroup([grad[:, : 3 * SUB] for grad in att_grads], pair_widths, fold)
        att_grads = [jnp.concatenate([g, t], axis=1) for g, t in zip(att_grads, tiny)]
    own_att = scatter_groups(dict(enumerate(att_grads)), order_a)
    d_start, *early_grads = call_kernel(
        functools.partial(ffn_backward_kernel, mp_n),
        [((rows, features), F32)]
        + [((features, part), BF16)] * mp_n
        + [((features, part + SUB), BF16)] * mp_n,
        start,
        d_first,
        gain[0],
        gain_one,
        gain_two,
        gg_last,
        *up_list,
        *down_list,
    )
    up_marks = []
    own_up = scatter_groups(dict(enumerate(early_grads[:mp_n])), order_a, up_marks)
    own_down = scatter_groups(dict(enumerate(early_grads[mp_n:])), order_b)

    def returned(own, away):
        other = flip_pair(away, "dp", 0).astype(own.dtype)
        first = batch == 0
        return jnp.stack([jnp.where(first, own, other), jnp.where(first, other, own)])

    def columns(value, index):
        return value[:, index * head_width : (index + 1) * head_width]

    tail = own_att[:, 3 * head_width :]
    per_channel = tail[bias_rows : bias_rows + channel_part]
    natural = lax.dot_general(
        tied(d_start, up_marks[0][1 << top_bit]), choice.astype(F32), NT, precision=lax.Precision.HIGHEST
    )
    final_rows = mm_nt(final_rows, choice).astype(BF16)
    return (
        returned(final_rows[:block], final_rows[block:]),
        returned(natural[:block], natural[block:].astype(BF16)),
        own_up,
        own_down[:, :part].T,
        jnp.stack([columns(own_att, i) for i in range(3)]),
        columns(own_middle, 0).T,
        tail[:bias_rows].reshape(heads, table_part),
        jnp.stack([columns(own_middle, 1), columns(own_middle, 2)]),
        per_channel[:, :kernel],
        per_channel[:, kernel:tap_n].T,
        columns(own_turn, 0).T,
        own_turn[:, head_width : head_width + part],
        own_turn[:, head_width + part :].T,
        own_down[:, part : part + 5].T,
    )


def solution(mesh):
    placed = (
        P(None, "dp", None),
        P(None, "dp", None),
        P("dp", "mp"),
        P("mp", "dp"),
        P(None, "dp", "mp"),
        P("mp", "dp"),
        P("mp", "dp"),
        P(None, "dp", "mp"),
        P(("mp", "dp"), None),
        P(None, ("mp", "dp")),
        P("mp", "dp"),
        P("dp", "mp"),
        P("mp", "dp"),
        P(None, "dp"),
    )
    returned = (P(None, ("dp", "mp"), None), P(None, ("dp", "mp"), None)) + placed[2:]
    return jax.shard_map(block_step, mesh=mesh, in_specs=placed, out_specs=returned, check_vma=False)
```

profile of v0, /device:TPU:0, one launch (start us, length us, event | category | flops | bytes accessed | tf_op | source)
XLA Modules:
  0.0 438.9 jit_solution(4098504447895504470)
XLA Ops:
  4.3 4.1 collective-permute-start
  26.9 2.9 collective-permute-done.1
  43.3 4.5 %collective-permute-done.22 = bf16[128,1536]{1,0:T(8,128)(2,1)S(1)} collective-permute-done((bf16[128,1536]{1,0:T(8,128)(2,1)S(1)}, bf16[128,1536]{1,0:T(8,128)(2,1)S(1)}, u32[]{:S(2)}, u32[]{:S(2)}) %collective-permute-start.22) | collective-permute-done | bytes 393248 | tf_op jit(solution)/shard_map/ppermute | solution.py:19
  48.4 3.6 collective-permute-done.10
  56.8 6.8 %collective-permute-done.5 = bf16[256,512]{1,0:T(8,128)(2,1)} collective-permute-done((bf16[256,512]{1,0:T(8,128)(2,1)S(1)}, bf16[256,512]{1,0:T(8,128)(2,1)}, u32[]{:S(2)}, u32[]{:S(2)}) %collective-permute-start.5) | collective-permute-done | bytes 262176 | tf_op jit(solution)/shard_map/ppermute | solution.py:19
  63.6 5.6 %collective-permute-done.19 = bf16[256,512]{1,0:T(8,128)(2,1)} collective-permute-done((bf16[256,512]{1,0:T(8,128)(2,1)S(1)}, bf16[256,512]{1,0:T(8,128)(2,1)}, u32[]{:S(2)}, u32[]{:S(2)}) %collective-permute-start.19) | collective-permute-done | bytes 262176 | tf_op jit(solution)/shard_map/ppermute | solution.py:19
  78.2 7.9 %collective-permute-done.23 = bf16[256,1536]{1,0:T(8,128)(2,1)} collective-permute-done((bf16[256,1536]{1,0:T(8,128)(2,1)S(1)}, bf16[256,1536]{1,0:T(8,128)(2,1)}, u32[]{:S(2)}, u32[]{:S(2)}) %collective-permute-start.23) | collective-permute-done | bytes 786464 | tf_op jit(solution)/shard_map/ppermute | solution.py:19
  90.7 6.1 %shard_map.254.v_ref = f32[512,512]{1,0:T(8,128)} custom-call(f32[512,512]{1,0:T(8,128)} %fusion.103.v_ref, f32[1,512]{1,0:T(1,128)} %slice.900.gain_ref, bf16[512,512]{1,0:T(8,128)(2,1)} %copy-done.5, bf16[512,512]{1,0:T(8,128)(2,1)} %copy-done.6, bf16[512,512]{1,0:T(8,128)(2,1)} %collective-permute-done.12.refs_2_, bf16[512,512]{1,0:T(8,128)(2,1)} %copy-done.9, ...), custom_call_target="tpu_custom_call" | custom-call | tf_op jit(solution)/shard_map/pallas_call | solution.py:193
  96.9 4.1 shard_map.255
  106.1 9.1 %collective-permute-done.28.refs_1_.refs_5_ = bf16[2,512,256]{2,1,0:T(8,128)(2,1)} collective-permute-done((bf16[2,512,256]{2,1,0:T(8,128)(2,1)}, bf16[2,512,256]{2,1,0:T(8,128)(2,1)}, u32[]{:S(2)}, u32[]{:S(2)}) %collective-permute-start.28) | collective-permute-done | bytes 524320 | tf_op jit(solution)/shard_map/ppermute | solution.py:19
  132.3 12.9 %attend_forward.2 = (bf16[512,256]{1,0:T(8,128)(2,1)}, f32[2,1,1024]{2,1,0:T(1,128)}, f32[512,256]{1,0:T(8,128)}) custom-call(s32[4]{0:T(128)} %add.477.qpos, s32[8]{0:T(128)} %stack.211.kpos, bf16[512,512]{1,0:T(8,128)(2,1)} %get-tuple-element.74.q_ref, f32[4,2,33,128]{3,2,1,0:T(8,128)} %pad.19.line_ref, ...), custom_call_target="tpu_custom_call" | custom-call | tf_op jit(solution)/shard_map/attend_forward/pallas_call | solution.py:531
  145.2 12.4 %attend_forward.3 = (bf16[512,256]{1,0:T(8,128)(2,1)}, f32[2,1,1024]{2,1,0:T(1,128)}, f32[512,256]{1,0:T(8,128)}) custom-call(s32[4]{0:T(128)} %add.477.qpos, s32[8]{0:T(128)} %stack.211.kpos, bf16[512,512]{1,0:T(8,128)(2,1)} %get-tuple-element.74.q_ref, f32[4,2,33,128]{3,2,1,0:T(8,128)} %pad.19.line_ref, ...), custom_call_target="tpu_custom_call" | custom-call | tf_op jit(solution)/shard_map/attend_forward/pallas_call | solution.py:531
  157.7 5.7 %shard_map.256 = (f32[512,512]{1,0:T(8,128)}, f32[512,512]{1,0:T(8,128)}, f32[512,512]{1,0:T(8,128)}, bf16[512,512]{1,0:T(8,128)(2,1)}) custom-call(f32[512,512]{1,0:T(8,128)} %shard_map.254.v_ref, f32[1,512]{1,0:T(1,128)} %slice.902.gain_ref, bf16[512,1536]{1,0:T(8,128)(2,1)} %copy-done.1, bf16[512,1536]{1,0:T(8,128)(2,1)} %collective-permute-done.24.refs_1_, ...), custom_call_target="tpu_custom_call" | custom-call | tf_op jit(solution)/shard_map/pallas_call | solution.py:193
  170.4 5.1 %fusion.141 = (f32[512]{0:T(512)S(1)}, f32[512]{0:T(512)S(1)}, f32[2,256,512]{2,1,0:T(8,128)}) fusion(f32[2,286,512]{2,1,0:T(8,128)S(1)} %maximum_convert_fusion, f32[512]{0:T(512)S(1)} %bitcast.282, f32[512]{0:T(512)S(1)} %bitcast.284, f32[512]{0:T(512)S(1)} %bitcast.286, f32[512]{0:T(512)S(1)} %bitcast.288, f32[512]{0:T(512)S(1)} %bitcast.290, ...), kind=kLoop, calls=%fused_computation.383 | loop fusion | flops 16776192 | bytes 33622016 | tf_op jit(solution)/shard_map/reduce_sum | solution.py:776
  180.5 3.6 collective-permute-done.39
  189.2 15.9 %turn.1 = (bf16[512,512]{1,0:T(8,128)(2,1)}, f32[512,512]{1,0:T(8,128)}, f32[512,512]{1,0:T(8,128)}, f32[2,512]{1,0:T(2,128)}, f32[2,512]{1,0:T(2,128)}, /*index...) custom-call(f32[512,512]{1,0:T(8,128)} %bitcast.220, ...), custom_call_target="tpu_custom_call" | custom-call | tf_op jit(solution)/shard_map/turn/pallas_call | solution.py:783
  219.1 3.6 multiply_reduce_fusion
  230.0 5.5 %fusion.14 = f32[2,256,512]{2,1,0:T(8,128)} fusion(f32[2,15,512]{2,1,0:T(8,128)S(1)} %get-tuple-element.340, f32[2,15,512]{2,1,0:T(8,128)S(1)} %get-tuple-element.339, f32[2,256,512]{2,1,0:T(8,128)S(1)} %bitcast.219, f32[512]{0:T(512)S(1)} %bitcast.283, f32[512]{0:T(512)S(1)} %bitcast.285, f32[512]{0:T(512)S(1)} %bitcast.287, f32[512]{0:T(512)S(1)} %bitcast.289, ...), kind=kLoop, calls=%fused_computation.57 | loop fusion | flops 23855104 | bytes 2283520 | tf_op jit(solution)/shard_map/add | solution.py:809
  235.7 8.0 %shard_map.257 = (f32[512,512]{1,0:T(8,128)}, f32[1,512]{1,0:T(1,128)}, bf16[512,512]{1,0:T(8,128)(2,1)}, bf16[512,384]{1,0:T(8,128)(2,1)}, bf16[512,384]{1,0:T(...) custom-call(f32[512,512]{1,0:T(8,128)} %bitcast.221, f32[512,512]{1,0:T(8,128)} %get-tuple-element.89.lin_ref, ...), custom_call_target="tpu_custom_call" | custom-call | tf_op jit(solution)/shard_map/pallas_call | solution.py:193
  247.7 22.1 %attend_backward.3 = (bf16[512,256]{1,0:T(8,128)(2,1)}, bf16[2,512,256]{2,1,0:T(8,128)(2,1)}, bf16[2,512,256]{2,1,0:T(8,128)(2,1)}, bf16[2,512,256]{2,1,0:T(8,12...) custom-call(s32[4]{0:T(128)} %add.477.qpos, s32[8]{0:T(128)} %stack.211.kpos, ...), custom_call_target="tpu_custom_call" | custom-call | tf_op jit(solution)/shard_map/attend_backward/pallas_call | solution.py:571
  269.8 22.1 %attend_backward.2 = (bf16[512,256]{1,0:T(8,128)(2,1)}, bf16[2,512,256]{2,1,0:T(8,128)(2,1)}, bf16[2,512,256]{2,1,0:T(8,128)(2,1)}, bf16[2,512,256]{2,1,0:T(8,12...) custom-call(s32[4]{0:T(128)} %add.477.qpos, s32[8]{0:T(128)} %stack.211.kpos, ...), custom_call_target="tpu_custom_call" | custom-call | tf_op jit(solution)/shard_map/attend_backward/pallas_call | solution.py:571
  299.2 4.5 %collective-permute-done.78 = bf16[256,384]{1,0:T(8,128)(2,1)S(1)} collective-permute-done((bf16[256,384]{1,0:T(8,128)(2,1)S(1)}, bf16[256,384]{1,0:T(8,128)(2,1)S(1)}, u32[]{:S(2)}, u32[]{:S(2)}) %collective-permute-start.78) | collective-permute-done | bytes 196640 | tf_op jit(solution)/shard_map/ppermute | solution.py:19
  311.8 3.3 collective-permute-done.80
  317.3 3.0 collective-permute-done.81
  323.7 11.4 %collective-permute-done.51 = bf16[2,512,256]{2,1,0:T(8,128)(2,1)S(1)} collective-permute-done((bf16[2,512,256]{2,1,0:T(8,128)(2,1)S(1)}, bf16[2,512,256]{2,1,0:T(8,128)(2,1)S(1)}, u32[]{:S(2)}, u32[]{:S(2)}) %collective-permute-start.51) | collective-permute-done | bytes 524320 | tf_op jit(solution)/shard_map/ppermute | solution.py:19
  336.1 8.9 %collective-permute-done.54 = bf16[2,512,256]{2,1,0:T(8,128)(2,1)S(1)} collective-permute-done((bf16[2,512,256]{2,1,0:T(8,128)(2,1)S(1)}, bf16[2,512,256]{2,1,0:T(8,128)(2,1)S(1)}, u32[]{:S(2)}, u32[]{:S(2)}) %collective-permute-start.54) | collective-permute-done | bytes 524320 | tf_op jit(solution)/shard_map/ppermute | solution.py:19
  346.1 6.7 %shard_map.258 = (f32[512,512]{1,0:T(8,128)}, f32[1,512]{1,0:T(1,128)}, bf16[512,512]{1,0:T(8,128)(2,1)}, bf16[512,512]{1,0:T(8,128)(2,1)}, bf16[512,512]{1,0:T(8,128)(2,1)}, /*index=5*/bf16[512,512]{1,0:T(8,128)(2,1)}) custom-call(f32[512,512]{1,0:T(8,128)} %shard_map.254.v_ref, f32[512,512]{1,0:T(8,128)} %get-tuple-element.92.d_ref, ...), custom_call_target="tpu_custom_call" | custom-call | tf_op jit(solution)/shard_map/pallas_call | solution.py:193
  352.7 11.8 %shard_map.259 = (f32[512,512]{1,0:T(8,128)}, bf16[512,512]{1,0:T(8,128)(2,1)}, bf16[512,512]{1,0:T(8,128)(2,1)}, bf16[512,512]{1,0:T(8,128)(2,1)}, bf16[512,512...) custom-call(f32[512,512]{1,0:T(8,128)} %fusion.103.v_ref, ...), custom_call_target="tpu_custom_call" | custom-call | tf_op jit(solution)/shard_map/pallas_call | solution.py:193
  374.0 12.4 %collective-permute-done.84 = bf16[256,1152]{1,0:T(8,128)(2,1)S(1)} collective-permute-done((bf16[256,1152]{1,0:T(8,128)(2,1)S(1)}, bf16[256,1152]{1,0:T(8,128)(2,1)S(1)}, u32[]{:S(2)}, u32[]{:S(2)}) %collective-permute-start.84) | collective-permute-done | bytes 589856 | tf_op jit(solution)/shard_map/ppermute | solution.py:19
  387.9 4.2 collective-permute-done.56
  395.0 3.6 collective-permute-done.65
  406.7 6.7 %collective-permute-done.71 = bf16[512,512]{1,0:T(8,128)(2,1)S(1)} collective-permute-done((bf16[512,512]{1,0:T(8,128)(2,1)S(1)}, bf16[512,512]{1,0:T(8,128)(2,1)S(1)}, u32[]{:S(2)}, u32[]{:S(2)}) %collective-permute-start.71) | collective-permute-done | bytes 524320 | tf_op jit(solution)/shard_map/ppermute | solution.py:19
  (558 shorter events, 187.5 us)
Async XLA Ops:
  4.3 18.7 %collective-permute-start = (bf16[64,512]{1,0:T(8,128)(2,1)S(1)}, bf16[64,512]{1,0:T(8,128)(2,1)S(1)}, u32[]{:S(2)}, u32[]{:S(2)}) collective-permute-start(bf16[64,512]{1,0:T(8,128)(2,1)S(1)} %maximum_maximum_fusion), channel_id=1, source_target_pairs={{0,16},{4,20},{8,24},{12,28},{16,0},{20,4},{24,8},{28,12},{1,17},{... | collective-permute-start | bytes 196616 | tf_op jit(solution)/shard_map/ppermute | solution.py:19
  8.6 16.7 %collective-permute-start.8 = (bf16[64,512]{1,0:T(8,128)(2,1)}, bf16[64,512]{1,0:T(8,128)(2,1)S(1)}, u32[]{:S(2)}, u32[]{:S(2)}) collective-permute-start(bf16[64,512]{1,0:T(8,128)(2,1)} %param.17), channel_id=1, source_target_pairs={{0,16},{4,20},{8,24},{12,28},{16,0},{20,4},{24,8},{28,12},{1,17},{... | collective-permute-start | bytes 196616 | tf_op jit(solution)/shard_map/ppermute | solution.py:19
  16.0 20.9 %collective-permute-start.21 = (bf16[64,1536]{1,0:T(8,128)(2,1)S(1)}, bf16[64,1536]{1,0:T(8,128)(2,1)S(1)}, u32[]{:S(2)}, u32[]{:S(2)}) collective-permute-start(bf16[64,1536]{1,0:T(8,128)(2,1)S(1)} %bitcast_dynamic-update-slice_fusion), channel_id=1, source_target_pairs={{0,16},{4,20},{8,24},{12,28},{16,0},{20,4},{24,8},{28,12},{1,17},{... | collective-permute-start | bytes 589832 | tf_op jit(solution)/shard_map/ppermute | solution.py:19
  17.3 19.8 %collective-permute-start.7 = (bf16[256,512]{1,0:T(8,128)(2,1)S(1)}, bf16[256,512]{1,0:T(8,128)(2,1)S(1)}, u32[]{:S(2)}, u32[]{:S(2)}) collective-permute-start(bf16[256,512]{1,0:T(8,128)(2,1)S(1)} %get-tuple-element.216), channel_id=1, source_target_pairs={{0,4},{4,0},{8,12},{12,8},{16,20},{20,16},{24,28},{28,24},{1,5},{5... | collective-permute-start | bytes 786440 | tf_op jit(solution)/shard_map/ppermute | solution.py:19
  29.8 24.5 %collective-permute-start.4 = (bf16[256,512]{1,0:T(8,128)(2,1)S(1)}, bf16[256,512]{1,0:T(8,128)(2,1)S(1)}, u32[]{:S(2)}, u32[]{:S(2)}) collective-permute-start(bf16[256,512]{1,0:T(8,128)(2,1)S(1)} %pad_maximum_fusion.10), channel_id=1, source_target_pairs={{0,2},{1,3},{2,0},{3,1},{4,6},{5,7},{6,4},{7,5},{8,10},{9,11},{10,... | collective-permute-start | bytes 786440 | tf_op jit(solution)/shard_map/ppermute | solution.py:19
  35.3 19.3 %collective-permute-start.18 = (bf16[256,512]{1,0:T(8,128)(2,1)S(1)}, bf16[256,512]{1,0:T(8,128)(2,1)S(1)}, u32[]{:S(2)}, u32[]{:S(2)}) collective-permute-start(bf16[256,512]{1,0:T(8,128)(2,1)S(1)} %pad_maximum_fusion.12), channel_id=1, source_target_pairs={{0,2},{1,3},{2,0},{3,1},{4,6},{5,7},{6,4},{7,5},{8,10},{9,11},{10,... | collective-permute-start | bytes 786440 | tf_op jit(solution)/shard_map/ppermute | solution.py:19
  37.0 19.3 %collective-permute-start.16 = (bf16[256,512]{1,0:T(8,128)(2,1)S(1)}, bf16[256,512]{1,0:T(8,128)(2,1)S(1)}, u32[]{:S(2)}, u32[]{:S(2)}) collective-permute-start(bf16[256,512]{1,0:T(8,128)(2,1)S(1)} %pad_maximum_fusion.12), channel_id=1, source_target_pairs={{0,4},{4,0},{8,12},{12,8},{16,20},{20,16},{24,28},{28,24},{1,5},{5... | collective-permute-start | bytes 786440 | tf_op jit(solution)/shard_map/ppermute | solution.py:19
  47.8 22.1 %collective-permute-start.25 = (bf16[256,1536]{1,0:T(8,128)(2,1)S(1)}, bf16[256,1536]{1,0:T(8,128)(2,1)}, u32[]{:S(2)}, u32[]{:S(2)}) collective-permute-start(bf16[256,1536]{1,0:T(8,128)(2,1)S(1)} %pad_maximum_fusion.4), channel_id=1, source_target_pairs={{0,2},{1,3},{2,0},{3,1},{4,6},{5,7},{6,4},{7,5},{8,10},{9,11},{10,... | collective-permute-start | bytes 2359304 | tf_op jit(solution)/shard_map/ppermute | solution.py:19
  52.8 24.8 %collective-permute-start.12 = (bf16[512,512]{1,0:T(8,128)(2,1)S(1)}, bf16[512,512]{1,0:T(8,128)(2,1)}, u32[]{:S(2)}, u32[]{:S(2)}) collective-permute-start(bf16[512,512]{1,0:T(8,128)(2,1)S(1)} %constant_dynamic-update-slice_fusion.2.refs_0_), channel_id=1, source_target_pairs={{0,2},{1,3},{2,0},{3,1},{4,6},{5,7},{6,4},{7,5},{8,10},{9,11},{10,... | collective-permute-start | bytes 1572872 | tf_op jit(solution)/shard_map/ppermute | solution.py:19
  56.4 29.7 %collective-permute-start.23 = (bf16[256,1536]{1,0:T(8,128)(2,1)S(1)}, bf16[256,1536]{1,0:T(8,128)(2,1)}, u32[]{:S(2)}, u32[]{:S(2)}) collective-permute-start(bf16[256,1536]{1,0:T(8,128)(2,1)S(1)} %pad_maximum_fusion.4), channel_id=1, source_target_pairs={{0,4},{4,0},{8,12},{12,8},{16,20},{20,16},{24,28},{28,24},{1,5},{5... | collective-permute-start | bytes 2359304 | tf_op jit(solution)/shard_map/ppermute | solution.py:19
  69.9 33.0 %collective-permute-start.26 = (bf16[256,1536]{1,0:T(8,128)(2,1)}, bf16[256,1536]{1,0:T(8,128)(2,1)}, u32[]{:S(2)}, u32[]{:S(2)}) collective-permute-start(bf16[256,1536]{1,0:T(8,128)(2,1)} %collective-permute-done.25), channel_id=1, source_target_pairs={{0,4},{4,0},{8,12},{12,8},{16,20},{20,16},{24,28},{28,24},{1,5},{5... | collective-permute-start | bytes 2359304 | tf_op jit(solution)/shard_map/ppermute | solution.py:19
  77.5 19.3 %collective-permute-start.3 = (bf16[512,512]{1,0:T(8,128)(2,1)}, bf16[512,512]{1,0:T(8,128)(2,1)}, u32[]{:S(2)}, u32[]{:S(2)}) collective-permute-start(bf16[512,512]{1,0:T(8,128)(2,1)} %pad_maximum_fusion.5.refs_0_), channel_id=1, source_target_pairs={{0,1},{1,0},{2,3},{3,2},{4,5},{5,4},{6,7},{7,6},{8,9},{9,8},{10,11... | collective-permute-start | bytes 1572872 | tf_op jit(solution)/shard_map/ppermute | solution.py:19
  77.6 19.3 %collective-permute-start.6 = (bf16[512,512]{1,0:T(8,128)(2,1)}, bf16[512,512]{1,0:T(8,128)(2,1)}, u32[]{:S(2)}, u32[]{:S(2)}) collective-permute-start(bf16[512,512]{1,0:T(8,128)(2,1)} %constant_dynamic-update-slice_fusion.refs_2_), channel_id=1, source_target_pairs={{0,1},{1,0},{2,3},{3,2},{4,5},{5,4},{6,7},{7,6},{8,9},{9,8},{10,11... | collective-permute-start | bytes 1572872 | tf_op jit(solution)/shard_map/ppermute | solution.py:19
  88.5 27.2 %collective-permute-start.34 = (bf16[256,512]{1,0:T(8,128)(2,1)}, bf16[256,512]{1,0:T(8,128)(2,1)}, u32[]{:S(2)}, u32[]{:S(2)}) collective-permute-start(bf16[256,512]{1,0:T(8,128)(2,1)} %get-tuple-element.214), channel_id=1, source_target_pairs={{0,4},{4,0},{8,12},{12,8},{16,20},{20,16},{24,28},{28,24},{1,5},{5... | collective-permute-start | bytes 786440 | tf_op jit(solution)/shard_map/ppermute | solution.py:19
  90.2 67.4 %collective-permute-start.24 = (bf16[512,1536]{1,0:T(8,128)(2,1)S(1)}, bf16[512,1536]{1,0:T(8,128)(2,1)}, u32[]{:S(2)}, u32[]{:S(2)}) collective-permute-start(bf16[512,1536]{1,0:T(8,128)(2,1)S(1)} %pad_maximum_fusion.refs_0_), channel_id=1, source_target_pairs={{0,1},{1,0},{2,3},{3,2},{4,5},{5,4},{6,7},{7,6},{8,9},{9,8},{10,11... | collective-permute-start | bytes 4718600 | tf_op jit(solution)/shard_map/ppermute | solution.py:19
  104.1 53.6 %collective-permute-start.27 = (bf16[512,1536]{1,0:T(8,128)(2,1)S(1)}, bf16[512,1536]{1,0:T(8,128)(2,1)}, u32[]{:S(2)}, u32[]{:S(2)}) collective-permute-start(bf16[512,1536]{1,0:T(8,128)(2,1)S(1)} %constant_dynamic-update-slice_fusion.13.refs_2_), channel_id=1, source_target_pairs={{0,1},{1,0},{2,3},{3,2},{4,5},{5,4},{6,7},{7,6},{8,9},{9,8},{10,11... | collective-permute-start | bytes 4718600 | tf_op jit(solution)/shard_map/ppermute | solution.py:19
  105.8 22.0 %collective-permute-start.29 = (bf16[2,512,256]{2,1,0:T(8,128)(2,1)}, bf16[2,512,256]{2,1,0:T(8,128)(2,1)}, u32[]{:S(2)}, u32[]{:S(2)}) collective-permute-start(bf16[2,512,256]{2,1,0:T(8,128)(2,1)} %get-tuple-element.78.refs_0_.refs_4_), channel_id=1, source_target_pairs={{0,1},{1,0},{2,3},{3,2},{4,5},{5,4},{6,7},{7,6},{8,9},{9,8},{10,11... | collective-permute-start | bytes 1572872 | tf_op jit(solution)/shard_map/ppermute | solution.py:19
  127.7 17.5 %collective-permute-start.32 = (bf16[2,512,256]{2,1,0:T(8,128)(2,1)}, bf16[2,512,256]{2,1,0:T(8,128)(2,1)}, u32[]{:S(2)}, u32[]{:S(2)}) collective-permute-start(bf16[2,512,256]{2,1,0:T(8,128)(2,1)} %get-tuple-element.76.refs_0_.refs_4_), channel_id=1, source_target_pairs={{0,1},{1,0},{2,3},{3,2},{4,5},{5,4},{6,7},{7,6},{8,9},{9,8},{10,11... | collective-permute-start | bytes 1572872 | tf_op jit(solution)/shard_map/ppermute | solution.py:19
  217.7 27.0 %collective-permute-start.41 = (bf16[256,512]{1,0:T(8,128)(2,1)}, bf16[256,512]{1,0:T(8,128)(2,1)}, u32[]{:S(2)}, u32[]{:S(2)}) collective-permute-start(bf16[256,512]{1,0:T(8,128)(2,1)} %slice.1250), channel_id=1, source_target_pairs={{0,4},{4,0},{8,12},{12,8},{16,20},{20,16},{24,28},{28,24},{1,5},{5... | collective-permute-start | bytes 786440 | tf_op jit(solution)/shard_map/ppermute | solution.py:19
  218.5 16.9 %collective-permute-start.48 = (bf16[512,1152]{1,0:T(8,128)(2,1)}, bf16[512,1152]{1,0:T(8,128)(2,1)S(1)}, u32[]{:S(2)}, u32[]{:S(2)}) collective-permute-start(bf16[512,1152]{1,0:T(8,128)(2,1)} %get-tuple-element.87), channel_id=1, source_target_pairs={{0,1},{1,0},{2,3},{3,2},{4,5},{5,4},{6,7},{7,6},{8,9},{9,8},{10,11... | collective-permute-start | bytes 3538952 | tf_op jit(solution)/shard_map/ppermute | solution.py:19
  218.5 146.6 %collective-permute-start.82 = (bf16[512,1152]{1,0:T(8,128)(2,1)}, bf16[512,1152]{1,0:T(8,128)(2,1)}, u32[]{:S(2)}, u32[]{:S(2)}) collective-permute-start(bf16[512,1152]{1,0:T(8,128)(2,1)} %get-tuple-element.133), channel_id=1, source_target_pairs={{0,1},{1,0},{2,3},{3,2},{4,5},{5,4},{6,7},{7,6},{8,9},{9,8},{10,11... | collective-permute-start | bytes 3538952 | tf_op jit(solution)/shard_map/ppermute | solution.py:19
  243.7 51.0 %collective-permute-start.77 = (bf16[512,384]{1,0:T(8,128)(2,1)}, bf16[512,384]{1,0:T(8,128)(2,1)}, u32[]{:S(2)}, u32[]{:S(2)}) collective-permute-start(bf16[512,384]{1,0:T(8,128)(2,1)} %get-tuple-element.131), channel_id=1, source_target_pairs={{0,1},{1,0},{2,3},{3,2},{4,5},{5,4},{6,7},{7,6},{8,9},{9,8},{10,11... | collective-permute-start | bytes 1179656 | tf_op jit(solution)/shard_map/ppermute | solution.py:19
  246.6 119.0 %collective-permute-start.83 = (bf16[512,1152]{1,0:T(8,128)(2,1)S(1)}, bf16[512,1152]{1,0:T(8,128)(2,1)S(1)}, u32[]{:S(2)}, u32[]{:S(2)}) collective-permute-start(bf16[512,1152]{1,0:T(8,128)(2,1)S(1)} %add_convert_fusion.2), channel_id=1, source_target_pairs={{0,2},{1,3},{2,0},{3,1},{4,6},{5,7},{6,4},{7,5},{8,10},{9,11},{10,... | collective-permute-start | bytes 3538952 | tf_op jit(solution)/shard_map/ppermute | solution.py:19
  247.7 49.5 %collective-permute-start.75 = (bf16[512,384]{1,0:T(8,128)(2,1)}, bf16[512,384]{1,0:T(8,128)(2,1)}, u32[]{:S(2)}, u32[]{:S(2)}) collective-permute-start(bf16[512,384]{1,0:T(8,128)(2,1)} %get-tuple-element.129), channel_id=1, source_target_pairs={{0,1},{1,0},{2,3},{3,2},{4,5},{5,4},{6,7},{7,6},{8,9},{9,8},{10,11... | collective-permute-start | bytes 1179656 | tf_op jit(solution)/shard_map/ppermute | solution.py:19
  307.0 29.2 %collective-permute-start.52 = (bf16[2,512,256]{2,1,0:T(8,128)(2,1)S(1)}, bf16[2,512,256]{2,1,0:T(8,128)(2,1)S(1)}, u32[]{:S(2)}, u32[]{:S(2)}) collective-permute-start(bf16[2,512,256]{2,1,0:T(8,128)(2,1)S(1)} %copy-done.87), channel_id=1, source_target_pairs={{0,1},{1,0},{2,3},{3,2},{4,5},{5,4},{6,7},{7,6},{8,9},{9,8},{10,11... | collective-permute-start | bytes 1572872 | tf_op jit(solution)/shard_map/ppermute | solution.py:19
  321.2 23.8 %collective-permute-start.54 = (bf16[2,512,256]{2,1,0:T(8,128)(2,1)S(1)}, bf16[2,512,256]{2,1,0:T(8,128)(2,1)S(1)}, u32[]{:S(2)}, u32[]{:S(2)}) collective-permute-start(bf16[2,512,256]{2,1,0:T(8,128)(2,1)S(1)} %add_convert_fusion.13), channel_id=1, source_target_pairs={{0,2},{1,3},{2,0},{3,1},{4,6},{5,7},{6,4},{7,5},{8,10},{9,11},{10,... | collective-permute-start | bytes 1572872 | tf_op jit(solution)/shard_map/ppermute | solution.py:19
  364.6 36.8 %collective-permute-start.57 = (bf16[512,512]{1,0:T(8,128)(2,1)}, bf16[512,512]{1,0:T(8,128)(2,1)S(1)}, u32[]{:S(2)}, u32[]{:S(2)}) collective-permute-start(bf16[512,512]{1,0:T(8,128)(2,1)} %get-tuple-element.119), channel_id=1, source_target_pairs={{0,1},{1,0},{2,3},{3,2},{4,5},{5,4},{6,7},{7,6},{8,9},{9,8},{10,11... | collective-permute-start | bytes 1572872 | tf_op jit(solution)/shard_map/ppermute | solution.py:19
  365.1 40.1 %collective-permute-start.69 = (bf16[512,512]{1,0:T(8,128)(2,1)}, bf16[512,512]{1,0:T(8,128)(2,1)S(1)}, u32[]{:S(2)}, u32[]{:S(2)}) collective-permute-start(bf16[512,512]{1,0:T(8,128)(2,1)} %get-tuple-element.125), channel_id=1, source_target_pairs={{0,1},{1,0},{2,3},{3,2},{4,5},{5,4},{6,7},{7,6},{8,9},{9,8},{10,11... | collective-permute-start | bytes 1572872 | tf_op jit(solution)/shard_map/ppermute | solution.py:19
  371.7 30.8 %collective-permute-start.58 = (bf16[512,512]{1,0:T(8,128)(2,1)S(1)}, bf16[512,512]{1,0:T(8,128)(2,1)S(1)}, u32[]{:S(2)}, u32[]{:S(2)}) collective-permute-start(bf16[512,512]{1,0:T(8,128)(2,1)S(1)} %add_convert_fusion.11), channel_id=1, source_target_pairs={{0,2},{1,3},{2,0},{3,1},{4,6},{5,7},{6,4},{7,5},{8,10},{9,11},{10,... | collective-permute-start | bytes 1572872 | tf_op jit(solution)/shard_map/ppermute | solution.py:19
  373.0 19.1 %collective-permute-start.56 = (bf16[256,512]{1,0:T(8,128)(2,1)S(1)}, bf16[256,512]{1,0:T(8,128)(2,1)S(1)}, u32[]{:S(2)}, u32[]{:S(2)}) collective-permute-start(bf16[256,512]{1,0:T(8,128)(2,1)S(1)} %slice.1863), channel_id=1, source_target_pairs={{0,4},{4,0},{8,12},{12,8},{16,20},{20,16},{24,28},{28,24},{1,5},{5... | collective-permute-start | bytes 786440 | tf_op jit(solution)/shard_map/ppermute | solution.py:19
  400.1 21.9 %collective-permute-start.63 = (bf16[256,640]{1,0:T(8,128)(2,1)S(1)}, bf16[256,640]{1,0:T(8,128)(2,1)S(1)}, u32[]{:S(2)}, u32[]{:S(2)}) collective-permute-start(bf16[256,640]{1,0:T(8,128)(2,1)S(1)} %slice.1361), channel_id=1, source_target_pairs={{0,4},{4,0},{8,12},{12,8},{16,20},{20,16},{24,28},{28,24},{1,5},{5... | collective-permute-start | bytes 983048 | tf_op jit(solution)/shard_map/ppermute | solution.py:19
  401.4 20.6 %collective-permute-start.66 = (bf16[256,640]{1,0:T(8,128)(2,1)S(1)}, bf16[256,640]{1,0:T(8,128)(2,1)S(1)}, u32[]{:S(2)}, u32[]{:S(2)}) collective-permute-start(bf16[256,640]{1,0:T(8,128)(2,1)S(1)} %add_convert_fusion.21), channel_id=1, source_target_pairs={{0,2},{1,3},{2,0},{3,1},{4,6},{5,7},{6,4},{7,5},{8,10},{9,11},{10,... | collective-permute-start | bytes 983048 | tf_op jit(solution)/shard_map/ppermute | solution.py:19
  (153 other events, 1452.6 us)
where the time goes:
time: 447 us; the launch traced here: 439 us
  waiting for transfers between devices  133 us (30%)
  Pallas kernels  128 us (29%)
  starting transfers between devices  77.9 us (17%)
  local copies, waits for them, and re-layouts  49.7 us (11%)
  other arithmetic  39.6 us (9%)
  matrix products  8.3 us (2%)
    ppermute x83, waiting for transfers between devices, flip_pair(): lax.ppermute(value, axis, [(i, i ^ 1 << bit) for i in range(lax.axis_size...  129 us
    ppermute x83, starting transfers between devices, flip_pair(): lax.ppermute(value, axis, [(i, i ^ 1 << bit) for i in range(lax.axis_size...  74.8 us
    pallas_call x2, Pallas kernels, attend_backward(): pl.pallas_call(functools.partial(attend_backward_kernel, pieces, heads),...  44.2 us
    pallas_call x6, Pallas kernels, call_kernel(): pl.pallas_call(kernel, out_shape=[jax.ShapeDtypeStruct(shape, dtype) for...  42.4 us
    pallas_call x2, Pallas kernels, attend_forward(): pl.pallas_call(functools.partial(attend_forward_kernel, pieces, heads), o...  25.4 us
    pallas_call x1, Pallas kernels, block_step(): pl.pallas_call(functools.partial(turn_kernel, groups, batch_rows), out_sh...  15.9 us
    unnamed x210, local copies, waits for them, and re-layouts  11.2 us
  transfers between devices with their start and end apart: 87, of which 40 were waited for; matrix products, arithmetic and copies ran while one was open for 19% of the time, Pallas kernels for 24%

commit v1 on v0

--- a/solution.py
+++ b/solution.py
@@ -260,13 +260,20 @@
     weights, smalls = refs[:groups], refs[groups : 2 * groups]
     dqs = refs[2 * groups : 2 * groups + halves]
     pairs = refs[2 * groups + halves : 2 * groups + 2 * halves]
-    out_ref, gg_ref = refs[2 * groups + 2 * halves : 2 * groups + 2 * halves + 2]
-    grads = refs[2 * groups + 2 * halves + 2 :]
+    others = refs[2 * groups + 2 * halves : 2 * groups + 3 * halves]
+    out_ref, gg_ref = refs[2 * groups + 3 * halves : 2 * groups + 3 * halves + 2]
+    grads = refs[2 * groups + 3 * halves + 2 :]
     normed, inverse = normed_of(v_ref[...])
     active_t = (normed * gain_ref[...]).astype(BF16).T
     total = jnp.zeros_like(d_ref[...])
     for i in range(3):
-        parts = [ref[...] for ref in dqs] if i == 0 else [ref[i - 1] for ref in pairs]
+        if i == 0:
+            parts = [ref[...] for ref in dqs]
+        else:
+            parts = [
+                (ref[i - 1].astype(F32) + other[i - 1].astype(F32)).astype(BF16)
+                for ref, other in zip(pairs, others)
+            ]
         error = jnp.concatenate(parts, axis=1) if halves > 1 else parts[0]
         total += mm_nt(error, column_join(weights, i))
         grad = mm(active_t, error).astype(BF16)
@@ -841,10 +848,6 @@
                 pieces[home] = (pieces[home].astype(F32) + other.astype(F32)).astype(BF16)
         kept_pairs.append(pieces[0])
         sent_pairs.append(flip_pair(pieces[1 << top_bit], "mp", top_bit))
-    d_pairs = [
-        (kept_pairs[h].astype(F32) + sent_pairs[halves - 1 - h].astype(F32)).astype(BF16)
-        for h in range(halves)
-    ]
     line_grad = jnp.concatenate(line_grads, axis=0)[:, :, 1:].reshape(mp_n, heads, -1, SUB)
     line_grad = jnp.einsum(
         "ghcl,lk->ghck", line_grad, lane_flip(F32), precision=lax.Precision.HIGHEST
@@ -877,7 +880,8 @@
         *att,
         *smalls,
         *d_queries,
-        *d_pairs,
+        *kept_pairs,
+        *sent_pairs[::-1],
     )
     if fold > 1:
         att_grads = ungroup([grad[:, : 3 * SUB] for grad in att_grads], pair_widths, fold)

time: 447 us -> 439 us (0.982)
  waiting for transfers between devices: 133 us -> 127 us
    ppermute x83, waiting for transfers between devices: 129 us -> 123 us  [flip_pair(): lax.ppermute(value, axis, [(i, i ^ 1 << bit) for i in range(lax.axis_size...]
    unnamed x210 -> x212, local copies, waits for them, and re-layouts: 11.2 us -> 12.7 us
  transfers between devices with their start and end apart: 87 -> 87, of which waited for: 40 -> 40; matrix products, arithmetic and copies ran while one was open for 19% -> 19% of each run, Pallas kernels for 24% -> 25%
where the time goes in v1:
time: 439 us; the launch traced here: 431 us
  Pallas kernels  128 us (29%)
  waiting for transfers between devices  127 us (29%)
  starting transfers between devices  74.5 us (17%)
  local copies, waits for them, and re-layouts  51.3 us (12%)
  other arithmetic  38.8 us (9%)
  matrix products  8.26 us (2%)
    ppermute x83, waiting for transfers between devices, flip_pair(): lax.ppermute(value, axis, [(i, i ^ 1 << bit) for i in range(lax.axis_size...  123 us
    ppermute x83, starting transfers between devices, flip_pair(): lax.ppermute(value, axis, [(i, i ^ 1 << bit) for i in range(lax.axis_size...  71.4 us
    pallas_call x2, Pallas kernels, attend_backward(): pl.pallas_call(functools.partial(attend_backward_kernel, pieces, heads),...  44.2 us
    pallas_call x6, Pallas kernels, call_kernel(): pl.pallas_call(kernel, out_shape=[jax.ShapeDtypeStruct(shape, dtype) for...  42.7 us
    pallas_call x2, Pallas kernels, attend_forward(): pl.pallas_call(functools.partial(attend_forward_kernel, pieces, heads), o...  25.4 us
    pallas_call x1, Pallas kernels, block_step(): pl.pallas_call(functools.partial(turn_kernel, groups, batch_rows), out_sh...  15.9 us
    unnamed x212, local copies, waits for them, and re-layouts  12.7 us
  transfers between devices with their start and end apart: 87, of which 40 were waited for; matrix products, arithmetic and copies ran while one was open for 19% of the time, Pallas kernels for 25%

profile of v1, /device:TPU:0, one launch (start us, length us, event | category | flops | bytes accessed | tf_op | source)
XLA Modules:
  0.0 430.9 jit_solution(6074978387361003124)
XLA Ops:
  4.3 4.1 collective-permute-start
  8.6 2.8 collective-permute-start.8
  26.9 2.9 collective-permute-done.1
  43.2 4.5 %collective-permute-done.22 = bf16[128,1536]{1,0:T(8,128)(2,1)S(1)} collective-permute-done((bf16[128,1536]{1,0:T(8,128)(2,1)S(1)}, bf16[128,1536]{1,0:T(8,128)(2,1)S(1)}, u32[]{:S(2)}, u32[]{:S(2)}) %collective-permute-start.22) | collective-permute-done | bytes 393248 | tf_op jit(solution)/shard_map/ppermute | solution.py:19
  48.4 3.6 collective-permute-done.10
  56.7 6.8 %collective-permute-done.5 = bf16[256,512]{1,0:T(8,128)(2,1)} collective-permute-done((bf16[256,512]{1,0:T(8,128)(2,1)S(1)}, bf16[256,512]{1,0:T(8,128)(2,1)}, u32[]{:S(2)}, u32[]{:S(2)}) %collective-permute-start.5) | collective-permute-done | bytes 262176 | tf_op jit(solution)/shard_map/ppermute | solution.py:19
  63.6 5.6 %collective-permute-done.19 = bf16[256,512]{1,0:T(8,128)(2,1)} collective-permute-done((bf16[256,512]{1,0:T(8,128)(2,1)S(1)}, bf16[256,512]{1,0:T(8,128)(2,1)}, u32[]{:S(2)}, u32[]{:S(2)}) %collective-permute-start.19) | collective-permute-done | bytes 262176 | tf_op jit(solution)/shard_map/ppermute | solution.py:19
  78.2 7.9 %collective-permute-done.23 = bf16[256,1536]{1,0:T(8,128)(2,1)} collective-permute-done((bf16[256,1536]{1,0:T(8,128)(2,1)S(1)}, bf16[256,1536]{1,0:T(8,128)(2,1)}, u32[]{:S(2)}, u32[]{:S(2)}) %collective-permute-start.23) | collective-permute-done | bytes 786464 | tf_op jit(solution)/shard_map/ppermute | solution.py:19
  90.7 6.1 %shard_map.254.v_ref = f32[512,512]{1,0:T(8,128)} custom-call(f32[512,512]{1,0:T(8,128)} %fusion.103.v_ref, f32[1,512]{1,0:T(1,128)} %slice.900.gain_ref, bf16[512,512]{1,0:T(8,128)(2,1)} %copy-done.5, bf16[512,512]{1,0:T(8,128)(2,1)} %copy-done.6, bf16[512,512]{1,0:T(8,128)(2,1)} %collective-permute-done.12.refs_2_, bf16[512,512]{1,0:T(8,128)(2,1)} %copy-done.9, ...), custom_call_target="tpu_custom_call" | custom-call | tf_op jit(solution)/shard_map/pallas_call | solution.py:193
  96.9 4.1 shard_map.255
  106.1 9.1 %collective-permute-done.28.refs_1_.refs_5_ = bf16[2,512,256]{2,1,0:T(8,128)(2,1)} collective-permute-done((bf16[2,512,256]{2,1,0:T(8,128)(2,1)}, bf16[2,512,256]{2,1,0:T(8,128)(2,1)}, u32[]{:S(2)}, u32[]{:S(2)}) %collective-permute-start.28) | collective-permute-done | bytes 524320 | tf_op jit(solution)/shard_map/ppermute | solution.py:19
  132.5 12.9 %attend_forward.2 = (bf16[512,256]{1,0:T(8,128)(2,1)}, f32[2,1,1024]{2,1,0:T(1,128)}, f32[512,256]{1,0:T(8,128)}) custom-call(s32[4]{0:T(128)} %add.471.qpos, s32[8]{0:T(128)} %stack.211.kpos, bf16[512,512]{1,0:T(8,128)(2,1)} %get-tuple-element.74.q_ref, f32[4,2,33,128]{3,2,1,0:T(8,128)} %pad.19.line_ref, ...), custom_call_target="tpu_custom_call" | custom-call | tf_op jit(solution)/shard_map/attend_forward/pallas_call | solution.py:538
  145.4 12.4 %attend_forward.3 = (bf16[512,256]{1,0:T(8,128)(2,1)}, f32[2,1,1024]{2,1,0:T(1,128)}, f32[512,256]{1,0:T(8,128)}) custom-call(s32[4]{0:T(128)} %add.471.qpos, s32[8]{0:T(128)} %stack.211.kpos, bf16[512,512]{1,0:T(8,128)(2,1)} %get-tuple-element.74.q_ref, f32[4,2,33,128]{3,2,1,0:T(8,128)} %pad.19.line_ref, ...), custom_call_target="tpu_custom_call" | custom-call | tf_op jit(solution)/shard_map/attend_forward/pallas_call | solution.py:538
  157.9 5.8 %shard_map.256 = (f32[512,512]{1,0:T(8,128)}, f32[512,512]{1,0:T(8,128)}, f32[512,512]{1,0:T(8,128)}, bf16[512,512]{1,0:T(8,128)(2,1)}) custom-call(f32[512,512]{1,0:T(8,128)} %shard_map.254.v_ref, f32[1,512]{1,0:T(1,128)} %slice.902.gain_ref, bf16[512,1536]{1,0:T(8,128)(2,1)} %copy-done.1, bf16[512,1536]{1,0:T(8,128)(2,1)} %collective-permute-done.24.refs_1_, ...), custom_call_target="tpu_custom_call" | custom-call | tf_op jit(solution)/shard_map/pallas_call | solution.py:193
  170.6 5.2 %fusion.141 = (f32[512]{0:T(512)S(1)}, f32[512]{0:T(512)S(1)}, f32[2,256,512]{2,1,0:T(8,128)}) fusion(f32[2,286,512]{2,1,0:T(8,128)S(1)} %maximum_convert_fusion, f32[512]{0:T(512)S(1)} %bitcast.282, f32[512]{0:T(512)S(1)} %bitcast.284, f32[512]{0:T(512)S(1)} %bitcast.286, f32[512]{0:T(512)S(1)} %bitcast.288, f32[512]{0:T(512)S(1)} %bitcast.290, ...), kind=kLoop, calls=%fused_computation.381 | loop fusion | flops 16776192 | bytes 33622016 | tf_op jit(solution)/shard_map/reduce_sum | solution.py:783
  180.8 3.6 collective-permute-done.39
  189.5 15.9 %turn.1 = (bf16[512,512]{1,0:T(8,128)(2,1)}, f32[512,512]{1,0:T(8,128)}, f32[512,512]{1,0:T(8,128)}, f32[2,512]{1,0:T(2,128)}, f32[2,512]{1,0:T(2,128)}, /*index...) custom-call(f32[512,512]{1,0:T(8,128)} %bitcast.220, ...), custom_call_target="tpu_custom_call" | custom-call | tf_op jit(solution)/shard_map/turn/pallas_call | solution.py:790
  219.4 3.6 multiply_reduce_fusion
  230.3 5.5 %fusion.14 = f32[2,256,512]{2,1,0:T(8,128)} fusion(f32[2,15,512]{2,1,0:T(8,128)S(1)} %get-tuple-element.340, f32[2,15,512]{2,1,0:T(8,128)S(1)} %get-tuple-element.339, f32[2,256,512]{2,1,0:T(8,128)S(1)} %bitcast.219, f32[512]{0:T(512)S(1)} %bitcast.283, f32[512]{0:T(512)S(1)} %bitcast.285, f32[512]{0:T(512)S(1)} %bitcast.287, f32[512]{0:T(512)S(1)} %bitcast.289, ...), kind=kLoop, calls=%fused_computation.57 | loop fusion | flops 23855104 | bytes 2283520 | tf_op jit(solution)/shard_map/add | solution.py:816
  239.0 7.9 %shard_map.257 = (f32[512,512]{1,0:T(8,128)}, f32[1,512]{1,0:T(1,128)}, bf16[512,512]{1,0:T(8,128)(2,1)}, bf16[512,384]{1,0:T(8,128)(2,1)}, bf16[512,384]{1,0:T(...) custom-call(f32[512,512]{1,0:T(8,128)} %bitcast.221, f32[512,512]{1,0:T(8,128)} %get-tuple-element.89.lin_ref, ...), custom_call_target="tpu_custom_call" | custom-call | tf_op jit(solution)/shard_map/pallas_call | solution.py:193
  247.9 22.1 %attend_backward.3 = (bf16[512,256]{1,0:T(8,128)(2,1)}, bf16[2,512,256]{2,1,0:T(8,128)(2,1)}, bf16[2,512,256]{2,1,0:T(8,128)(2,1)}, bf16[2,512,256]{2,1,0:T(8,12...) custom-call(s32[4]{0:T(128)} %add.471.qpos, s32[8]{0:T(128)} %stack.211.kpos, ...), custom_call_target="tpu_custom_call" | custom-call | tf_op jit(solution)/shard_map/attend_backward/pallas_call | solution.py:578
  270.0 22.1 %attend_backward.2 = (bf16[512,256]{1,0:T(8,128)(2,1)}, bf16[2,512,256]{2,1,0:T(8,128)(2,1)}, bf16[2,512,256]{2,1,0:T(8,128)(2,1)}, bf16[2,512,256]{2,1,0:T(8,12...) custom-call(s32[4]{0:T(128)} %add.471.qpos, s32[8]{0:T(128)} %stack.211.kpos, ...), custom_call_target="tpu_custom_call" | custom-call | tf_op jit(solution)/shard_map/attend_backward/pallas_call | solution.py:578
  300.1 5.1 %collective-permute-done.78 = bf16[256,384]{1,0:T(8,128)(2,1)S(1)} collective-permute-done((bf16[256,384]{1,0:T(8,128)(2,1)S(1)}, bf16[256,384]{1,0:T(8,128)(2,1)S(1)}, u32[]{:S(2)}, u32[]{:S(2)}) %collective-permute-start.78) | collective-permute-done | bytes 196640 | tf_op jit(solution)/shard_map/ppermute | solution.py:19
  307.8 3.8 collective-permute-done.76
  327.5 9.7 %collective-permute-done.54.refs_13_ = bf16[2,512,256]{2,1,0:T(8,128)(2,1)S(1)} collective-permute-done((bf16[2,512,256]{2,1,0:T(8,128)(2,1)S(1)}, bf16[2,512,256]{2,1,0:T(8,128)(2,1)S(1)}, u32[]{:S(2)}, u32[]{:S(2)}) %collective-permute-start.54) | collective-permute-done | bytes 524320 | tf_op jit(solution)/shard_map/ppermute | solution.py:19
  337.9 7.0 %shard_map.258 = (f32[512,512]{1,0:T(8,128)}, f32[1,512]{1,0:T(1,128)}, bf16[512,512]{1,0:T(8,128)(2,1)}, bf16[512,512]{1,0:T(8,128)(2,1)}, bf16[512,512]{1,0:T(8,128)(2,1)}, /*index=5*/bf16[512,512]{1,0:T(8,128)(2,1)}) custom-call(f32[512,512]{1,0:T(8,128)} %shard_map.254.v_ref, f32[512,512]{1,0:T(8,128)} %get-tuple-element.92.d_ref, ...), custom_call_target="tpu_custom_call" | custom-call | tf_op jit(solution)/shard_map/pallas_call | solution.py:193
  344.9 11.8 %shard_map.259 = (f32[512,512]{1,0:T(8,128)}, bf16[512,512]{1,0:T(8,128)(2,1)}, bf16[512,512]{1,0:T(8,128)(2,1)}, bf16[512,512]{1,0:T(8,128)(2,1)}, bf16[512,512...) custom-call(f32[512,512]{1,0:T(8,128)} %fusion.103.v_ref, ...), custom_call_target="tpu_custom_call" | custom-call | tf_op jit(solution)/shard_map/pallas_call | solution.py:193
  366.3 12.3 %collective-permute-done.84 = bf16[256,1152]{1,0:T(8,128)(2,1)S(1)} collective-permute-done((bf16[256,1152]{1,0:T(8,128)(2,1)S(1)}, bf16[256,1152]{1,0:T(8,128)(2,1)S(1)}, u32[]{:S(2)}, u32[]{:S(2)}) %collective-permute-start.84) | collective-permute-done | bytes 589856 | tf_op jit(solution)/shard_map/ppermute | solution.py:19
  380.1 4.2 collective-permute-done.56
  387.5 3.3 collective-permute-done.65
  398.0 7.6 %collective-permute-done.71 = bf16[512,512]{1,0:T(8,128)(2,1)S(1)} collective-permute-done((bf16[512,512]{1,0:T(8,128)(2,1)S(1)}, bf16[512,512]{1,0:T(8,128)(2,1)S(1)}, u32[]{:S(2)}, u32[]{:S(2)}) %collective-permute-start.71) | collective-permute-done | bytes 524320 | tf_op jit(solution)/shard_map/ppermute | solution.py:19
  423.1 2.9 collective-permute-done.74
  (560 shorter events, 185.7 us)
Async XLA Ops:
  4.3 18.7 %collective-permute-start = (bf16[64,512]{1,0:T(8,128)(2,1)S(1)}, bf16[64,512]{1,0:T(8,128)(2,1)S(1)}, u32[]{:S(2)}, u32[]{:S(2)}) collective-permute-start(bf16[64,512]{1,0:T(8,128)(2,1)S(1)} %maximum_maximum_fusion), channel_id=1, source_target_pairs={{0,16},{4,20},{8,24},{12,28},{16,0},{20,4},{24,8},{28,12},{1,17},{... | collective-permute-start | bytes 196616 | tf_op jit(solution)/shard_map/ppermute | solution.py:19
  8.6 16.7 %collective-permute-start.8 = (bf16[64,512]{1,0:T(8,128)(2,1)}, bf16[64,512]{1,0:T(8,128)(2,1)S(1)}, u32[]{:S(2)}, u32[]{:S(2)}) collective-permute-start(bf16[64,512]{1,0:T(8,128)(2,1)} %param.17), channel_id=1, source_target_pairs={{0,16},{4,20},{8,24},{12,28},{16,0},{20,4},{24,8},{28,12},{1,17},{... | collective-permute-start | bytes 196616 | tf_op jit(solution)/shard_map/ppermute | solution.py:19
  16.0 20.9 %collective-permute-start.21 = (bf16[64,1536]{1,0:T(8,128)(2,1)S(1)}, bf16[64,1536]{1,0:T(8,128)(2,1)S(1)}, u32[]{:S(2)}, u32[]{:S(2)}) collective-permute-start(bf16[64,1536]{1,0:T(8,128)(2,1)S(1)} %bitcast_dynamic-update-slice_fusion), channel_id=1, source_target_pairs={{0,16},{4,20},{8,24},{12,28},{16,0},{20,4},{24,8},{28,12},{1,17},{... | collective-permute-start | bytes 589832 | tf_op jit(solution)/shard_map/ppermute | solution.py:19
  17.3 19.8 %collective-permute-start.7 = (bf16[256,512]{1,0:T(8,128)(2,1)S(1)}, bf16[256,512]{1,0:T(8,128)(2,1)S(1)}, u32[]{:S(2)}, u32[]{:S(2)}) collective-permute-start(bf16[256,512]{1,0:T(8,128)(2,1)S(1)} %get-tuple-element.216), channel_id=1, source_target_pairs={{0,4},{4,0},{8,12},{12,8},{16,20},{20,16},{24,28},{28,24},{1,5},{5... | collective-permute-start | bytes 786440 | tf_op jit(solution)/shard_map/ppermute | solution.py:19
  29.8 24.5 %collective-permute-start.4 = (bf16[256,512]{1,0:T(8,128)(2,1)S(1)}, bf16[256,512]{1,0:T(8,128)(2,1)S(1)}, u32[]{:S(2)}, u32[]{:S(2)}) collective-permute-start(bf16[256,512]{1,0:T(8,128)(2,1)S(1)} %pad_maximum_fusion.10), channel_id=1, source_target_pairs={{0,2},{1,3},{2,0},{3,1},{4,6},{5,7},{6,4},{7,5},{8,10},{9,11},{10,... | collective-permute-start | bytes 786440 | tf_op jit(solution)/shard_map/ppermute | solution.py:19
  35.3 19.2 %collective-permute-start.18 = (bf16[256,512]{1,0:T(8,128)(2,1)S(1)}, bf16[256,512]{1,0:T(8,128)(2,1)S(1)}, u32[]{:S(2)}, u32[]{:S(2)}) collective-permute-start(bf16[256,512]{1,0:T(8,128)(2,1)S(1)} %pad_maximum_fusion.12), channel_id=1, source_target_pairs={{0,2},{1,3},{2,0},{3,1},{4,6},{5,7},{6,4},{7,5},{8,10},{9,11},{10,... | collective-permute-start | bytes 786440 | tf_op jit(solution)/shard_map/ppermute | solution.py:19
  37.0 19.3 %collective-permute-start.16 = (bf16[256,512]{1,0:T(8,128)(2,1)S(1)}, bf16[256,512]{1,0:T(8,128)(2,1)S(1)}, u32[]{:S(2)}, u32[]{:S(2)}) collective-permute-start(bf16[256,512]{1,0:T(8,128)(2,1)S(1)} %pad_maximum_fusion.12), channel_id=1, source_target_pairs={{0,4},{4,0},{8,12},{12,8},{16,20},{20,16},{24,28},{28,24},{1,5},{5... | collective-permute-start | bytes 786440 | tf_op jit(solution)/shard_map/ppermute | solution.py:19
  47.8 22.1 %collective-permute-start.25 = (bf16[256,1536]{1,0:T(8,128)(2,1)S(1)}, bf16[256,1536]{1,0:T(8,128)(2,1)}, u32[]{:S(2)}, u32[]{:S(2)}) collective-permute-start(bf16[256,1536]{1,0:T(8,128)(2,1)S(1)} %pad_maximum_fusion.4), channel_id=1, source_target_pairs={{0,2},{1,3},{2,0},{3,1},{4,6},{5,7},{6,4},{7,5},{8,10},{9,11},{10,... | collective-permute-start | bytes 2359304 | tf_op jit(solution)/shard_map/ppermute | solution.py:19
  52.8 24.8 %collective-permute-start.12 = (bf16[512,512]{1,0:T(8,128)(2,1)S(1)}, bf16[512,512]{1,0:T(8,128)(2,1)}, u32[]{:S(2)}, u32[]{:S(2)}) collective-permute-start(bf16[512,512]{1,0:T(8,128)(2,1)S(1)} %constant_dynamic-update-slice_fusion.2.refs_0_), channel_id=1, source_target_pairs={{0,2},{1,3},{2,0},{3,1},{4,6},{5,7},{6,4},{7,5},{8,10},{9,11},{10,... | collective-permute-start | bytes 1572872 | tf_op jit(solution)/shard_map/ppermute | solution.py:19
  56.4 29.7 %collective-permute-start.23 = (bf16[256,1536]{1,0:T(8,128)(2,1)S(1)}, bf16[256,1536]{1,0:T(8,128)(2,1)}, u32[]{:S(2)}, u32[]{:S(2)}) collective-permute-start(bf16[256,1536]{1,0:T(8,128)(2,1)S(1)} %pad_maximum_fusion.4), channel_id=1, source_target_pairs={{0,4},{4,0},{8,12},{12,8},{16,20},{20,16},{24,28},{28,24},{1,5},{5... | collective-permute-start | bytes 2359304 | tf_op jit(solution)/shard_map/ppermute | solution.py:19
  69.9 33.0 %collective-permute-start.26 = (bf16[256,1536]{1,0:T(8,128)(2,1)}, bf16[256,1536]{1,0:T(8,128)(2,1)}, u32[]{:S(2)}, u32[]{:S(2)}) collective-permute-start(bf16[256,1536]{1,0:T(8,128)(2,1)} %collective-permute-done.25), channel_id=1, source_target_pairs={{0,4},{4,0},{8,12},{12,8},{16,20},{20,16},{24,28},{28,24},{1,5},{5... | collective-permute-start | bytes 2359304 | tf_op jit(solution)/shard_map/ppermute | solution.py:19
  77.5 19.3 %collective-permute-start.3 = (bf16[512,512]{1,0:T(8,128)(2,1)}, bf16[512,512]{1,0:T(8,128)(2,1)}, u32[]{:S(2)}, u32[]{:S(2)}) collective-permute-start(bf16[512,512]{1,0:T(8,128)(2,1)} %pad_maximum_fusion.5.refs_0_), channel_id=1, source_target_pairs={{0,1},{1,0},{2,3},{3,2},{4,5},{5,4},{6,7},{7,6},{8,9},{9,8},{10,11... | collective-permute-start | bytes 1572872 | tf_op jit(solution)/shard_map/ppermute | solution.py:19
  77.6 19.3 %collective-permute-start.6 = (bf16[512,512]{1,0:T(8,128)(2,1)}, bf16[512,512]{1,0:T(8,128)(2,1)}, u32[]{:S(2)}, u32[]{:S(2)}) collective-permute-start(bf16[512,512]{1,0:T(8,128)(2,1)} %constant_dynamic-update-slice_fusion.refs_2_), channel_id=1, source_target_pairs={{0,1},{1,0},{2,3},{3,2},{4,5},{5,4},{6,7},{7,6},{8,9},{9,8},{10,11... | collective-permute-start | bytes 1572872 | tf_op jit(solution)/shard_map/ppermute | solution.py:19
  88.5 27.2 %collective-permute-start.34 = (bf16[256,512]{1,0:T(8,128)(2,1)}, bf16[256,512]{1,0:T(8,128)(2,1)}, u32[]{:S(2)}, u32[]{:S(2)}) collective-permute-start(bf16[256,512]{1,0:T(8,128)(2,1)} %get-tuple-element.214), channel_id=1, source_target_pairs={{0,4},{4,0},{8,12},{12,8},{16,20},{20,16},{24,28},{28,24},{1,5},{5... | collective-permute-start | bytes 786440 | tf_op jit(solution)/shard_map/ppermute | solution.py:19
  90.2 67.7 %collective-permute-start.24 = (bf16[512,1536]{1,0:T(8,128)(2,1)S(1)}, bf16[512,1536]{1,0:T(8,128)(2,1)}, u32[]{:S(2)}, u32[]{:S(2)}) collective-permute-start(bf16[512,1536]{1,0:T(8,128)(2,1)S(1)} %pad_maximum_fusion.refs_0_), channel_id=1, source_target_pairs={{0,1},{1,0},{2,3},{3,2},{4,5},{5,4},{6,7},{7,6},{8,9},{9,8},{10,11... | collective-permute-start | bytes 4718600 | tf_op jit(solution)/shard_map/ppermute | solution.py:19
  104.1 53.8 %collective-permute-start.27 = (bf16[512,1536]{1,0:T(8,128)(2,1)S(1)}, bf16[512,1536]{1,0:T(8,128)(2,1)}, u32[]{:S(2)}, u32[]{:S(2)}) collective-permute-start(bf16[512,1536]{1,0:T(8,128)(2,1)S(1)} %constant_dynamic-update-slice_fusion.13.refs_2_), channel_id=1, source_target_pairs={{0,1},{1,0},{2,3},{3,2},{4,5},{5,4},{6,7},{7,6},{8,9},{9,8},{10,11... | collective-permute-start | bytes 4718600 | tf_op jit(solution)/shard_map/ppermute | solution.py:19
  105.8 22.0 %collective-permute-start.29 = (bf16[2,512,256]{2,1,0:T(8,128)(2,1)}, bf16[2,512,256]{2,1,0:T(8,128)(2,1)}, u32[]{:S(2)}, u32[]{:S(2)}) collective-permute-start(bf16[2,512,256]{2,1,0:T(8,128)(2,1)} %get-tuple-element.78.refs_0_.refs_4_), channel_id=1, source_target_pairs={{0,1},{1,0},{2,3},{3,2},{4,5},{5,4},{6,7},{7,6},{8,9},{9,8},{10,11... | collective-permute-start | bytes 1572872 | tf_op jit(solution)/shard_map/ppermute | solution.py:19
  127.7 17.7 %collective-permute-start.32 = (bf16[2,512,256]{2,1,0:T(8,128)(2,1)}, bf16[2,512,256]{2,1,0:T(8,128)(2,1)}, u32[]{:S(2)}, u32[]{:S(2)}) collective-permute-start(bf16[2,512,256]{2,1,0:T(8,128)(2,1)} %get-tuple-element.76.refs_0_.refs_4_), channel_id=1, source_target_pairs={{0,1},{1,0},{2,3},{3,2},{4,5},{5,4},{6,7},{7,6},{8,9},{9,8},{10,11... | collective-permute-start | bytes 1572872 | tf_op jit(solution)/shard_map/ppermute | solution.py:19
  128.5 16.9 %collective-permute-start.33 = (bf16[2,512,256]{2,1,0:T(8,128)(2,1)}, bf16[2,512,256]{2,1,0:T(8,128)(2,1)}, u32[]{:S(2)}, u32[]{:S(2)}) collective-permute-start(bf16[2,512,256]{2,1,0:T(8,128)(2,1)} %collective-permute-done.31.refs_1_.refs_5_), channel_id=1, source_target_pairs={{0,1},{1,0},{2,3},{3,2},{4,5},{5,4},{6,7},{7,6},{8,9},{9,8},{10,11... | collective-permute-start | bytes 1572872 | tf_op jit(solution)/shard_map/ppermute | solution.py:19
  218.1 17.7 %collective-permute-start.41 = (bf16[256,512]{1,0:T(8,128)(2,1)}, bf16[256,512]{1,0:T(8,128)(2,1)}, u32[]{:S(2)}, u32[]{:S(2)}) collective-permute-start(bf16[256,512]{1,0:T(8,128)(2,1)} %slice.1250), channel_id=1, source_target_pairs={{0,4},{4,0},{8,12},{12,8},{16,20},{20,16},{24,28},{28,24},{1,5},{5... | collective-permute-start | bytes 786440 | tf_op jit(solution)/shard_map/ppermute | solution.py:19
  218.9 18.9 %collective-permute-start.48 = (bf16[512,1152]{1,0:T(8,128)(2,1)}, bf16[512,1152]{1,0:T(8,128)(2,1)S(1)}, u32[]{:S(2)}, u32[]{:S(2)}) collective-permute-start(bf16[512,1152]{1,0:T(8,128)(2,1)} %get-tuple-element.87), channel_id=1, source_target_pairs={{0,1},{1,0},{2,3},{3,2},{4,5},{5,4},{6,7},{7,6},{8,9},{9,8},{10,11... | collective-permute-start | bytes 3538952 | tf_op jit(solution)/shard_map/ppermute | solution.py:19
  218.9 138.4 %collective-permute-start.82 = (bf16[512,1152]{1,0:T(8,128)(2,1)}, bf16[512,1152]{1,0:T(8,128)(2,1)}, u32[]{:S(2)}, u32[]{:S(2)}) collective-permute-start(bf16[512,1152]{1,0:T(8,128)(2,1)} %get-tuple-element.133), channel_id=1, source_target_pairs={{0,1},{1,0},{2,3},{3,2},{4,5},{5,4},{6,7},{7,6},{8,9},{9,8},{10,11... | collective-permute-start | bytes 3538952 | tf_op jit(solution)/shard_map/ppermute | solution.py:19
  238.0 119.7 %collective-permute-start.83 = (bf16[512,1152]{1,0:T(8,128)(2,1)S(1)}, bf16[512,1152]{1,0:T(8,128)(2,1)S(1)}, u32[]{:S(2)}, u32[]{:S(2)}) collective-permute-start(bf16[512,1152]{1,0:T(8,128)(2,1)S(1)} %add_convert_fusion.2), channel_id=1, source_target_pairs={{0,2},{1,3},{2,0},{3,1},{4,6},{5,7},{6,4},{7,5},{8,10},{9,11},{10,... | collective-permute-start | bytes 3538952 | tf_op jit(solution)/shard_map/ppermute | solution.py:19
  246.9 48.6 %collective-permute-start.75 = (bf16[512,384]{1,0:T(8,128)(2,1)}, bf16[512,384]{1,0:T(8,128)(2,1)S(1)}, u32[]{:S(2)}, u32[]{:S(2)}) collective-permute-start(bf16[512,384]{1,0:T(8,128)(2,1)} %get-tuple-element.129), channel_id=1, source_target_pairs={{0,1},{1,0},{2,3},{3,2},{4,5},{5,4},{6,7},{7,6},{8,9},{9,8},{10,11... | collective-permute-start | bytes 1179656 | tf_op jit(solution)/shard_map/ppermute | solution.py:19
  297.5 16.3 %collective-permute-start.53 = (bf16[2,512,256]{2,1,0:T(8,128)(2,1)S(1)}, bf16[2,512,256]{2,1,0:T(8,128)(2,1)S(1)}, u32[]{:S(2)}, u32[]{:S(2)}) collective-permute-start(bf16[2,512,256]{2,1,0:T(8,128)(2,1)S(1)} %copy-done.90), channel_id=1, source_target_pairs={{0,1},{1,0},{2,3},{3,2},{4,5},{5,4},{6,7},{7,6},{8,9},{9,8},{10,11... | collective-permute-start | bytes 1572872 | tf_op jit(solution)/shard_map/ppermute | solution.py:19
  318.5 18.6 %collective-permute-start.54 = (bf16[2,512,256]{2,1,0:T(8,128)(2,1)S(1)}, bf16[2,512,256]{2,1,0:T(8,128)(2,1)S(1)}, u32[]{:S(2)}, u32[]{:S(2)}) collective-permute-start(bf16[2,512,256]{2,1,0:T(8,128)(2,1)S(1)} %add_convert_fusion.12), channel_id=1, source_target_pairs={{0,2},{1,3},{2,0},{3,1},{4,6},{5,7},{6,4},{7,5},{8,10},{9,11},{10,... | collective-permute-start | bytes 1572872 | tf_op jit(solution)/shard_map/ppermute | solution.py:19
  356.7 37.2 %collective-permute-start.57 = (bf16[512,512]{1,0:T(8,128)(2,1)}, bf16[512,512]{1,0:T(8,128)(2,1)S(1)}, u32[]{:S(2)}, u32[]{:S(2)}) collective-permute-start(bf16[512,512]{1,0:T(8,128)(2,1)} %get-tuple-element.119), channel_id=1, source_target_pairs={{0,1},{1,0},{2,3},{3,2},{4,5},{5,4},{6,7},{7,6},{8,9},{9,8},{10,11... | collective-permute-start | bytes 1572872 | tf_op jit(solution)/shard_map/ppermute | solution.py:19
  357.2 39.2 %collective-permute-start.69 = (bf16[512,512]{1,0:T(8,128)(2,1)}, bf16[512,512]{1,0:T(8,128)(2,1)S(1)}, u32[]{:S(2)}, u32[]{:S(2)}) collective-permute-start(bf16[512,512]{1,0:T(8,128)(2,1)} %get-tuple-element.125), channel_id=1, source_target_pairs={{0,1},{1,0},{2,3},{3,2},{4,5},{5,4},{6,7},{7,6},{8,9},{9,8},{10,11... | collective-permute-start | bytes 1572872 | tf_op jit(solution)/shard_map/ppermute | solution.py:19
  363.9 31.1 %collective-permute-start.58 = (bf16[512,512]{1,0:T(8,128)(2,1)S(1)}, bf16[512,512]{1,0:T(8,128)(2,1)S(1)}, u32[]{:S(2)}, u32[]{:S(2)}) collective-permute-start(bf16[512,512]{1,0:T(8,128)(2,1)S(1)} %add_convert_fusion.11), channel_id=1, source_target_pairs={{0,2},{1,3},{2,0},{3,1},{4,6},{5,7},{6,4},{7,5},{8,10},{9,11},{10,... | collective-permute-start | bytes 1572872 | tf_op jit(solution)/shard_map/ppermute | solution.py:19
  365.2 19.0 %collective-permute-start.56 = (bf16[256,512]{1,0:T(8,128)(2,1)S(1)}, bf16[256,512]{1,0:T(8,128)(2,1)S(1)}, u32[]{:S(2)}, u32[]{:S(2)}) collective-permute-start(bf16[256,512]{1,0:T(8,128)(2,1)S(1)} %slice.1863), channel_id=1, source_target_pairs={{0,4},{4,0},{8,12},{12,8},{16,20},{20,16},{24,28},{28,24},{1,5},{5... | collective-permute-start | bytes 786440 | tf_op jit(solution)/shard_map/ppermute | solution.py:19
  392.5 21.9 %collective-permute-start.63 = (bf16[256,640]{1,0:T(8,128)(2,1)S(1)}, bf16[256,640]{1,0:T(8,128)(2,1)S(1)}, u32[]{:S(2)}, u32[]{:S(2)}) collective-permute-start(bf16[256,640]{1,0:T(8,128)(2,1)S(1)} %slice.1361), channel_id=1, source_target_pairs={{0,4},{4,0},{8,12},{12,8},{16,20},{20,16},{24,28},{28,24},{1,5},{5... | collective-permute-start | bytes 983048 | tf_op jit(solution)/shard_map/ppermute | solution.py:19
  393.9 20.5 %collective-permute-start.66 = (bf16[256,640]{1,0:T(8,128)(2,1)S(1)}, bf16[256,640]{1,0:T(8,128)(2,1)S(1)}, u32[]{:S(2)}, u32[]{:S(2)}) collective-permute-start(bf16[256,640]{1,0:T(8,128)(2,1)S(1)} %add_convert_fusion.19), channel_id=1, source_target_pairs={{0,2},{1,3},{2,0},{3,1},{4,6},{5,7},{6,4},{7,5},{8,10},{9,11},{10,... | collective-permute-start | bytes 983048 | tf_op jit(solution)/shard_map/ppermute | solution.py:19
  (154 other events, 1377.5 us)

commit v2 on v1

--- a/solution.py
+++ b/solution.py
@@ -259,10 +259,9 @@
 def project_backward_kernel(groups, halves, v_ref, d_ref, gain_ref, *refs):
     weights, smalls = refs[:groups], refs[groups : 2 * groups]
     dqs = refs[2 * groups : 2 * groups + halves]
-    pairs = refs[2 * groups + halves : 2 * groups + 2 * halves]
-    others = refs[2 * groups + 2 * halves : 2 * groups + 3 * halves]
-    out_ref, gg_ref = refs[2 * groups + 3 * halves : 2 * groups + 3 * halves + 2]
-    grads = refs[2 * groups + 3 * halves + 2 :]
+    pairs, tail = refs[2 * groups + halves : -2 - groups], refs[-2 - groups :]
+    each = len(pairs) // halves
+    out_ref, gg_ref, grads = tail[0], tail[1], tail[2:]
     normed, inverse = normed_of(v_ref[...])
     active_t = (normed * gain_ref[...]).astype(BF16).T
     total = jnp.zeros_like(d_ref[...])
@@ -271,8 +270,8 @@
             parts = [ref[...] for ref in dqs]
         else:
             parts = [
-                (ref[i - 1].astype(F32) + other[i - 1].astype(F32)).astype(BF16)
-                for ref, other in zip(pairs, others)
+                sum(ref[i - 1].astype(F32) for ref in pairs[h * each : (h + 1) * each]).astype(BF16)
+                for h in range(halves)
             ]
         error = jnp.concatenate(parts, axis=1) if halves > 1 else parts[0]
         total += mm_nt(error, column_join(weights, i))
@@ -327,17 +326,17 @@
 
 
 def turn_kernel(groups, batch_rows, conv_ref, stat_ref, bn_ref, v_ref, up_ref, gains_ref, *refs):
-    weights = refs[:groups]
-    final_ref, out_ref, dpre_ref, gg_ref, sums_ref = refs[groups : groups + 5]
-    grads, pres = refs[groups + 5 : -1], refs[-1]
+    mids, weights = refs[:groups], refs[groups : 2 * groups]
+    final_ref, out_ref, dpre_ref, gg_ref, sums_ref = refs[2 * groups : 2 * groups + 5]
+    grads, pres = refs[2 * groups + 5 : -1], refs[-1]
     part = pres.shape[2]
-    top, bottom = slice(4 * SUB, 4 * SUB + part), slice(4 * SUB + part, 4 * SUB + 2 * part)
+    top, bottom = slice(0, part), slice(part, 2 * part)
     gain_three, gain_four = gains_ref[3:4], gains_ref[4:5]
     mean = stat_ref[0:1] / batch_rows
     white = (conv_ref[...] - mean) * lax.rsqrt(stat_ref[1:2] / batch_rows - mean * mean + EPS)
     bn_pre = bn_ref[0:1] * white + bn_ref[1:2]
     activated = (bn_pre * jax.nn.sigmoid(bn_pre)).astype(BF16)
-    outward = column_join(weights, 3)
+    outward = column_join(mids, 3)
     third = v_ref[...] + mm_nt(activated, outward)
     normed, inverse = normed_of(third)
     active = (normed * gain_three).astype(BF16)
@@ -672,20 +671,13 @@
     start = exchanged(block_input)
     pair_widths = [head_width] * 3
     att_shard = jnp.concatenate([attention_in[0], attention_in[1], attention_in[2], small], axis=1)
-    att_held = gather_groups(att_shard, order_b)
-    rest_widths = [head_width] * 4 + [part] * 2
-    rest_shard = jnp.concatenate(
-        [
-            attention_out.T,
-            pointwise_in[0],
-            pointwise_in[1],
-            pointwise_out.T,
-            late_up,
-            late_down.T,
-        ],
-        axis=1,
-    )
-    rest = listed(gather_groups(rest_shard, order_b), rest_widths)
+    att_held = gather_groups(att_shard, order_a)
+    mid_shard = jnp.concatenate(
+        [attention_out.T, pointwise_in[0], pointwise_in[1], pointwise_out.T], axis=1
+    )
+    late_shard = jnp.concatenate([late_up, late_down.T], axis=1)
+    mid = listed(gather_groups(mid_shard, order_b), [head_width] * 4)
+    late = listed(gather_groups(late_shard, order_a), [part] * 2)
     if fold == 1:
         att = [att_held[delta] for delta in range(mp_n)]
     else:
@@ -768,7 +760,7 @@
         [((rows, features), F32), (wide, F32), (wide, F32), (wide, BF16)],
         after_first,
         gain[2],
-        *rest,
+        *mid,
         *contexts,
     )
     cotangent = exchanged(out_cotangent)
@@ -799,7 +791,7 @@
         + [jax.ShapeDtypeStruct((features, SUB + 2 * wide_part), BF16)] * groups,
         scratch_shapes=[pltpu.VMEM((groups, rows, wide_part), F32)],
         name="turn",
-    )(conv, sums, bn_rows, after_second, cotangent, gains, *rest)
+    )(conv, sums, bn_rows, after_second, cotangent, gains, *mid, *late)
     turn_marks = []
     own_turn = scatter_groups(unlisted(turn_grads, turn_widths), order_a, turn_marks)
 
@@ -826,7 +818,7 @@
         after_second,
         d_third,
         gain[2],
-        *rest,
+        *mid,
         *contexts,
     )
     own_middle = scatter_groups(unlisted(middle_grads, pair_widths), order_b)
@@ -841,12 +833,15 @@
         pieces = dict(zip(kept, grads[1:-1]))
         if fold > 1:
             pieces = {delta: swap_groups(value, mp_n, delta) for delta, value in pieces.items()}
+        kept_pairs.append([pieces[0]])
         for bit in range(top_bit):
             for delta in [d for d in pieces if d >> bit & 1]:
                 other = flip_pair(pieces.pop(delta), "mp", bit)
                 home = delta ^ 1 << bit
-                pieces[home] = (pieces[home].astype(F32) + other.astype(F32)).astype(BF16)
-        kept_pairs.append(pieces[0])
+                if home == 0:
+                    kept_pairs[h].append(other)
+                else:
+                    pieces[home] = (pieces[home].astype(F32) + other.astype(F32)).astype(BF16)
         sent_pairs.append(flip_pair(pieces[1 << top_bit], "mp", top_bit))
     line_grad = jnp.concatenate(line_grads, axis=0)[:, :, 1:].reshape(mp_n, heads, -1, SUB)
     line_grad = jnp.einsum(
@@ -880,8 +875,11 @@
         *att,
         *smalls,
         *d_queries,
-        *kept_pairs,
-        *sent_pairs[::-1],
+        *[
+            part
+            for h in range(halves)
+            for part in kept_pairs[h] + [sent_pairs[halves - 1 - h]]
+        ],
     )
     if fold > 1:
         att_grads = ungroup([grad[:, : 3 * SUB] for grad in att_grads], pair_widths, fold)

time: 439 us -> 450 us (1.025)
  waiting for transfers between devices: 127 us -> 141 us
  local copies, waits for them, and re-layouts: 51.3 us -> 41.4 us
  other arithmetic: 38.8 us -> 43.3 us
    ppermute x83 -> x88, waiting for transfers between devices: 123 us -> 137 us  [flip_pair(): lax.ppermute(value, axis, [(i, i ^ 1 << bit) for i in range(lax.axis_size...]
    unnamed x212 -> x238, local copies, waits for them, and re-layouts: 12.7 us -> 8.8 us
    ppermute x83 -> x88, starting transfers between devices: 71.4 us -> 73.9 us  [flip_pair(): lax.ppermute(value, axis, [(i, i ^ 1 << bit) for i in range(lax.axis_size...]
  transfers between devices with their start and end apart: 87 -> 92, of which waited for: 40 -> 37; matrix products, arithmetic and copies ran while one was open for 19% -> 19% of each run, Pallas kernels for 25% -> 25%
where the time goes in v2:
time: 450 us; the launch traced here: 442 us
  waiting for transfers between devices  141 us (31%)
  Pallas kernels  128 us (28%)
  starting transfers between devices  77 us (17%)
  other arithmetic  43.3 us (10%)
  local copies, waits for them, and re-layouts  41.4 us (9%)
  matrix products  8.01 us (2%)
    ppermute x88, waiting for transfers between devices, flip_pair(): lax.ppermute(value, axis, [(i, i ^ 1 << bit) for i in range(lax.axis_size...  137 us
    ppermute x88, starting transfers between devices, flip_pair(): lax.ppermute(value, axis, [(i, i ^ 1 << bit) for i in range(lax.axis_size...  73.9 us
    pallas_call x2, Pallas kernels, attend_backward(): pl.pallas_call(functools.partial(attend_backward_kernel, pieces, heads),...  45.4 us
    pallas_call x6, Pallas kernels, call_kernel(): pl.pallas_call(kernel, out_shape=[jax.ShapeDtypeStruct(shape, dtype) for...  40.9 us
    pallas_call x2, Pallas kernels, attend_forward(): pl.pallas_call(functools.partial(attend_forward_kernel, pieces, heads), o...  26.2 us
    pallas_call x1, Pallas kernels, block_step(): pl.pallas_call(functools.partial(turn_kernel, groups, batch_rows), out_sh...  15.9 us
  transfers between devices with their start and end apart: 92, of which 37 were waited for; matrix products, arithmetic and copies ran while one was open for 19% of the time, Pallas kernels for 25%

profile of v2, /device:TPU:0, one launch (start us, length us, event | category | flops | bytes accessed | tf_op | source)
XLA Modules:
  0.0 441.9 jit_solution(6138827067098024901)
XLA Ops:
  2.2 4.1 collective-permute-start.20
  31.7 3.3 collective-permute-done.14
  42.1 3.7 collective-permute-done.9
  47.4 4.0 collective-permute-done.2
  52.9 3.1 collective-permute-done.15
  63.1 8.7 %collective-permute-done.4.refs_2_ = bf16[512,512]{1,0:T(8,128)(2,1)S(1)} collective-permute-done((bf16[512,512]{1,0:T(8,128)(2,1)S(1)}, bf16[512,512]{1,0:T(8,128)(2,1)S(1)}, u32[]{:S(2)}, u32[]{:S(2)}) %collective-permute-start.4) | collective-permute-done | bytes 524320 | tf_op jit(solution)/shard_map/ppermute | solution.py:19
  77.8 6.1 %shard_map.254.v_ref = f32[512,512]{1,0:T(8,128)} custom-call(f32[512,512]{1,0:T(8,128)} %fusion.103.v_ref, f32[1,512]{1,0:T(1,128)} %slice.900.gain_ref, bf16[512,512]{1,0:T(8,128)(2,1)} %copy-done.16, bf16[512,512]{1,0:T(8,128)(2,1)} %copy-done.17, bf16[512,512]{1,0:T(8,128)(2,1)} %collective-permute-done.11.refs_2_, ...), custom_call_target="tpu_custom_call" | custom-call | tf_op jit(solution)/shard_map/pallas_call | solution.py:193
  85.7 4.1 shard_map.255
  95.0 14.1 %collective-permute-done.24 = bf16[256,512]{1,0:T(8,128)(2,1)S(1)} collective-permute-done((bf16[256,512]{1,0:T(8,128)(2,1)S(1)}, bf16[256,512]{1,0:T(8,128)(2,1)S(1)}, u32[]{:S(2)}, u32[]{:S(2)}) %collective-permute-start.24) | collective-permute-done | bytes 262176 | tf_op jit(solution)/shard_map/ppermute | solution.py:19
  132.9 13.2 %attend_forward.2 = (bf16[512,256]{1,0:T(8,128)(2,1)}, f32[2,1,1024]{2,1,0:T(1,128)}, f32[512,256]{1,0:T(8,128)}) custom-call(s32[4]{0:T(128)} %add.465.qpos, s32[8]{0:T(128)} %stack.211.kpos, bf16[512,512]{1,0:T(8,128)(2,1)} %get-tuple-element.74.q_ref, f32[4,2,33,128]{3,2,1,0:T(8,128)} %pad.19.line_ref, ...), custom_call_target="tpu_custom_call" | custom-call | tf_op jit(solution)/shard_map/attend_forward/pallas_call | solution.py:537
  146.1 3.9 collective-permute-done.44.refs_6_
  151.6 13.0 %attend_forward.3 = (bf16[512,256]{1,0:T(8,128)(2,1)}, f32[2,1,1024]{2,1,0:T(1,128)}, f32[512,256]{1,0:T(8,128)}) custom-call(s32[4]{0:T(128)} %add.465.qpos, s32[8]{0:T(128)} %stack.211.kpos, bf16[512,512]{1,0:T(8,128)(2,1)} %get-tuple-element.74.q_ref, f32[4,2,33,128]{3,2,1,0:T(8,128)} %pad.19.line_ref, ...), custom_call_target="tpu_custom_call" | custom-call | tf_op jit(solution)/shard_map/attend_forward/pallas_call | solution.py:537
  164.6 4.6 %shard_map.256 = (f32[512,512]{1,0:T(8,128)}, f32[512,512]{1,0:T(8,128)}, f32[512,512]{1,0:T(8,128)}, bf16[512,512]{1,0:T(8,128)(2,1)}) custom-call(f32[512,512]{1,0:T(8,128)} %shard_map.254.v_ref, f32[1,512]{1,0:T(1,128)} %slice.902.gain_ref, bf16[512,512]{1,0:T(8,128)(2,1)} %pad_maximum_fusion.7.refs_0_, bf16[512,512]{1,0:T(8,128)(2,1)} %collective-permute-done.23.refs_1_, ...), custom_call_target="tpu_custom_call" | custom-call | tf_op jit(solution)/shard_map/pallas_call | solution.py:193
  176.2 5.4 %fusion.141 = (f32[512]{0:T(512)S(1)}, f32[512]{0:T(512)S(1)}, f32[2,256,512]{2,1,0:T(8,128)}) fusion(f32[2,286,512]{2,1,0:T(8,128)S(1)} %maximum_convert_fusion, f32[512]{0:T(512)S(1)} %bitcast.292, f32[512]{0:T(512)S(1)} %bitcast.294, f32[512]{0:T(512)S(1)} %bitcast.296, f32[512]{0:T(512)S(1)} %bitcast.298, f32[512]{0:T(512)S(1)} %bitcast.300, ...), kind=kLoop, calls=%fused_computation.378 | loop fusion | flops 16776192 | bytes 33622016 | tf_op jit(solution)/shard_map/reduce_sum | solution.py:775
  196.3 15.9 %turn.1 = (bf16[512,512]{1,0:T(8,128)(2,1)}, f32[512,512]{1,0:T(8,128)}, f32[512,512]{1,0:T(8,128)}, f32[2,512]{1,0:T(2,128)}, f32[2,512]{1,0:T(2,128)}, /*index...) custom-call(f32[512,512]{1,0:T(8,128)} %bitcast.217, ...), custom_call_target="tpu_custom_call" | custom-call | tf_op jit(solution)/shard_map/turn/pallas_call | solution.py:782
  226.2 3.4 multiply_reduce_fusion
  237.1 5.5 %fusion.14 = f32[2,256,512]{2,1,0:T(8,128)} fusion(f32[2,15,512]{2,1,0:T(8,128)S(1)} %get-tuple-element.342, f32[2,15,512]{2,1,0:T(8,128)S(1)} %get-tuple-element.341, f32[2,256,512]{2,1,0:T(8,128)S(1)} %bitcast.216, f32[512]{0:T(512)S(1)} %bitcast.293, f32[512]{0:T(512)S(1)} %bitcast.295, f32[512]{0:T(512)S(1)} %bitcast.297, f32[512]{0:T(512)S(1)} %bitcast.299, ...), kind=kLoop, calls=%fused_computation.56 | loop fusion | flops 23855104 | bytes 2283520 | tf_op jit(solution)/shard_map/add | solution.py:808
  242.9 6.8 %shard_map.257 = (f32[512,512]{1,0:T(8,128)}, f32[1,512]{1,0:T(1,128)}, bf16[512,512]{1,0:T(8,128)(2,1)}, bf16[512,384]{1,0:T(8,128)(2,1)}, bf16[512,384]{1,0:T(...) custom-call(f32[512,512]{1,0:T(8,128)} %bitcast.219, f32[512,512]{1,0:T(8,128)} %get-tuple-element.89.lin_ref, ...), custom_call_target="tpu_custom_call" | custom-call | tf_op jit(solution)/shard_map/pallas_call | solution.py:193
  253.7 22.4 %attend_backward.3 = (bf16[512,256]{1,0:T(8,128)(2,1)}, bf16[2,512,256]{2,1,0:T(8,128)(2,1)}, bf16[2,512,256]{2,1,0:T(8,128)(2,1)}, bf16[2,512,256]{2,1,0:T(8,12...) custom-call(s32[4]{0:T(128)} %add.465.qpos, s32[8]{0:T(128)} %stack.211.kpos, ...), custom_call_target="tpu_custom_call" | custom-call | tf_op jit(solution)/shard_map/attend_backward/pallas_call | solution.py:577
  276.1 23.0 %attend_backward.2 = (bf16[512,256]{1,0:T(8,128)(2,1)}, bf16[2,512,256]{2,1,0:T(8,128)(2,1)}, bf16[2,512,256]{2,1,0:T(8,128)(2,1)}, bf16[2,512,256]{2,1,0:T(8,12...) custom-call(s32[4]{0:T(128)} %add.465.qpos, s32[8]{0:T(128)} %stack.211.kpos, ...), custom_call_target="tpu_custom_call" | custom-call | tf_op jit(solution)/shard_map/attend_backward/pallas_call | solution.py:577
  305.2 4.5 %collective-permute-done.83 = bf16[256,384]{1,0:T(8,128)(2,1)S(1)} collective-permute-done((bf16[256,384]{1,0:T(8,128)(2,1)S(1)}, bf16[256,384]{1,0:T(8,128)(2,1)S(1)}, u32[]{:S(2)}, u32[]{:S(2)}) %collective-permute-start.83) | collective-permute-done | bytes 196640 | tf_op jit(solution)/shard_map/ppermute | solution.py:19
  316.9 4.0 collective-permute-done.85
  323.9 3.3 collective-permute-done.86
  329.3 8.5 %collective-permute-done.56.refs_12_ = bf16[2,512,256]{2,1,0:T(8,128)(2,1)S(1)} collective-permute-done((bf16[2,512,256]{2,1,0:T(8,128)(2,1)S(1)}, bf16[2,512,256]{2,1,0:T(8,128)(2,1)S(1)}, u32[]{:S(2)}, u32[]{:S(2)}) %collective-permute-start.56) | collective-permute-done | bytes 524320 | tf_op jit(solution)/shard_map/ppermute | solution.py:19
  337.8 10.5 %collective-permute-done.59.refs_15_ = bf16[2,512,256]{2,1,0:T(8,128)(2,1)S(1)} collective-permute-done((bf16[2,512,256]{2,1,0:T(8,128)(2,1)S(1)}, bf16[2,512,256]{2,1,0:T(8,128)(2,1)S(1)}, u32[]{:S(2)}, u32[]{:S(2)}) %collective-permute-start.59) | collective-permute-done | bytes 524320 | tf_op jit(solution)/shard_map/ppermute | solution.py:19
  349.1 7.4 %shard_map.258 = (f32[512,512]{1,0:T(8,128)}, f32[1,512]{1,0:T(1,128)}, bf16[512,512]{1,0:T(8,128)(2,1)}, bf16[512,512]{1,0:T(8,128)(2,1)}, bf16[512,512]{1,0:T(8,128)(2,1)}, /*index=5*/bf16[512,512]{1,0:T(8,128)(2,1)}) custom-call(f32[512,512]{1,0:T(8,128)} %shard_map.254.v_ref, f32[512,512]{1,0:T(8,128)} %get-tuple-element.92.d_ref, ...), custom_call_target="tpu_custom_call" | custom-call | tf_op jit(solution)/shard_map/pallas_call | solution.py:193
  356.5 11.9 %shard_map.259 = (f32[512,512]{1,0:T(8,128)}, bf16[512,512]{1,0:T(8,128)(2,1)}, bf16[512,512]{1,0:T(8,128)(2,1)}, bf16[512,512]{1,0:T(8,128)(2,1)}, bf16[512,512...) custom-call(f32[512,512]{1,0:T(8,128)} %fusion.103.v_ref, ...), custom_call_target="tpu_custom_call" | custom-call | tf_op jit(solution)/shard_map/pallas_call | solution.py:193
  377.9 12.6 %collective-permute-done.89 = bf16[256,1152]{1,0:T(8,128)(2,1)S(1)} collective-permute-done((bf16[256,1152]{1,0:T(8,128)(2,1)S(1)}, bf16[256,1152]{1,0:T(8,128)(2,1)S(1)}, u32[]{:S(2)}, u32[]{:S(2)}) %collective-permute-start.89) | collective-permute-done | bytes 589856 | tf_op jit(solution)/shard_map/ppermute | solution.py:19
  391.2 4.9 %collective-permute-done.61 = bf16[256,512]{1,0:T(8,128)(2,1)S(1)} collective-permute-done((bf16[256,512]{1,0:T(8,128)(2,1)S(1)}, bf16[256,512]{1,0:T(8,128)(2,1)S(1)}, u32[]{:S(2)}, u32[]{:S(2)}) %collective-permute-start.61) | collective-permute-done | bytes 262176 | tf_op jit(solution)/shard_map/ppermute | solution.py:19
  398.2 4.3 collective-permute-done.70
  408.6 8.8 %collective-permute-done.76 = bf16[512,512]{1,0:T(8,128)(2,1)S(1)} collective-permute-done((bf16[512,512]{1,0:T(8,128)(2,1)S(1)}, bf16[512,512]{1,0:T(8,128)(2,1)S(1)}, u32[]{:S(2)}, u32[]{:S(2)}) %collective-permute-start.76) | collective-permute-done | bytes 524320 | tf_op jit(solution)/shard_map/ppermute | solution.py:19
  420.8 3.3 collective-permute-done.77
  (600 shorter events, 186.6 us)
Async XLA Ops:
  2.2 27.2 %collective-permute-start.20 = (bf16[64,512]{1,0:T(8,128)(2,1)S(1)}, bf16[64,512]{1,0:T(8,128)(2,1)S(1)}, u32[]{:S(2)}, u32[]{:S(2)}) collective-permute-start(bf16[64,512]{1,0:T(8,128)(2,1)S(1)} %pad_maximum_fusion.23), channel_id=1, source_target_pairs={{0,16},{4,20},{8,24},{12,28},{16,0},{20,4},{24,8},{28,12},{1,17},{... | collective-permute-start | bytes 196616 | tf_op jit(solution)/shard_map/ppermute | solution.py:19
  13.9 24.9 %collective-permute-start.40 = (bf16[64,1024]{1,0:T(8,128)(2,1)S(1)}, bf16[64,1024]{1,0:T(8,128)(2,1)S(1)}, u32[]{:S(2)}, u32[]{:S(2)}) collective-permute-start(bf16[64,1024]{1,0:T(8,128)(2,1)S(1)} %pad_maximum_fusion.21), channel_id=1, source_target_pairs={{0,16},{4,20},{8,24},{12,28},{16,0},{20,4},{24,8},{28,12},{1,17},{... | collective-permute-start | bytes 393224 | tf_op jit(solution)/shard_map/ppermute | solution.py:19
  25.5 34.9 %collective-permute-start.6 = (bf16[256,512]{1,0:T(8,128)(2,1)}, bf16[256,512]{1,0:T(8,128)(2,1)S(1)}, u32[]{:S(2)}, u32[]{:S(2)}) collective-permute-start(bf16[256,512]{1,0:T(8,128)(2,1)} %get-tuple-element.216), channel_id=1, source_target_pairs={{0,4},{4,0},{8,12},{12,8},{16,20},{20,16},{24,28},{28,24},{1,5},{5... | collective-permute-start | bytes 786440 | tf_op jit(solution)/shard_map/ppermute | solution.py:19
  38.8 17.2 %collective-permute-start.15 = (bf16[256,512]{1,0:T(8,128)(2,1)S(1)}, bf16[256,512]{1,0:T(8,128)(2,1)S(1)}, u32[]{:S(2)}, u32[]{:S(2)}) collective-permute-start(bf16[256,512]{1,0:T(8,128)(2,1)S(1)} %pad_maximum_fusion.12), channel_id=1, source_target_pairs={{0,4},{4,0},{8,12},{12,8},{16,20},{20,16},{24,28},{28,24},{1,5},{5... | collective-permute-start | bytes 786440 | tf_op jit(solution)/shard_map/ppermute | solution.py:19
  41.4 17.4 %collective-permute-start.18 = (bf16[256,512]{1,0:T(8,128)(2,1)S(1)}, bf16[256,512]{1,0:T(8,128)(2,1)S(1)}, u32[]{:S(2)}, u32[]{:S(2)}) collective-permute-start(bf16[256,512]{1,0:T(8,128)(2,1)S(1)} %collective-permute-done.17), channel_id=1, source_target_pairs={{0,4},{4,0},{8,12},{12,8},{16,20},{20,16},{24,28},{28,24},{1,5},{5... | collective-permute-start | bytes 786440 | tf_op jit(solution)/shard_map/ppermute | solution.py:19
  62.6 21.5 %collective-permute-start.3 = (bf16[512,512]{1,0:T(8,128)(2,1)S(1)}, bf16[512,512]{1,0:T(8,128)(2,1)S(1)}, u32[]{:S(2)}, u32[]{:S(2)}) collective-permute-start(bf16[512,512]{1,0:T(8,128)(2,1)S(1)} %pad_maximum_fusion.4.refs_0_), channel_id=1, source_target_pairs={{0,1},{1,0},{2,3},{3,2},{4,5},{5,4},{6,7},{7,6},{8,9},{9,8},{10,11... | collective-permute-start | bytes 1572872 | tf_op jit(solution)/shard_map/ppermute | solution.py:19
  72.8 19.6 %collective-permute-start.33 = (bf16[256,512]{1,0:T(8,128)(2,1)}, bf16[256,512]{1,0:T(8,128)(2,1)}, u32[]{:S(2)}, u32[]{:S(2)}) collective-permute-start(bf16[256,512]{1,0:T(8,128)(2,1)} %get-tuple-element.214), channel_id=1, source_target_pairs={{0,4},{4,0},{8,12},{12,8},{16,20},{20,16},{24,28},{28,24},{1,5},{5... | collective-permute-start | bytes 786440 | tf_op jit(solution)/shard_map/ppermute | solution.py:19
  73.6 17.5 %collective-permute-start.21 = (bf16[128,512]{1,0:T(8,128)(2,1)}, bf16[128,512]{1,0:T(8,128)(2,1)S(1)}, u32[]{:S(2)}, u32[]{:S(2)}) collective-permute-start(bf16[128,512]{1,0:T(8,128)(2,1)} %pad_maximum_fusion.20), channel_id=1, source_target_pairs={{0,8},{4,12},{8,0},{12,4},{16,24},{20,28},{24,16},{28,20},{1,9},{5... | collective-permute-start | bytes 393224 | tf_op jit(solution)/shard_map/ppermute | solution.py:19
  76.3 38.5 %collective-permute-start.42 = (bf16[256,1024]{1,0:T(8,128)(2,1)}, bf16[256,1024]{1,0:T(8,128)(2,1)}, u32[]{:S(2)}, u32[]{:S(2)}) collective-permute-start(bf16[256,1024]{1,0:T(8,128)(2,1)} %pad_maximum_fusion.8), channel_id=1, source_target_pairs={{0,4},{4,0},{8,12},{12,8},{16,20},{20,16},{24,28},{28,24},{1,5},{5... | collective-permute-start | bytes 1572872 | tf_op jit(solution)/shard_map/ppermute | solution.py:19
  89.8 23.7 %collective-permute-start.27 = (bf16[2,512,256]{2,1,0:T(8,128)(2,1)}, bf16[2,512,256]{2,1,0:T(8,128)(2,1)S(1)}, u32[]{:S(2)}, u32[]{:S(2)}) collective-permute-start(bf16[2,512,256]{2,1,0:T(8,128)(2,1)} %get-tuple-element.76.refs_0_.refs_4_), channel_id=1, source_target_pairs={{0,2},{1,3},{2,0},{3,1},{4,6},{5,7},{6,4},{7,5},{8,10},{9,11},{10,... | collective-permute-start | bytes 1572872 | tf_op jit(solution)/shard_map/ppermute | solution.py:19
  91.1 17.9 %collective-permute-start.24 = (bf16[256,512]{1,0:T(8,128)(2,1)S(1)}, bf16[256,512]{1,0:T(8,128)(2,1)S(1)}, u32[]{:S(2)}, u32[]{:S(2)}) collective-permute-start(bf16[256,512]{1,0:T(8,128)(2,1)S(1)} %pad_maximum_fusion.13), channel_id=1, source_target_pairs={{0,2},{1,3},{2,0},{3,1},{4,6},{5,7},{6,4},{7,5},{8,10},{9,11},{10,... | collective-permute-start | bytes 786440 | tf_op jit(solution)/shard_map/ppermute | solution.py:19
  91.9 17.7 %collective-permute-start.22 = (bf16[256,512]{1,0:T(8,128)(2,1)S(1)}, bf16[256,512]{1,0:T(8,128)(2,1)S(1)}, u32[]{:S(2)}, u32[]{:S(2)}) collective-permute-start(bf16[256,512]{1,0:T(8,128)(2,1)S(1)} %pad_maximum_fusion.13), channel_id=1, source_target_pairs={{0,4},{4,0},{8,12},{12,8},{16,20},{20,16},{24,28},{28,24},{1,5},{5... | collective-permute-start | bytes 786440 | tf_op jit(solution)/shard_map/ppermute | solution.py:19
  112.9 51.7 %collective-permute-start.23 = (bf16[512,512]{1,0:T(8,128)(2,1)}, bf16[512,512]{1,0:T(8,128)(2,1)}, u32[]{:S(2)}, u32[]{:S(2)}) collective-permute-start(bf16[512,512]{1,0:T(8,128)(2,1)} %pad_maximum_fusion.7.refs_0_), channel_id=1, source_target_pairs={{0,1},{1,0},{2,3},{3,2},{4,5},{5,4},{6,7},{7,6},{8,9},{9,8},{10,11... | collective-permute-start | bytes 1572872 | tf_op jit(solution)/shard_map/ppermute | solution.py:19
  117.0 33.0 %collective-permute-start.44 = (bf16[512,1024]{1,0:T(8,128)(2,1)}, bf16[512,1024]{1,0:T(8,128)(2,1)}, u32[]{:S(2)}, u32[]{:S(2)}) collective-permute-start(bf16[512,1024]{1,0:T(8,128)(2,1)} %pad_maximum_fusion.2.refs_4_), channel_id=1, source_target_pairs={{0,2},{1,3},{2,0},{3,1},{4,6},{5,7},{6,4},{7,5},{8,10},{9,11},{10,... | collective-permute-start | bytes 3145736 | tf_op jit(solution)/shard_map/ppermute | solution.py:19
  125.0 39.6 %collective-permute-start.26 = (bf16[512,512]{1,0:T(8,128)(2,1)S(1)}, bf16[512,512]{1,0:T(8,128)(2,1)}, u32[]{:S(2)}, u32[]{:S(2)}) collective-permute-start(bf16[512,512]{1,0:T(8,128)(2,1)S(1)} %constant_dynamic-update-slice_fusion.6.refs_2_), channel_id=1, source_target_pairs={{0,1},{1,0},{2,3},{3,2},{4,5},{5,4},{6,7},{7,6},{8,9},{9,8},{10,11... | collective-permute-start | bytes 1572872 | tf_op jit(solution)/shard_map/ppermute | solution.py:19
  128.4 21.6 %collective-permute-start.31 = (bf16[2,512,256]{2,1,0:T(8,128)(2,1)S(1)}, bf16[2,512,256]{2,1,0:T(8,128)(2,1)S(1)}, u32[]{:S(2)}, u32[]{:S(2)}) collective-permute-start(bf16[2,512,256]{2,1,0:T(8,128)(2,1)S(1)} %copy-done.4), channel_id=1, source_target_pairs={{0,1},{1,0},{2,3},{3,2},{4,5},{5,4},{6,7},{7,6},{8,9},{9,8},{10,11... | collective-permute-start | bytes 1572872 | tf_op jit(solution)/shard_map/ppermute | solution.py:19
  128.4 22.1 %collective-permute-start.32 = (bf16[2,512,256]{2,1,0:T(8,128)(2,1)}, bf16[2,512,256]{2,1,0:T(8,128)(2,1)S(1)}, u32[]{:S(2)}, u32[]{:S(2)}) collective-permute-start(bf16[2,512,256]{2,1,0:T(8,128)(2,1)} %collective-permute-done.30.refs_1_.refs_5_), channel_id=1, source_target_pairs={{0,1},{1,0},{2,3},{3,2},{4,5},{5,4},{6,7},{7,6},{8,9},{9,8},{10,11... | collective-permute-start | bytes 1572872 | tf_op jit(solution)/shard_map/ppermute | solution.py:19
  150.0 45.3 %collective-permute-start.43 = (bf16[512,1024]{1,0:T(8,128)(2,1)}, bf16[512,1024]{1,0:T(8,128)(2,1)}, u32[]{:S(2)}, u32[]{:S(2)}) collective-permute-start(bf16[512,1024]{1,0:T(8,128)(2,1)} %pad_maximum_fusion.2.refs_4_), channel_id=1, source_target_pairs={{0,1},{1,0},{2,3},{3,2},{4,5},{5,4},{6,7},{7,6},{8,9},{9,8},{10,11... | collective-permute-start | bytes 3145736 | tf_op jit(solution)/shard_map/ppermute | solution.py:19
  150.0 45.3 %collective-permute-start.45 = (bf16[512,1024]{1,0:T(8,128)(2,1)}, bf16[512,1024]{1,0:T(8,128)(2,1)S(1)}, u32[]{:S(2)}, u32[]{:S(2)}) collective-permute-start(bf16[512,1024]{1,0:T(8,128)(2,1)} %collective-permute-done.44.refs_6_), channel_id=1, source_target_pairs={{0,1},{1,0},{2,3},{3,2},{4,5},{5,4},{6,7},{7,6},{8,9},{9,8},{10,11... | collective-permute-start | bytes 3145736 | tf_op jit(solution)/shard_map/ppermute | solution.py:19
  223.5 27.2 %collective-permute-start.46 = (bf16[256,512]{1,0:T(8,128)(2,1)}, bf16[256,512]{1,0:T(8,128)(2,1)}, u32[]{:S(2)}, u32[]{:S(2)}) collective-permute-start(bf16[256,512]{1,0:T(8,128)(2,1)} %slice.1250), channel_id=1, source_target_pairs={{0,4},{4,0},{8,12},{12,8},{16,20},{20,16},{24,28},{28,24},{1,5},{5... | collective-permute-start | bytes 786440 | tf_op jit(solution)/shard_map/ppermute | solution.py:19
  224.9 17.6 %collective-permute-start.53 = (bf16[512,1152]{1,0:T(8,128)(2,1)}, bf16[512,1152]{1,0:T(8,128)(2,1)S(1)}, u32[]{:S(2)}, u32[]{:S(2)}) collective-permute-start(bf16[512,1152]{1,0:T(8,128)(2,1)} %get-tuple-element.87), channel_id=1, source_target_pairs={{0,1},{1,0},{2,3},{3,2},{4,5},{5,4},{6,7},{7,6},{8,9},{9,8},{10,11... | collective-permute-start | bytes 3538952 | tf_op jit(solution)/shard_map/ppermute | solution.py:19
  224.9 144.1 %collective-permute-start.87 = (bf16[512,1152]{1,0:T(8,128)(2,1)}, bf16[512,1152]{1,0:T(8,128)(2,1)}, u32[]{:S(2)}, u32[]{:S(2)}) collective-permute-start(bf16[512,1152]{1,0:T(8,128)(2,1)} %get-tuple-element.133), channel_id=1, source_target_pairs={{0,1},{1,0},{2,3},{3,2},{4,5},{5,4},{6,7},{7,6},{8,9},{9,8},{10,11... | collective-permute-start | bytes 3538952 | tf_op jit(solution)/shard_map/ppermute | solution.py:19
  249.6 52.1 %collective-permute-start.82 = (bf16[512,384]{1,0:T(8,128)(2,1)}, bf16[512,384]{1,0:T(8,128)(2,1)S(1)}, u32[]{:S(2)}, u32[]{:S(2)}) collective-permute-start(bf16[512,384]{1,0:T(8,128)(2,1)} %get-tuple-element.131), channel_id=1, source_target_pairs={{0,1},{1,0},{2,3},{3,2},{4,5},{5,4},{6,7},{7,6},{8,9},{9,8},{10,11... | collective-permute-start | bytes 1179656 | tf_op jit(solution)/shard_map/ppermute | solution.py:19
  252.5 117.0 %collective-permute-start.88 = (bf16[512,1152]{1,0:T(8,128)(2,1)S(1)}, bf16[512,1152]{1,0:T(8,128)(2,1)S(1)}, u32[]{:S(2)}, u32[]{:S(2)}) collective-permute-start(bf16[512,1152]{1,0:T(8,128)(2,1)S(1)} %add_convert_fusion.2), channel_id=1, source_target_pairs={{0,2},{1,3},{2,0},{3,1},{4,6},{5,7},{6,4},{7,5},{8,10},{9,11},{10,... | collective-permute-start | bytes 3538952 | tf_op jit(solution)/shard_map/ppermute | solution.py:19
  253.6 49.8 %collective-permute-start.80 = (bf16[512,384]{1,0:T(8,128)(2,1)}, bf16[512,384]{1,0:T(8,128)(2,1)}, u32[]{:S(2)}, u32[]{:S(2)}) collective-permute-start(bf16[512,384]{1,0:T(8,128)(2,1)} %get-tuple-element.129), channel_id=1, source_target_pairs={{0,1},{1,0},{2,3},{3,2},{4,5},{5,4},{6,7},{7,6},{8,9},{9,8},{10,11... | collective-permute-start | bytes 1179656 | tf_op jit(solution)/shard_map/ppermute | solution.py:19
  327.2 21.1 %collective-permute-start.59 = (bf16[2,512,256]{2,1,0:T(8,128)(2,1)S(1)}, bf16[2,512,256]{2,1,0:T(8,128)(2,1)S(1)}, u32[]{:S(2)}, u32[]{:S(2)}) collective-permute-start(bf16[2,512,256]{2,1,0:T(8,128)(2,1)S(1)} %add_convert_fusion.12), channel_id=1, source_target_pairs={{0,2},{1,3},{2,0},{3,1},{4,6},{5,7},{6,4},{7,5},{8,10},{9,11},{10,... | collective-permute-start | bytes 1572872 | tf_op jit(solution)/shard_map/ppermute | solution.py:19
  368.4 36.2 %collective-permute-start.62 = (bf16[512,512]{1,0:T(8,128)(2,1)}, bf16[512,512]{1,0:T(8,128)(2,1)S(1)}, u32[]{:S(2)}, u32[]{:S(2)}) collective-permute-start(bf16[512,512]{1,0:T(8,128)(2,1)} %get-tuple-element.119), channel_id=1, source_target_pairs={{0,1},{1,0},{2,3},{3,2},{4,5},{5,4},{6,7},{7,6},{8,9},{9,8},{10,11... | collective-permute-start | bytes 1572872 | tf_op jit(solution)/shard_map/ppermute | solution.py:19
  368.9 39.0 %collective-permute-start.74 = (bf16[512,512]{1,0:T(8,128)(2,1)}, bf16[512,512]{1,0:T(8,128)(2,1)S(1)}, u32[]{:S(2)}, u32[]{:S(2)}) collective-permute-start(bf16[512,512]{1,0:T(8,128)(2,1)} %get-tuple-element.125), channel_id=1, source_target_pairs={{0,1},{1,0},{2,3},{3,2},{4,5},{5,4},{6,7},{7,6},{8,9},{9,8},{10,11... | collective-permute-start | bytes 1572872 | tf_op jit(solution)/shard_map/ppermute | solution.py:19
  375.0 30.6 %collective-permute-start.63 = (bf16[512,512]{1,0:T(8,128)(2,1)S(1)}, bf16[512,512]{1,0:T(8,128)(2,1)S(1)}, u32[]{:S(2)}, u32[]{:S(2)}) collective-permute-start(bf16[512,512]{1,0:T(8,128)(2,1)S(1)} %add_convert_fusion.11), channel_id=1, source_target_pairs={{0,2},{1,3},{2,0},{3,1},{4,6},{5,7},{6,4},{7,5},{8,10},{9,11},{10,... | collective-permute-start | bytes 1572872 | tf_op jit(solution)/shard_map/ppermute | solution.py:19
  376.1 19.9 %collective-permute-start.61 = (bf16[256,512]{1,0:T(8,128)(2,1)S(1)}, bf16[256,512]{1,0:T(8,128)(2,1)S(1)}, u32[]{:S(2)}, u32[]{:S(2)}) collective-permute-start(bf16[256,512]{1,0:T(8,128)(2,1)S(1)} %slice.1863), channel_id=1, source_target_pairs={{0,4},{4,0},{8,12},{12,8},{16,20},{20,16},{24,28},{28,24},{1,5},{5... | collective-permute-start | bytes 786440 | tf_op jit(solution)/shard_map/ppermute | solution.py:19
  404.0 21.2 %collective-permute-start.68 = (bf16[256,640]{1,0:T(8,128)(2,1)S(1)}, bf16[256,640]{1,0:T(8,128)(2,1)S(1)}, u32[]{:S(2)}, u32[]{:S(2)}) collective-permute-start(bf16[256,640]{1,0:T(8,128)(2,1)S(1)} %slice.1361), channel_id=1, source_target_pairs={{0,4},{4,0},{8,12},{12,8},{16,20},{20,16},{24,28},{28,24},{1,5},{5... | collective-permute-start | bytes 983048 | tf_op jit(solution)/shard_map/ppermute | solution.py:19
  404.7 20.5 %collective-permute-start.71 = (bf16[256,640]{1,0:T(8,128)(2,1)S(1)}, bf16[256,640]{1,0:T(8,128)(2,1)S(1)}, u32[]{:S(2)}, u32[]{:S(2)}) collective-permute-start(bf16[256,640]{1,0:T(8,128)(2,1)S(1)} %add_convert_fusion.17), channel_id=1, source_target_pairs={{0,2},{1,3},{2,0},{3,1},{4,6},{5,7},{6,4},{7,5},{8,10},{9,11},{10,... | collective-permute-start | bytes 983048 | tf_op jit(solution)/shard_map/ppermute | solution.py:19
  (177 other events, 1427.3 us)

commit v3 on v2

--- a/solution.py
+++ b/solution.py
@@ -704,6 +704,8 @@
     taps = (
         tiny[:, :, bias_rows : bias_rows + channel_part, :tap_n].reshape(channels, tap_n).T.astype(F32)
     )
+    tap_rows = [taps[tap] for tap in range(kernel)]
+    bn_rows = taps[kernel:]
 
     half_of_slot = jnp.stack([batch, 1 - batch]).astype(jnp.int32)
     kept = [0]
@@ -770,12 +772,11 @@
     extended = jnp.concatenate([before[:, 1:], glu, after[:, :margin]], axis=1).astype(F32)
     conv = jnp.zeros((2, block, channels), F32)
     for tap in range(kernel):
-        conv = conv + taps[tap] * extended[:, tap : tap + block]
+        conv = conv + tap_rows[tap] * extended[:, tap : tap + block]
     conv = conv.reshape(rows, channels)
     sums = channel_total(jnp.stack([jnp.sum(conv, axis=0), jnp.sum(conv * conv, axis=0)]))
     bmean = sums[0:1] / batch_rows
     binv = lax.rsqrt(sums[1:2] / batch_rows - bmean * bmean + EPS)
-    bn_rows = taps[kernel:]
 
     wide_part = part * fold
     turn_widths = [head_width, part, part]
@@ -805,7 +806,7 @@
     d_glu = jnp.zeros((2, block, channels), F32)
     tap_grads = []
     for tap in range(kernel):
-        d_glu = d_glu + taps[tap] * d_extended[:, kernel - 1 - tap : kernel - 1 - tap + block]
+        d_glu = d_glu + tap_rows[tap] * d_extended[:, kernel - 1 - tap : kernel - 1 - tap + block]
         tap_grads.append(jnp.sum(extended[:, tap : tap + block] * d_conv, axis=(0, 1)))
     tap_grads = jnp.stack(tap_grads + [local_sums[1], local_sums[0]])
     d_second, gain_two, d_context, *middle_grads = call_kernel(

time: 450 us -> 450 us (level)
  no operation moved by 1% of the time
where the time goes in v3:
time: 450 us; the launch traced here: 442 us
  waiting for transfers between devices  141 us (31%)
  Pallas kernels  128 us (28%)
  starting transfers between devices  77 us (17%)
  other arithmetic  43.3 us (10%)
  local copies, waits for them, and re-layouts  41.4 us (9%)
  matrix products  8.01 us (2%)
    ppermute x88, waiting for transfers between devices, flip_pair(): lax.ppermute(value, axis, [(i, i ^ 1 << bit) for i in range(lax.axis_size...  137 us
    ppermute x88, starting transfers between devices, flip_pair(): lax.ppermute(value, axis, [(i, i ^ 1 << bit) for i in range(lax.axis_size...  73.9 us
    pallas_call x2, Pallas kernels, attend_backward(): pl.pallas_call(functools.partial(attend_backward_kernel, pieces, heads),...  45.4 us
    pallas_call x6, Pallas kernels, call_kernel(): pl.pallas_call(kernel, out_shape=[jax.ShapeDtypeStruct(shape, dtype) for...  40.9 us
    pallas_call x2, Pallas kernels, attend_forward(): pl.pallas_call(functools.partial(attend_forward_kernel, pieces, heads), o...  26.2 us
    pallas_call x1, Pallas kernels, block_step(): pl.pallas_call(functools.partial(turn_kernel, groups, batch_rows), out_sh...  15.9 us
  transfers between devices with their start and end apart: 92, of which 37 were waited for; matrix products, arithmetic and copies ran while one was open for 19% of the time, Pallas kernels for 25%

profile of v3, /device:TPU:0, one launch (start us, length us, event | category | flops | bytes accessed | tf_op | source)
XLA Modules:
  0.0 441.9 jit_solution(6138827067098024901)
XLA Ops:
  2.2 4.1 collective-permute-start.20
  31.7 3.3 collective-permute-done.14
  42.1 3.7 collective-permute-done.9
  47.4 4.0 collective-permute-done.2
  52.9 3.1 collective-permute-done.15
  63.1 8.7 %collective-permute-done.4.refs_2_ = bf16[512,512]{1,0:T(8,128)(2,1)S(1)} collective-permute-done((bf16[512,512]{1,0:T(8,128)(2,1)S(1)}, bf16[512,512]{1,0:T(8,128)(2,1)S(1)}, u32[]{:S(2)}, u32[]{:S(2)}) %collective-permute-start.4) | collective-permute-done | bytes 524320 | tf_op jit(solution)/shard_map/ppermute | solution.py:19
  77.8 6.1 %shard_map.254.v_ref = f32[512,512]{1,0:T(8,128)} custom-call(f32[512,512]{1,0:T(8,128)} %fusion.103.v_ref, f32[1,512]{1,0:T(1,128)} %slice.869.gain_ref, bf16[512,512]{1,0:T(8,128)(2,1)} %copy-done.16, bf16[512,512]{1,0:T(8,128)(2,1)} %copy-done.17, bf16[512,512]{1,0:T(8,128)(2,1)} %collective-permute-done.11.refs_2_, ...), custom_call_target="tpu_custom_call" | custom-call | tf_op jit(solution)/shard_map/pallas_call | solution.py:193
  85.7 4.1 shard_map.255
  95.0 14.1 %collective-permute-done.24 = bf16[256,512]{1,0:T(8,128)(2,1)S(1)} collective-permute-done((bf16[256,512]{1,0:T(8,128)(2,1)S(1)}, bf16[256,512]{1,0:T(8,128)(2,1)S(1)}, u32[]{:S(2)}, u32[]{:S(2)}) %collective-permute-start.24) | collective-permute-done | bytes 262176 | tf_op jit(solution)/shard_map/ppermute | solution.py:19
  132.9 13.2 %attend_forward.2 = (bf16[512,256]{1,0:T(8,128)(2,1)}, f32[2,1,1024]{2,1,0:T(1,128)}, f32[512,256]{1,0:T(8,128)}) custom-call(s32[4]{0:T(128)} %add.465.qpos, s32[8]{0:T(128)} %stack.211.kpos, bf16[512,512]{1,0:T(8,128)(2,1)} %get-tuple-element.74.q_ref, f32[4,2,33,128]{3,2,1,0:T(8,128)} %pad.19.line_ref, ...), custom_call_target="tpu_custom_call" | custom-call | tf_op jit(solution)/shard_map/attend_forward/pallas_call | solution.py:537
  146.1 3.9 collective-permute-done.44.refs_6_
  151.6 13.0 %attend_forward.3 = (bf16[512,256]{1,0:T(8,128)(2,1)}, f32[2,1,1024]{2,1,0:T(1,128)}, f32[512,256]{1,0:T(8,128)}) custom-call(s32[4]{0:T(128)} %add.465.qpos, s32[8]{0:T(128)} %stack.211.kpos, bf16[512,512]{1,0:T(8,128)(2,1)} %get-tuple-element.74.q_ref, f32[4,2,33,128]{3,2,1,0:T(8,128)} %pad.19.line_ref, ...), custom_call_target="tpu_custom_call" | custom-call | tf_op jit(solution)/shard_map/attend_forward/pallas_call | solution.py:537
  164.6 4.6 %shard_map.256 = (f32[512,512]{1,0:T(8,128)}, f32[512,512]{1,0:T(8,128)}, f32[512,512]{1,0:T(8,128)}, bf16[512,512]{1,0:T(8,128)(2,1)}) custom-call(f32[512,512]{1,0:T(8,128)} %shard_map.254.v_ref, f32[1,512]{1,0:T(1,128)} %slice.871.gain_ref, bf16[512,512]{1,0:T(8,128)(2,1)} %pad_maximum_fusion.7.refs_0_, bf16[512,512]{1,0:T(8,128)(2,1)} %collective-permute-done.23.refs_1_, ...), custom_call_target="tpu_custom_call" | custom-call | tf_op jit(solution)/shard_map/pallas_call | solution.py:193
  176.2 5.4 %fusion.141 = (f32[512]{0:T(512)S(1)}, f32[512]{0:T(512)S(1)}, f32[2,256,512]{2,1,0:T(8,128)}) fusion(f32[2,286,512]{2,1,0:T(8,128)S(1)} %maximum_convert_fusion, f32[512]{0:T(512)S(1)} %bitcast.292, f32[512]{0:T(512)S(1)} %bitcast.294, f32[512]{0:T(512)S(1)} %bitcast.296, f32[512]{0:T(512)S(1)} %bitcast.298, f32[512]{0:T(512)S(1)} %bitcast.300, ...), kind=kLoop, calls=%fused_computation.378 | loop fusion | flops 16776192 | bytes 33622016 | tf_op jit(solution)/shard_map/reduce_sum | solution.py:777
  196.3 15.9 %turn.1 = (bf16[512,512]{1,0:T(8,128)(2,1)}, f32[512,512]{1,0:T(8,128)}, f32[512,512]{1,0:T(8,128)}, f32[2,512]{1,0:T(2,128)}, f32[2,512]{1,0:T(2,128)}, /*index...) custom-call(f32[512,512]{1,0:T(8,128)} %bitcast.217, ...), custom_call_target="tpu_custom_call" | custom-call | tf_op jit(solution)/shard_map/turn/pallas_call | solution.py:783
  226.2 3.4 multiply_reduce_fusion
  237.1 5.5 %fusion.14 = f32[2,256,512]{2,1,0:T(8,128)} fusion(f32[2,15,512]{2,1,0:T(8,128)S(1)} %get-tuple-element.342, f32[2,15,512]{2,1,0:T(8,128)S(1)} %get-tuple-element.341, f32[2,256,512]{2,1,0:T(8,128)S(1)} %bitcast.216, f32[512]{0:T(512)S(1)} %bitcast.293, f32[512]{0:T(512)S(1)} %bitcast.295, f32[512]{0:T(512)S(1)} %bitcast.297, f32[512]{0:T(512)S(1)} %bitcast.299, ...), kind=kLoop, calls=%fused_computation.56 | loop fusion | flops 23855104 | bytes 2283520 | tf_op jit(solution)/shard_map/add | solution.py:809
  242.9 6.8 %shard_map.257 = (f32[512,512]{1,0:T(8,128)}, f32[1,512]{1,0:T(1,128)}, bf16[512,512]{1,0:T(8,128)(2,1)}, bf16[512,384]{1,0:T(8,128)(2,1)}, bf16[512,384]{1,0:T(...) custom-call(f32[512,512]{1,0:T(8,128)} %bitcast.219, f32[512,512]{1,0:T(8,128)} %get-tuple-element.89.lin_ref, ...), custom_call_target="tpu_custom_call" | custom-call | tf_op jit(solution)/shard_map/pallas_call | solution.py:193
  253.7 22.4 %attend_backward.3 = (bf16[512,256]{1,0:T(8,128)(2,1)}, bf16[2,512,256]{2,1,0:T(8,128)(2,1)}, bf16[2,512,256]{2,1,0:T(8,128)(2,1)}, bf16[2,512,256]{2,1,0:T(8,12...) custom-call(s32[4]{0:T(128)} %add.465.qpos, s32[8]{0:T(128)} %stack.211.kpos, ...), custom_call_target="tpu_custom_call" | custom-call | tf_op jit(solution)/shard_map/attend_backward/pallas_call | solution.py:577
  276.1 23.0 %attend_backward.2 = (bf16[512,256]{1,0:T(8,128)(2,1)}, bf16[2,512,256]{2,1,0:T(8,128)(2,1)}, bf16[2,512,256]{2,1,0:T(8,128)(2,1)}, bf16[2,512,256]{2,1,0:T(8,12...) custom-call(s32[4]{0:T(128)} %add.465.qpos, s32[8]{0:T(128)} %stack.211.kpos, ...), custom_call_target="tpu_custom_call" | custom-call | tf_op jit(solution)/shard_map/attend_backward/pallas_call | solution.py:577
  305.2 4.5 %collective-permute-done.83 = bf16[256,384]{1,0:T(8,128)(2,1)S(1)} collective-permute-done((bf16[256,384]{1,0:T(8,128)(2,1)S(1)}, bf16[256,384]{1,0:T(8,128)(2,1)S(1)}, u32[]{:S(2)}, u32[]{:S(2)}) %collective-permute-start.83) | collective-permute-done | bytes 196640 | tf_op jit(solution)/shard_map/ppermute | solution.py:19
  316.9 4.0 collective-permute-done.85
  323.9 3.3 collective-permute-done.86
  329.3 8.5 %collective-permute-done.56.refs_12_ = bf16[2,512,256]{2,1,0:T(8,128)(2,1)S(1)} collective-permute-done((bf16[2,512,256]{2,1,0:T(8,128)(2,1)S(1)}, bf16[2,512,256]{2,1,0:T(8,128)(2,1)S(1)}, u32[]{:S(2)}, u32[]{:S(2)}) %collective-permute-start.56) | collective-permute-done | bytes 524320 | tf_op jit(solution)/shard_map/ppermute | solution.py:19
  337.8 10.5 %collective-permute-done.59.refs_15_ = bf16[2,512,256]{2,1,0:T(8,128)(2,1)S(1)} collective-permute-done((bf16[2,512,256]{2,1,0:T(8,128)(2,1)S(1)}, bf16[2,512,256]{2,1,0:T(8,128)(2,1)S(1)}, u32[]{:S(2)}, u32[]{:S(2)}) %collective-permute-start.59) | collective-permute-done | bytes 524320 | tf_op jit(solution)/shard_map/ppermute | solution.py:19
  349.1 7.4 %shard_map.258 = (f32[512,512]{1,0:T(8,128)}, f32[1,512]{1,0:T(1,128)}, bf16[512,512]{1,0:T(8,128)(2,1)}, bf16[512,512]{1,0:T(8,128)(2,1)}, bf16[512,512]{1,0:T(8,128)(2,1)}, /*index=5*/bf16[512,512]{1,0:T(8,128)(2,1)}) custom-call(f32[512,512]{1,0:T(8,128)} %shard_map.254.v_ref, f32[512,512]{1,0:T(8,128)} %get-tuple-element.92.d_ref, ...), custom_call_target="tpu_custom_call" | custom-call | tf_op jit(solution)/shard_map/pallas_call | solution.py:193
  356.5 11.9 %shard_map.259 = (f32[512,512]{1,0:T(8,128)}, bf16[512,512]{1,0:T(8,128)(2,1)}, bf16[512,512]{1,0:T(8,128)(2,1)}, bf16[512,512]{1,0:T(8,128)(2,1)}, bf16[512,512...) custom-call(f32[512,512]{1,0:T(8,128)} %fusion.103.v_ref, ...), custom_call_target="tpu_custom_call" | custom-call | tf_op jit(solution)/shard_map/pallas_call | solution.py:193
  377.9 12.6 %collective-permute-done.89 = bf16[256,1152]{1,0:T(8,128)(2,1)S(1)} collective-permute-done((bf16[256,1152]{1,0:T(8,128)(2,1)S(1)}, bf16[256,1152]{1,0:T(8,128)(2,1)S(1)}, u32[]{:S(2)}, u32[]{:S(2)}) %collective-permute-start.89) | collective-permute-done | bytes 589856 | tf_op jit(solution)/shard_map/ppermute | solution.py:19
  391.2 4.9 %collective-permute-done.61 = bf16[256,512]{1,0:T(8,128)(2,1)S(1)} collective-permute-done((bf16[256,512]{1,0:T(8,128)(2,1)S(1)}, bf16[256,512]{1,0:T(8,128)(2,1)S(1)}, u32[]{:S(2)}, u32[]{:S(2)}) %collective-permute-start.61) | collective-permute-done | bytes 262176 | tf_op jit(solution)/shard_map/ppermute | solution.py:19
  398.2 4.3 collective-permute-done.70
  408.6 8.8 %collective-permute-done.76 = bf16[512,512]{1,0:T(8,128)(2,1)S(1)} collective-permute-done((bf16[512,512]{1,0:T(8,128)(2,1)S(1)}, bf16[512,512]{1,0:T(8,128)(2,1)S(1)}, u32[]{:S(2)}, u32[]{:S(2)}) %collective-permute-start.76) | collective-permute-done | bytes 524320 | tf_op jit(solution)/shard_map/ppermute | solution.py:19
  420.8 3.3 collective-permute-done.77
  (600 shorter events, 186.6 us)
Async XLA Ops:
  2.2 27.2 %collective-permute-start.20 = (bf16[64,512]{1,0:T(8,128)(2,1)S(1)}, bf16[64,512]{1,0:T(8,128)(2,1)S(1)}, u32[]{:S(2)}, u32[]{:S(2)}) collective-permute-start(bf16[64,512]{1,0:T(8,128)(2,1)S(1)} %pad_maximum_fusion.23), channel_id=1, source_target_pairs={{0,16},{4,20},{8,24},{12,28},{16,0},{20,4},{24,8},{28,12},{1,17},{... | collective-permute-start | bytes 196616 | tf_op jit(solution)/shard_map/ppermute | solution.py:19
  13.9 24.9 %collective-permute-start.40 = (bf16[64,1024]{1,0:T(8,128)(2,1)S(1)}, bf16[64,1024]{1,0:T(8,128)(2,1)S(1)}, u32[]{:S(2)}, u32[]{:S(2)}) collective-permute-start(bf16[64,1024]{1,0:T(8,128)(2,1)S(1)} %pad_maximum_fusion.21), channel_id=1, source_target_pairs={{0,16},{4,20},{8,24},{12,28},{16,0},{20,4},{24,8},{28,12},{1,17},{... | collective-permute-start | bytes 393224 | tf_op jit(solution)/shard_map/ppermute | solution.py:19
  25.5 34.9 %collective-permute-start.6 = (bf16[256,512]{1,0:T(8,128)(2,1)}, bf16[256,512]{1,0:T(8,128)(2,1)S(1)}, u32[]{:S(2)}, u32[]{:S(2)}) collective-permute-start(bf16[256,512]{1,0:T(8,128)(2,1)} %get-tuple-element.216), channel_id=1, source_target_pairs={{0,4},{4,0},{8,12},{12,8},{16,20},{20,16},{24,28},{28,24},{1,5},{5... | collective-permute-start | bytes 786440 | tf_op jit(solution)/shard_map/ppermute | solution.py:19
  38.8 17.2 %collective-permute-start.15 = (bf16[256,512]{1,0:T(8,128)(2,1)S(1)}, bf16[256,512]{1,0:T(8,128)(2,1)S(1)}, u32[]{:S(2)}, u32[]{:S(2)}) collective-permute-start(bf16[256,512]{1,0:T(8,128)(2,1)S(1)} %pad_maximum_fusion.12), channel_id=1, source_target_pairs={{0,4},{4,0},{8,12},{12,8},{16,20},{20,16},{24,28},{28,24},{1,5},{5... | collective-permute-start | bytes 786440 | tf_op jit(solution)/shard_map/ppermute | solution.py:19
  41.4 17.4 %collective-permute-start.18 = (bf16[256,512]{1,0:T(8,128)(2,1)S(1)}, bf16[256,512]{1,0:T(8,128)(2,1)S(1)}, u32[]{:S(2)}, u32[]{:S(2)}) collective-permute-start(bf16[256,512]{1,0:T(8,128)(2,1)S(1)} %collective-permute-done.17), channel_id=1, source_target_pairs={{0,4},{4,0},{8,12},{12,8},{16,20},{20,16},{24,28},{28,24},{1,5},{5... | collective-permute-start | bytes 786440 | tf_op jit(solution)/shard_map/ppermute | solution.py:19
  62.6 21.5 %collective-permute-start.3 = (bf16[512,512]{1,0:T(8,128)(2,1)S(1)}, bf16[512,512]{1,0:T(8,128)(2,1)S(1)}, u32[]{:S(2)}, u32[]{:S(2)}) collective-permute-start(bf16[512,512]{1,0:T(8,128)(2,1)S(1)} %pad_maximum_fusion.4.refs_0_), channel_id=1, source_target_pairs={{0,1},{1,0},{2,3},{3,2},{4,5},{5,4},{6,7},{7,6},{8,9},{9,8},{10,11... | collective-permute-start | bytes 1572872 | tf_op jit(solution)/shard_map/ppermute | solution.py:19
  72.8 19.6 %collective-permute-start.33 = (bf16[256,512]{1,0:T(8,128)(2,1)}, bf16[256,512]{1,0:T(8,128)(2,1)}, u32[]{:S(2)}, u32[]{:S(2)}) collective-permute-start(bf16[256,512]{1,0:T(8,128)(2,1)} %get-tuple-element.214), channel_id=1, source_target_pairs={{0,4},{4,0},{8,12},{12,8},{16,20},{20,16},{24,28},{28,24},{1,5},{5... | collective-permute-start | bytes 786440 | tf_op jit(solution)/shard_map/ppermute | solution.py:19
  73.6 17.5 %collective-permute-start.21 = (bf16[128,512]{1,0:T(8,128)(2,1)}, bf16[128,512]{1,0:T(8,128)(2,1)S(1)}, u32[]{:S(2)}, u32[]{:S(2)}) collective-permute-start(bf16[128,512]{1,0:T(8,128)(2,1)} %pad_maximum_fusion.20), channel_id=1, source_target_pairs={{0,8},{4,12},{8,0},{12,4},{16,24},{20,28},{24,16},{28,20},{1,9},{5... | collective-permute-start | bytes 393224 | tf_op jit(solution)/shard_map/ppermute | solution.py:19
  76.3 38.5 %collective-permute-start.42 = (bf16[256,1024]{1,0:T(8,128)(2,1)}, bf16[256,1024]{1,0:T(8,128)(2,1)}, u32[]{:S(2)}, u32[]{:S(2)}) collective-permute-start(bf16[256,1024]{1,0:T(8,128)(2,1)} %pad_maximum_fusion.8), channel_id=1, source_target_pairs={{0,4},{4,0},{8,12},{12,8},{16,20},{20,16},{24,28},{28,24},{1,5},{5... | collective-permute-start | bytes 1572872 | tf_op jit(solution)/shard_map/ppermute | solution.py:19
  89.8 23.7 %collective-permute-start.27 = (bf16[2,512,256]{2,1,0:T(8,128)(2,1)}, bf16[2,512,256]{2,1,0:T(8,128)(2,1)S(1)}, u32[]{:S(2)}, u32[]{:S(2)}) collective-permute-start(bf16[2,512,256]{2,1,0:T(8,128)(2,1)} %get-tuple-element.76.refs_0_.refs_4_), channel_id=1, source_target_pairs={{0,2},{1,3},{2,0},{3,1},{4,6},{5,7},{6,4},{7,5},{8,10},{9,11},{10,... | collective-permute-start | bytes 1572872 | tf_op jit(solution)/shard_map/ppermute | solution.py:19
  91.1 17.9 %collective-permute-start.24 = (bf16[256,512]{1,0:T(8,128)(2,1)S(1)}, bf16[256,512]{1,0:T(8,128)(2,1)S(1)}, u32[]{:S(2)}, u32[]{:S(2)}) collective-permute-start(bf16[256,512]{1,0:T(8,128)(2,1)S(1)} %pad_maximum_fusion.13), channel_id=1, source_target_pairs={{0,2},{1,3},{2,0},{3,1},{4,6},{5,7},{6,4},{7,5},{8,10},{9,11},{10,... | collective-permute-start | bytes 786440 | tf_op jit(solution)/shard_map/ppermute | solution.py:19
  91.9 17.7 %collective-permute-start.22 = (bf16[256,512]{1,0:T(8,128)(2,1)S(1)}, bf16[256,512]{1,0:T(8,128)(2,1)S(1)}, u32[]{:S(2)}, u32[]{:S(2)}) collective-permute-start(bf16[256,512]{1,0:T(8,128)(2,1)S(1)} %pad_maximum_fusion.13), channel_id=1, source_target_pairs={{0,4},{4,0},{8,12},{12,8},{16,20},{20,16},{24,28},{28,24},{1,5},{5... | collective-permute-start | bytes 786440 | tf_op jit(solution)/shard_map/ppermute | solution.py:19
  112.9 51.7 %collective-permute-start.23 = (bf16[512,512]{1,0:T(8,128)(2,1)}, bf16[512,512]{1,0:T(8,128)(2,1)}, u32[]{:S(2)}, u32[]{:S(2)}) collective-permute-start(bf16[512,512]{1,0:T(8,128)(2,1)} %pad_maximum_fusion.7.refs_0_), channel_id=1, source_target_pairs={{0,1},{1,0},{2,3},{3,2},{4,5},{5,4},{6,7},{7,6},{8,9},{9,8},{10,11... | collective-permute-start | bytes 1572872 | tf_op jit(solution)/shard_map/ppermute | solution.py:19
  117.0 33.0 %collective-permute-start.44 = (bf16[512,1024]{1,0:T(8,128)(2,1)}, bf16[512,1024]{1,0:T(8,128)(2,1)}, u32[]{:S(2)}, u32[]{:S(2)}) collective-permute-start(bf16[512,1024]{1,0:T(8,128)(2,1)} %pad_maximum_fusion.2.refs_4_), channel_id=1, source_target_pairs={{0,2},{1,3},{2,0},{3,1},{4,6},{5,7},{6,4},{7,5},{8,10},{9,11},{10,... | collective-permute-start | bytes 3145736 | tf_op jit(solution)/shard_map/ppermute | solution.py:19
  125.0 39.6 %collective-permute-start.26 = (bf16[512,512]{1,0:T(8,128)(2,1)S(1)}, bf16[512,512]{1,0:T(8,128)(2,1)}, u32[]{:S(2)}, u32[]{:S(2)}) collective-permute-start(bf16[512,512]{1,0:T(8,128)(2,1)S(1)} %constant_dynamic-update-slice_fusion.6.refs_2_), channel_id=1, source_target_pairs={{0,1},{1,0},{2,3},{3,2},{4,5},{5,4},{6,7},{7,6},{8,9},{9,8},{10,11... | collective-permute-start | bytes 1572872 | tf_op jit(solution)/shard_map/ppermute | solution.py:19
  128.4 21.6 %collective-permute-start.31 = (bf16[2,512,256]{2,1,0:T(8,128)(2,1)S(1)}, bf16[2,512,256]{2,1,0:T(8,128)(2,1)S(1)}, u32[]{:S(2)}, u32[]{:S(2)}) collective-permute-start(bf16[2,512,256]{2,1,0:T(8,128)(2,1)S(1)} %copy-done.4), channel_id=1, source_target_pairs={{0,1},{1,0},{2,3},{3,2},{4,5},{5,4},{6,7},{7,6},{8,9},{9,8},{10,11... | collective-permute-start | bytes 1572872 | tf_op jit(solution)/shard_map/ppermute | solution.py:19
  128.4 22.1 %collective-permute-start.32 = (bf16[2,512,256]{2,1,0:T(8,128)(2,1)}, bf16[2,512,256]{2,1,0:T(8,128)(2,1)S(1)}, u32[]{:S(2)}, u32[]{:S(2)}) collective-permute-start(bf16[2,512,256]{2,1,0:T(8,128)(2,1)} %collective-permute-done.30.refs_1_.refs_5_), channel_id=1, source_target_pairs={{0,1},{1,0},{2,3},{3,2},{4,5},{5,4},{6,7},{7,6},{8,9},{9,8},{10,11... | collective-permute-start | bytes 1572872 | tf_op jit(solution)/shard_map/ppermute | solution.py:19
  150.0 45.3 %collective-permute-start.43 = (bf16[512,1024]{1,0:T(8,128)(2,1)}, bf16[512,1024]{1,0:T(8,128)(2,1)}, u32[]{:S(2)}, u32[]{:S(2)}) collective-permute-start(bf16[512,1024]{1,0:T(8,128)(2,1)} %pad_maximum_fusion.2.refs_4_), channel_id=1, source_target_pairs={{0,1},{1,0},{2,3},{3,2},{4,5},{5,4},{6,7},{7,6},{8,9},{9,8},{10,11... | collective-permute-start | bytes 3145736 | tf_op jit(solution)/shard_map/ppermute | solution.py:19
  150.0 45.3 %collective-permute-start.45 = (bf16[512,1024]{1,0:T(8,128)(2,1)}, bf16[512,1024]{1,0:T(8,128)(2,1)S(1)}, u32[]{:S(2)}, u32[]{:S(2)}) collective-permute-start(bf16[512,1024]{1,0:T(8,128)(2,1)} %collective-permute-done.44.refs_6_), channel_id=1, source_target_pairs={{0,1},{1,0},{2,3},{3,2},{4,5},{5,4},{6,7},{7,6},{8,9},{9,8},{10,11... | collective-permute-start | bytes 3145736 | tf_op jit(solution)/shard_map/ppermute | solution.py:19
  223.5 27.2 %collective-permute-start.46 = (bf16[256,512]{1,0:T(8,128)(2,1)}, bf16[256,512]{1,0:T(8,128)(2,1)}, u32[]{:S(2)}, u32[]{:S(2)}) collective-permute-start(bf16[256,512]{1,0:T(8,128)(2,1)} %slice.1219), channel_id=1, source_target_pairs={{0,4},{4,0},{8,12},{12,8},{16,20},{20,16},{24,28},{28,24},{1,5},{5... | collective-permute-start | bytes 786440 | tf_op jit(solution)/shard_map/ppermute | solution.py:19
  224.9 17.6 %collective-permute-start.53 = (bf16[512,1152]{1,0:T(8,128)(2,1)}, bf16[512,1152]{1,0:T(8,128)(2,1)S(1)}, u32[]{:S(2)}, u32[]{:S(2)}) collective-permute-start(bf16[512,1152]{1,0:T(8,128)(2,1)} %get-tuple-element.87), channel_id=1, source_target_pairs={{0,1},{1,0},{2,3},{3,2},{4,5},{5,4},{6,7},{7,6},{8,9},{9,8},{10,11... | collective-permute-start | bytes 3538952 | tf_op jit(solution)/shard_map/ppermute | solution.py:19
  224.9 144.1 %collective-permute-start.87 = (bf16[512,1152]{1,0:T(8,128)(2,1)}, bf16[512,1152]{1,0:T(8,128)(2,1)}, u32[]{:S(2)}, u32[]{:S(2)}) collective-permute-start(bf16[512,1152]{1,0:T(8,128)(2,1)} %get-tuple-element.133), channel_id=1, source_target_pairs={{0,1},{1,0},{2,3},{3,2},{4,5},{5,4},{6,7},{7,6},{8,9},{9,8},{10,11... | collective-permute-start | bytes 3538952 | tf_op jit(solution)/shard_map/ppermute | solution.py:19
  249.6 52.1 %collective-permute-start.82 = (bf16[512,384]{1,0:T(8,128)(2,1)}, bf16[512,384]{1,0:T(8,128)(2,1)S(1)}, u32[]{:S(2)}, u32[]{:S(2)}) collective-permute-start(bf16[512,384]{1,0:T(8,128)(2,1)} %get-tuple-element.131), channel_id=1, source_target_pairs={{0,1},{1,0},{2,3},{3,2},{4,5},{5,4},{6,7},{7,6},{8,9},{9,8},{10,11... | collective-permute-start | bytes 1179656 | tf_op jit(solution)/shard_map/ppermute | solution.py:19
  252.5 117.0 %collective-permute-start.88 = (bf16[512,1152]{1,0:T(8,128)(2,1)S(1)}, bf16[512,1152]{1,0:T(8,128)(2,1)S(1)}, u32[]{:S(2)}, u32[]{:S(2)}) collective-permute-start(bf16[512,1152]{1,0:T(8,128)(2,1)S(1)} %add_convert_fusion.2), channel_id=1, source_target_pairs={{0,2},{1,3},{2,0},{3,1},{4,6},{5,7},{6,4},{7,5},{8,10},{9,11},{10,... | collective-permute-start | bytes 3538952 | tf_op jit(solution)/shard_map/ppermute | solution.py:19
  253.6 49.8 %collective-permute-start.80 = (bf16[512,384]{1,0:T(8,128)(2,1)}, bf16[512,384]{1,0:T(8,128)(2,1)}, u32[]{:S(2)}, u32[]{:S(2)}) collective-permute-start(bf16[512,384]{1,0:T(8,128)(2,1)} %get-tuple-element.129), channel_id=1, source_target_pairs={{0,1},{1,0},{2,3},{3,2},{4,5},{5,4},{6,7},{7,6},{8,9},{9,8},{10,11... | collective-permute-start | bytes 1179656 | tf_op jit(solution)/shard_map/ppermute | solution.py:19
  327.2 21.1 %collective-permute-start.59 = (bf16[2,512,256]{2,1,0:T(8,128)(2,1)S(1)}, bf16[2,512,256]{2,1,0:T(8,128)(2,1)S(1)}, u32[]{:S(2)}, u32[]{:S(2)}) collective-permute-start(bf16[2,512,256]{2,1,0:T(8,128)(2,1)S(1)} %add_convert_fusion.12), channel_id=1, source_target_pairs={{0,2},{1,3},{2,0},{3,1},{4,6},{5,7},{6,4},{7,5},{8,10},{9,11},{10,... | collective-permute-start | bytes 1572872 | tf_op jit(solution)/shard_map/ppermute | solution.py:19
  368.4 36.2 %collective-permute-start.62 = (bf16[512,512]{1,0:T(8,128)(2,1)}, bf16[512,512]{1,0:T(8,128)(2,1)S(1)}, u32[]{:S(2)}, u32[]{:S(2)}) collective-permute-start(bf16[512,512]{1,0:T(8,128)(2,1)} %get-tuple-element.119), channel_id=1, source_target_pairs={{0,1},{1,0},{2,3},{3,2},{4,5},{5,4},{6,7},{7,6},{8,9},{9,8},{10,11... | collective-permute-start | bytes 1572872 | tf_op jit(solution)/shard_map/ppermute | solution.py:19
  368.9 39.0 %collective-permute-start.74 = (bf16[512,512]{1,0:T(8,128)(2,1)}, bf16[512,512]{1,0:T(8,128)(2,1)S(1)}, u32[]{:S(2)}, u32[]{:S(2)}) collective-permute-start(bf16[512,512]{1,0:T(8,128)(2,1)} %get-tuple-element.125), channel_id=1, source_target_pairs={{0,1},{1,0},{2,3},{3,2},{4,5},{5,4},{6,7},{7,6},{8,9},{9,8},{10,11... | collective-permute-start | bytes 1572872 | tf_op jit(solution)/shard_map/ppermute | solution.py:19
  375.0 30.6 %collective-permute-start.63 = (bf16[512,512]{1,0:T(8,128)(2,1)S(1)}, bf16[512,512]{1,0:T(8,128)(2,1)S(1)}, u32[]{:S(2)}, u32[]{:S(2)}) collective-permute-start(bf16[512,512]{1,0:T(8,128)(2,1)S(1)} %add_convert_fusion.11), channel_id=1, source_target_pairs={{0,2},{1,3},{2,0},{3,1},{4,6},{5,7},{6,4},{7,5},{8,10},{9,11},{10,... | collective-permute-start | bytes 1572872 | tf_op jit(solution)/shard_map/ppermute | solution.py:19
  376.1 19.9 %collective-permute-start.61 = (bf16[256,512]{1,0:T(8,128)(2,1)S(1)}, bf16[256,512]{1,0:T(8,128)(2,1)S(1)}, u32[]{:S(2)}, u32[]{:S(2)}) collective-permute-start(bf16[256,512]{1,0:T(8,128)(2,1)S(1)} %slice.1832), channel_id=1, source_target_pairs={{0,4},{4,0},{8,12},{12,8},{16,20},{20,16},{24,28},{28,24},{1,5},{5... | collective-permute-start | bytes 786440 | tf_op jit(solution)/shard_map/ppermute | solution.py:19
  404.0 21.2 %collective-permute-start.68 = (bf16[256,640]{1,0:T(8,128)(2,1)S(1)}, bf16[256,640]{1,0:T(8,128)(2,1)S(1)}, u32[]{:S(2)}, u32[]{:S(2)}) collective-permute-start(bf16[256,640]{1,0:T(8,128)(2,1)S(1)} %slice.1330), channel_id=1, source_target_pairs={{0,4},{4,0},{8,12},{12,8},{16,20},{20,16},{24,28},{28,24},{1,5},{5... | collective-permute-start | bytes 983048 | tf_op jit(solution)/shard_map/ppermute | solution.py:19
  404.7 20.5 %collective-permute-start.71 = (bf16[256,640]{1,0:T(8,128)(2,1)S(1)}, bf16[256,640]{1,0:T(8,128)(2,1)S(1)}, u32[]{:S(2)}, u32[]{:S(2)}) collective-permute-start(bf16[256,640]{1,0:T(8,128)(2,1)S(1)} %add_convert_fusion.17), channel_id=1, source_target_pairs={{0,2},{1,3},{2,0},{3,1},{4,6},{5,7},{6,4},{7,5},{8,10},{9,11},{10,... | collective-permute-start | bytes 983048 | tf_op jit(solution)/shard_map/ppermute | solution.py:19
  (177 other events, 1427.3 us)

commit v4 on v3

--- a/solution.py
+++ b/solution.py
@@ -900,9 +900,9 @@
         *up_list,
         *down_list,
     )
-    up_marks = []
-    own_up = scatter_groups(dict(enumerate(early_grads[:mp_n])), order_a, up_marks)
-    own_down = scatter_groups(dict(enumerate(early_grads[mp_n:])), order_b)
+    own_up = scatter_groups(dict(enumerate(early_grads[:mp_n])), order_a)
+    down_marks = []
+    own_down = scatter_groups(dict(enumerate(early_grads[mp_n:])), order_b, down_marks)
 
     def returned(own, away):
         other = flip_pair(away, "dp", 0).astype(own.dtype)
@@ -915,7 +915,7 @@
     tail = own_att[:, 3 * head_width :]
     per_channel = tail[bias_rows : bias_rows + channel_part]
     natural = lax.dot_general(
-        tied(d_start, up_marks[0][1 << top_bit]), choice.astype(F32), NT, precision=lax.Precision.HIGHEST
+        tied(d_start, down_marks[1][1 << top_bit]), choice.astype(F32), NT, precision=lax.Precision.HIGHEST
     )
     final_rows = mm_nt(final_rows, choice).astype(BF16)
     return (

time: 450 us -> 456 us (1.013)
  waiting for transfers between devices: 141 us -> 148 us
    ppermute x88, waiting for transfers between devices: 137 us -> 144 us  [flip_pair(): lax.ppermute(value, axis, [(i, i ^ 1 << bit) for i in range(lax.axis_size...]
  transfers between devices with their start and end apart: 92 -> 92, of which waited for: 37 -> 41; matrix products, arithmetic and copies ran while one was open for 19% -> 19% of each run, Pallas kernels for 25% -> 25%
where the time goes in v4:
time: 456 us; the launch traced here: 448 us
  waiting for transfers between devices  148 us (32%)
  Pallas kernels  128 us (28%)
  starting transfers between devices  76 us (17%)
  other arithmetic  43.3 us (9%)
  local copies, waits for them, and re-layouts  41.2 us (9%)
  matrix products  8.01 us (2%)
    ppermute x88, waiting for transfers between devices, flip_pair(): lax.ppermute(value, axis, [(i, i ^ 1 << bit) for i in range(lax.axis_size...  144 us
    ppermute x88, starting transfers between devices, flip_pair(): lax.ppermute(value, axis, [(i, i ^ 1 << bit) for i in range(lax.axis_size...  72.8 us
    pallas_call x2, Pallas kernels, attend_backward(): pl.pallas_call(functools.partial(attend_backward_kernel, pieces, heads),...  45.4 us
    pallas_call x6, Pallas kernels, call_kernel(): pl.pallas_call(kernel, out_shape=[jax.ShapeDtypeStruct(shape, dtype) for...  40.9 us
    pallas_call x2, Pallas kernels, attend_forward(): pl.pallas_call(functools.partial(attend_forward_kernel, pieces, heads), o...  26.2 us
    pallas_call x1, Pallas kernels, block_step(): pl.pallas_call(functools.partial(turn_kernel, groups, batch_rows), out_sh...  15.9 us
  transfers between devices with their start and end apart: 92, of which 41 were waited for; matrix products, arithmetic and copies ran while one was open for 19% of the time, Pallas kernels for 25%

profile of v4, /device:TPU:0, one launch (start us, length us, event | category | flops | bytes accessed | tf_op | source)
XLA Modules:
  0.0 447.8 jit_solution(12173957131369101965)
XLA Ops:
  2.2 4.1 collective-permute-start.20
  31.7 3.3 collective-permute-done.14
  42.1 3.7 collective-permute-done.9
  47.4 4.0 collective-permute-done.2
  63.1 8.7 %collective-permute-done.4.refs_2_ = bf16[512,512]{1,0:T(8,128)(2,1)S(1)} collective-permute-done((bf16[512,512]{1,0:T(8,128)(2,1)S(1)}, bf16[512,512]{1,0:T(8,128)(2,1)S(1)}, u32[]{:S(2)}, u32[]{:S(2)}) %collective-permute-start.4) | collective-permute-done | bytes 524320 | tf_op jit(solution)/shard_map/ppermute | solution.py:19
  77.8 6.1 %shard_map.254.v_ref = f32[512,512]{1,0:T(8,128)} custom-call(f32[512,512]{1,0:T(8,128)} %fusion.103.v_ref, f32[1,512]{1,0:T(1,128)} %slice.869.gain_ref, bf16[512,512]{1,0:T(8,128)(2,1)} %copy-done.16, bf16[512,512]{1,0:T(8,128)(2,1)} %copy-done.17, bf16[512,512]{1,0:T(8,128)(2,1)} %collective-permute-done.11.refs_2_, ...), custom_call_target="tpu_custom_call" | custom-call | tf_op jit(solution)/shard_map/pallas_call | solution.py:193
  85.7 4.1 shard_map.255
  95.0 14.1 %collective-permute-done.24 = bf16[256,512]{1,0:T(8,128)(2,1)S(1)} collective-permute-done((bf16[256,512]{1,0:T(8,128)(2,1)S(1)}, bf16[256,512]{1,0:T(8,128)(2,1)S(1)}, u32[]{:S(2)}, u32[]{:S(2)}) %collective-permute-start.24) | collective-permute-done | bytes 262176 | tf_op jit(solution)/shard_map/ppermute | solution.py:19
  132.9 13.2 %attend_forward.2 = (bf16[512,256]{1,0:T(8,128)(2,1)}, f32[2,1,1024]{2,1,0:T(1,128)}, f32[512,256]{1,0:T(8,128)}) custom-call(s32[4]{0:T(128)} %add.465.qpos, s32[8]{0:T(128)} %stack.211.kpos, bf16[512,512]{1,0:T(8,128)(2,1)} %get-tuple-element.74.q_ref, f32[4,2,33,128]{3,2,1,0:T(8,128)} %pad.19.line_ref, ...), custom_call_target="tpu_custom_call" | custom-call | tf_op jit(solution)/shard_map/attend_forward/pallas_call | solution.py:537
  146.1 3.9 collective-permute-done.44.refs_6_
  151.6 13.0 %attend_forward.3 = (bf16[512,256]{1,0:T(8,128)(2,1)}, f32[2,1,1024]{2,1,0:T(1,128)}, f32[512,256]{1,0:T(8,128)}) custom-call(s32[4]{0:T(128)} %add.465.qpos, s32[8]{0:T(128)} %stack.211.kpos, bf16[512,512]{1,0:T(8,128)(2,1)} %get-tuple-element.74.q_ref, f32[4,2,33,128]{3,2,1,0:T(8,128)} %pad.19.line_ref, ...), custom_call_target="tpu_custom_call" | custom-call | tf_op jit(solution)/shard_map/attend_forward/pallas_call | solution.py:537
  164.6 4.6 %shard_map.256 = (f32[512,512]{1,0:T(8,128)}, f32[512,512]{1,0:T(8,128)}, f32[512,512]{1,0:T(8,128)}, bf16[512,512]{1,0:T(8,128)(2,1)}) custom-call(f32[512,512]{1,0:T(8,128)} %shard_map.254.v_ref, f32[1,512]{1,0:T(1,128)} %slice.871.gain_ref, bf16[512,512]{1,0:T(8,128)(2,1)} %pad_maximum_fusion.7.refs_0_, bf16[512,512]{1,0:T(8,128)(2,1)} %collective-permute-done.23.refs_1_, ...), custom_call_target="tpu_custom_call" | custom-call | tf_op jit(solution)/shard_map/pallas_call | solution.py:193
  176.2 5.4 %fusion.141 = (f32[512]{0:T(512)S(1)}, f32[512]{0:T(512)S(1)}, f32[2,256,512]{2,1,0:T(8,128)}) fusion(f32[2,286,512]{2,1,0:T(8,128)S(1)} %maximum_convert_fusion, f32[512]{0:T(512)S(1)} %bitcast.292, f32[512]{0:T(512)S(1)} %bitcast.294, f32[512]{0:T(512)S(1)} %bitcast.296, f32[512]{0:T(512)S(1)} %bitcast.298, f32[512]{0:T(512)S(1)} %bitcast.300, ...), kind=kLoop, calls=%fused_computation.378 | loop fusion | flops 16776192 | bytes 33622016 | tf_op jit(solution)/shard_map/reduce_sum | solution.py:777
  196.3 15.9 %turn.1 = (bf16[512,512]{1,0:T(8,128)(2,1)}, f32[512,512]{1,0:T(8,128)}, f32[512,512]{1,0:T(8,128)}, f32[2,512]{1,0:T(2,128)}, f32[2,512]{1,0:T(2,128)}, /*index...) custom-call(f32[512,512]{1,0:T(8,128)} %bitcast.217, ...), custom_call_target="tpu_custom_call" | custom-call | tf_op jit(solution)/shard_map/turn/pallas_call | solution.py:783
  226.2 3.4 multiply_reduce_fusion
  237.1 5.5 %fusion.14 = f32[2,256,512]{2,1,0:T(8,128)} fusion(f32[2,15,512]{2,1,0:T(8,128)S(1)} %get-tuple-element.342, f32[2,15,512]{2,1,0:T(8,128)S(1)} %get-tuple-element.341, f32[2,256,512]{2,1,0:T(8,128)S(1)} %bitcast.216, f32[512]{0:T(512)S(1)} %bitcast.293, f32[512]{0:T(512)S(1)} %bitcast.295, f32[512]{0:T(512)S(1)} %bitcast.297, f32[512]{0:T(512)S(1)} %bitcast.299, ...), kind=kLoop, calls=%fused_computation.56 | loop fusion | flops 23855104 | bytes 2283520 | tf_op jit(solution)/shard_map/add | solution.py:809
  242.9 6.8 %shard_map.257 = (f32[512,512]{1,0:T(8,128)}, f32[1,512]{1,0:T(1,128)}, bf16[512,512]{1,0:T(8,128)(2,1)}, bf16[512,384]{1,0:T(8,128)(2,1)}, bf16[512,384]{1,0:T(...) custom-call(f32[512,512]{1,0:T(8,128)} %bitcast.219, f32[512,512]{1,0:T(8,128)} %get-tuple-element.89.lin_ref, ...), custom_call_target="tpu_custom_call" | custom-call | tf_op jit(solution)/shard_map/pallas_call | solution.py:193
  253.7 22.4 %attend_backward.3 = (bf16[512,256]{1,0:T(8,128)(2,1)}, bf16[2,512,256]{2,1,0:T(8,128)(2,1)}, bf16[2,512,256]{2,1,0:T(8,128)(2,1)}, bf16[2,512,256]{2,1,0:T(8,12...) custom-call(s32[4]{0:T(128)} %add.465.qpos, s32[8]{0:T(128)} %stack.211.kpos, ...), custom_call_target="tpu_custom_call" | custom-call | tf_op jit(solution)/shard_map/attend_backward/pallas_call | solution.py:577
  276.1 23.1 %attend_backward.2 = (bf16[512,256]{1,0:T(8,128)(2,1)}, bf16[2,512,256]{2,1,0:T(8,128)(2,1)}, bf16[2,512,256]{2,1,0:T(8,128)(2,1)}, bf16[2,512,256]{2,1,0:T(8,12...) custom-call(s32[4]{0:T(128)} %add.465.qpos, s32[8]{0:T(128)} %stack.211.kpos, ...), custom_call_target="tpu_custom_call" | custom-call | tf_op jit(solution)/shard_map/attend_backward/pallas_call | solution.py:577
  305.2 4.5 %collective-permute-done.83 = bf16[256,384]{1,0:T(8,128)(2,1)S(1)} collective-permute-done((bf16[256,384]{1,0:T(8,128)(2,1)S(1)}, bf16[256,384]{1,0:T(8,128)(2,1)S(1)}, u32[]{:S(2)}, u32[]{:S(2)}) %collective-permute-start.83) | collective-permute-done | bytes 196640 | tf_op jit(solution)/shard_map/ppermute | solution.py:19
  316.9 4.0 collective-permute-done.85
  323.9 3.3 collective-permute-done.86
  329.3 8.5 %collective-permute-done.56.refs_12_ = bf16[2,512,256]{2,1,0:T(8,128)(2,1)S(1)} collective-permute-done((bf16[2,512,256]{2,1,0:T(8,128)(2,1)S(1)}, bf16[2,512,256]{2,1,0:T(8,128)(2,1)S(1)}, u32[]{:S(2)}, u32[]{:S(2)}) %collective-permute-start.56) | collective-permute-done | bytes 524320 | tf_op jit(solution)/shard_map/ppermute | solution.py:19
  337.8 10.5 %collective-permute-done.59.refs_15_ = bf16[2,512,256]{2,1,0:T(8,128)(2,1)S(1)} collective-permute-done((bf16[2,512,256]{2,1,0:T(8,128)(2,1)S(1)}, bf16[2,512,256]{2,1,0:T(8,128)(2,1)S(1)}, u32[]{:S(2)}, u32[]{:S(2)}) %collective-permute-start.59) | collective-permute-done | bytes 524320 | tf_op jit(solution)/shard_map/ppermute | solution.py:19
  349.1 7.4 %shard_map.258 = (f32[512,512]{1,0:T(8,128)}, f32[1,512]{1,0:T(1,128)}, bf16[512,512]{1,0:T(8,128)(2,1)}, bf16[512,512]{1,0:T(8,128)(2,1)}, bf16[512,512]{1,0:T(8,128)(2,1)}, /*index=5*/bf16[512,512]{1,0:T(8,128)(2,1)}) custom-call(f32[512,512]{1,0:T(8,128)} %shard_map.254.v_ref, f32[512,512]{1,0:T(8,128)} %get-tuple-element.92.d_ref, ...), custom_call_target="tpu_custom_call" | custom-call | tf_op jit(solution)/shard_map/pallas_call | solution.py:193
  356.5 11.9 %shard_map.259 = (f32[512,512]{1,0:T(8,128)}, bf16[512,512]{1,0:T(8,128)(2,1)}, bf16[512,512]{1,0:T(8,128)(2,1)}, bf16[512,512]{1,0:T(8,128)(2,1)}, bf16[512,512...) custom-call(f32[512,512]{1,0:T(8,128)} %fusion.103.v_ref, ...), custom_call_target="tpu_custom_call" | custom-call | tf_op jit(solution)/shard_map/pallas_call | solution.py:193
  376.3 12.1 %collective-permute-done.89 = bf16[256,1152]{1,0:T(8,128)(2,1)S(1)} collective-permute-done((bf16[256,1152]{1,0:T(8,128)(2,1)S(1)}, bf16[256,1152]{1,0:T(8,128)(2,1)S(1)}, u32[]{:S(2)}, u32[]{:S(2)}) %collective-permute-start.89) | collective-permute-done | bytes 589856 | tf_op jit(solution)/shard_map/ppermute | solution.py:19
  389.2 8.3 %collective-permute-done.61 = bf16[256,640]{1,0:T(8,128)(2,1)S(1)} collective-permute-done((bf16[256,640]{1,0:T(8,128)(2,1)S(1)}, bf16[256,640]{1,0:T(8,128)(2,1)S(1)}, u32[]{:S(2)}, u32[]{:S(2)}) %collective-permute-start.61) | collective-permute-done | bytes 327712 | tf_op jit(solution)/shard_map/ppermute | solution.py:19
  400.0 5.2 %collective-permute-done.90 = bf16[128,1152]{1,0:T(8,128)(2,1)S(1)} collective-permute-done((bf16[128,1152]{1,0:T(8,128)(2,1)S(1)}, bf16[128,1152]{1,0:T(8,128)(2,1)S(1)}, u32[]{:S(2)}, u32[]{:S(2)}) %collective-permute-start.90) | collective-permute-done | bytes 294944 | tf_op jit(solution)/shard_map/ppermute | solution.py:19
  411.5 4.7 %collective-permute-done.91 = bf16[64,1152]{1,0:T(8,128)(2,1)S(1)} collective-permute-done((bf16[64,1152]{1,0:T(8,128)(2,1)S(1)}, bf16[64,1152]{1,0:T(8,128)(2,1)S(1)}, u32[]{:S(2)}, u32[]{:S(2)}) %collective-permute-start.91) | collective-permute-done | bytes 147488 | tf_op jit(solution)/shard_map/ppermute | solution.py:19
  418.1 3.3 collective-permute-done.62
  422.5 4.0 collective-permute-done.66
  (600 shorter events, 191.8 us)
Async XLA Ops:
  2.2 27.2 %collective-permute-start.20 = (bf16[64,512]{1,0:T(8,128)(2,1)S(1)}, bf16[64,512]{1,0:T(8,128)(2,1)S(1)}, u32[]{:S(2)}, u32[]{:S(2)}) collective-permute-start(bf16[64,512]{1,0:T(8,128)(2,1)S(1)} %pad_maximum_fusion.23), channel_id=1, source_target_pairs={{0,16},{4,20},{8,24},{12,28},{16,0},{20,4},{24,8},{28,12},{1,17},{... | collective-permute-start | bytes 196616 | tf_op jit(solution)/shard_map/ppermute | solution.py:19
  13.9 24.9 %collective-permute-start.40 = (bf16[64,1024]{1,0:T(8,128)(2,1)S(1)}, bf16[64,1024]{1,0:T(8,128)(2,1)S(1)}, u32[]{:S(2)}, u32[]{:S(2)}) collective-permute-start(bf16[64,1024]{1,0:T(8,128)(2,1)S(1)} %pad_maximum_fusion.21), channel_id=1, source_target_pairs={{0,16},{4,20},{8,24},{12,28},{16,0},{20,4},{24,8},{28,12},{1,17},{... | collective-permute-start | bytes 393224 | tf_op jit(solution)/shard_map/ppermute | solution.py:19
  25.5 34.9 %collective-permute-start.6 = (bf16[256,512]{1,0:T(8,128)(2,1)}, bf16[256,512]{1,0:T(8,128)(2,1)S(1)}, u32[]{:S(2)}, u32[]{:S(2)}) collective-permute-start(bf16[256,512]{1,0:T(8,128)(2,1)} %get-tuple-element.216), channel_id=1, source_target_pairs={{0,4},{4,0},{8,12},{12,8},{16,20},{20,16},{24,28},{28,24},{1,5},{5... | collective-permute-start | bytes 786440 | tf_op jit(solution)/shard_map/ppermute | solution.py:19
  38.8 17.2 %collective-permute-start.15 = (bf16[256,512]{1,0:T(8,128)(2,1)S(1)}, bf16[256,512]{1,0:T(8,128)(2,1)S(1)}, u32[]{:S(2)}, u32[]{:S(2)}) collective-permute-start(bf16[256,512]{1,0:T(8,128)(2,1)S(1)} %pad_maximum_fusion.12), channel_id=1, source_target_pairs={{0,4},{4,0},{8,12},{12,8},{16,20},{20,16},{24,28},{28,24},{1,5},{5... | collective-permute-start | bytes 786440 | tf_op jit(solution)/shard_map/ppermute | solution.py:19
  41.4 17.4 %collective-permute-start.18 = (bf16[256,512]{1,0:T(8,128)(2,1)S(1)}, bf16[256,512]{1,0:T(8,128)(2,1)S(1)}, u32[]{:S(2)}, u32[]{:S(2)}) collective-permute-start(bf16[256,512]{1,0:T(8,128)(2,1)S(1)} %collective-permute-done.17), channel_id=1, source_target_pairs={{0,4},{4,0},{8,12},{12,8},{16,20},{20,16},{24,28},{28,24},{1,5},{5... | collective-permute-start | bytes 786440 | tf_op jit(solution)/shard_map/ppermute | solution.py:19
  62.6 21.5 %collective-permute-start.3 = (bf16[512,512]{1,0:T(8,128)(2,1)S(1)}, bf16[512,512]{1,0:T(8,128)(2,1)S(1)}, u32[]{:S(2)}, u32[]{:S(2)}) collective-permute-start(bf16[512,512]{1,0:T(8,128)(2,1)S(1)} %pad_maximum_fusion.4.refs_0_), channel_id=1, source_target_pairs={{0,1},{1,0},{2,3},{3,2},{4,5},{5,4},{6,7},{7,6},{8,9},{9,8},{10,11... | collective-permute-start | bytes 1572872 | tf_op jit(solution)/shard_map/ppermute | solution.py:19
  72.8 19.6 %collective-permute-start.33 = (bf16[256,512]{1,0:T(8,128)(2,1)}, bf16[256,512]{1,0:T(8,128)(2,1)}, u32[]{:S(2)}, u32[]{:S(2)}) collective-permute-start(bf16[256,512]{1,0:T(8,128)(2,1)} %get-tuple-element.214), channel_id=1, source_target_pairs={{0,4},{4,0},{8,12},{12,8},{16,20},{20,16},{24,28},{28,24},{1,5},{5... | collective-permute-start | bytes 786440 | tf_op jit(solution)/shard_map/ppermute | solution.py:19
  73.6 17.5 %collective-permute-start.21 = (bf16[128,512]{1,0:T(8,128)(2,1)}, bf16[128,512]{1,0:T(8,128)(2,1)S(1)}, u32[]{:S(2)}, u32[]{:S(2)}) collective-permute-start(bf16[128,512]{1,0:T(8,128)(2,1)} %pad_maximum_fusion.20), channel_id=1, source_target_pairs={{0,8},{4,12},{8,0},{12,4},{16,24},{20,28},{24,16},{28,20},{1,9},{5... | collective-permute-start | bytes 393224 | tf_op jit(solution)/shard_map/ppermute | solution.py:19
  76.3 38.5 %collective-permute-start.42 = (bf16[256,1024]{1,0:T(8,128)(2,1)}, bf16[256,1024]{1,0:T(8,128)(2,1)}, u32[]{:S(2)}, u32[]{:S(2)}) collective-permute-start(bf16[256,1024]{1,0:T(8,128)(2,1)} %pad_maximum_fusion.8), channel_id=1, source_target_pairs={{0,4},{4,0},{8,12},{12,8},{16,20},{20,16},{24,28},{28,24},{1,5},{5... | collective-permute-start | bytes 1572872 | tf_op jit(solution)/shard_map/ppermute | solution.py:19
  89.8 23.7 %collective-permute-start.27 = (bf16[2,512,256]{2,1,0:T(8,128)(2,1)}, bf16[2,512,256]{2,1,0:T(8,128)(2,1)S(1)}, u32[]{:S(2)}, u32[]{:S(2)}) collective-permute-start(bf16[2,512,256]{2,1,0:T(8,128)(2,1)} %get-tuple-element.76.refs_0_.refs_4_), channel_id=1, source_target_pairs={{0,2},{1,3},{2,0},{3,1},{4,6},{5,7},{6,4},{7,5},{8,10},{9,11},{10,... | collective-permute-start | bytes 1572872 | tf_op jit(solution)/shard_map/ppermute | solution.py:19
  91.1 17.9 %collective-permute-start.24 = (bf16[256,512]{1,0:T(8,128)(2,1)S(1)}, bf16[256,512]{1,0:T(8,128)(2,1)S(1)}, u32[]{:S(2)}, u32[]{:S(2)}) collective-permute-start(bf16[256,512]{1,0:T(8,128)(2,1)S(1)} %pad_maximum_fusion.13), channel_id=1, source_target_pairs={{0,2},{1,3},{2,0},{3,1},{4,6},{5,7},{6,4},{7,5},{8,10},{9,11},{10,... | collective-permute-start | bytes 786440 | tf_op jit(solution)/shard_map/ppermute | solution.py:19
  91.9 17.7 %collective-permute-start.22 = (bf16[256,512]{1,0:T(8,128)(2,1)S(1)}, bf16[256,512]{1,0:T(8,128)(2,1)S(1)}, u32[]{:S(2)}, u32[]{:S(2)}) collective-permute-start(bf16[256,512]{1,0:T(8,128)(2,1)S(1)} %pad_maximum_fusion.13), channel_id=1, source_target_pairs={{0,4},{4,0},{8,12},{12,8},{16,20},{20,16},{24,28},{28,24},{1,5},{5... | collective-permute-start | bytes 786440 | tf_op jit(solution)/shard_map/ppermute | solution.py:19
  112.9 51.7 %collective-permute-start.23 = (bf16[512,512]{1,0:T(8,128)(2,1)}, bf16[512,512]{1,0:T(8,128)(2,1)}, u32[]{:S(2)}, u32[]{:S(2)}) collective-permute-start(bf16[512,512]{1,0:T(8,128)(2,1)} %pad_maximum_fusion.7.refs_0_), channel_id=1, source_target_pairs={{0,1},{1,0},{2,3},{3,2},{4,5},{5,4},{6,7},{7,6},{8,9},{9,8},{10,11... | collective-permute-start | bytes 1572872 | tf_op jit(solution)/shard_map/ppermute | solution.py:19
  117.0 33.0 %collective-permute-start.44 = (bf16[512,1024]{1,0:T(8,128)(2,1)}, bf16[512,1024]{1,0:T(8,128)(2,1)}, u32[]{:S(2)}, u32[]{:S(2)}) collective-permute-start(bf16[512,1024]{1,0:T(8,128)(2,1)} %pad_maximum_fusion.2.refs_4_), channel_id=1, source_target_pairs={{0,2},{1,3},{2,0},{3,1},{4,6},{5,7},{6,4},{7,5},{8,10},{9,11},{10,... | collective-permute-start | bytes 3145736 | tf_op jit(solution)/shard_map/ppermute | solution.py:19
  125.0 39.6 %collective-permute-start.26 = (bf16[512,512]{1,0:T(8,128)(2,1)S(1)}, bf16[512,512]{1,0:T(8,128)(2,1)}, u32[]{:S(2)}, u32[]{:S(2)}) collective-permute-start(bf16[512,512]{1,0:T(8,128)(2,1)S(1)} %constant_dynamic-update-slice_fusion.6.refs_2_), channel_id=1, source_target_pairs={{0,1},{1,0},{2,3},{3,2},{4,5},{5,4},{6,7},{7,6},{8,9},{9,8},{10,11... | collective-permute-start | bytes 1572872 | tf_op jit(solution)/shard_map/ppermute | solution.py:19
  128.4 21.6 %collective-permute-start.31 = (bf16[2,512,256]{2,1,0:T(8,128)(2,1)S(1)}, bf16[2,512,256]{2,1,0:T(8,128)(2,1)S(1)}, u32[]{:S(2)}, u32[]{:S(2)}) collective-permute-start(bf16[2,512,256]{2,1,0:T(8,128)(2,1)S(1)} %copy-done.4), channel_id=1, source_target_pairs={{0,1},{1,0},{2,3},{3,2},{4,5},{5,4},{6,7},{7,6},{8,9},{9,8},{10,11... | collective-permute-start | bytes 1572872 | tf_op jit(solution)/shard_map/ppermute | solution.py:19
  128.4 22.1 %collective-permute-start.32 = (bf16[2,512,256]{2,1,0:T(8,128)(2,1)}, bf16[2,512,256]{2,1,0:T(8,128)(2,1)S(1)}, u32[]{:S(2)}, u32[]{:S(2)}) collective-permute-start(bf16[2,512,256]{2,1,0:T(8,128)(2,1)} %collective-permute-done.30.refs_1_.refs_5_), channel_id=1, source_target_pairs={{0,1},{1,0},{2,3},{3,2},{4,5},{5,4},{6,7},{7,6},{8,9},{9,8},{10,11... | collective-permute-start | bytes 1572872 | tf_op jit(solution)/shard_map/ppermute | solution.py:19
  150.0 45.3 %collective-permute-start.43 = (bf16[512,1024]{1,0:T(8,128)(2,1)}, bf16[512,1024]{1,0:T(8,128)(2,1)}, u32[]{:S(2)}, u32[]{:S(2)}) collective-permute-start(bf16[512,1024]{1,0:T(8,128)(2,1)} %pad_maximum_fusion.2.refs_4_), channel_id=1, source_target_pairs={{0,1},{1,0},{2,3},{3,2},{4,5},{5,4},{6,7},{7,6},{8,9},{9,8},{10,11... | collective-permute-start | bytes 3145736 | tf_op jit(solution)/shard_map/ppermute | solution.py:19
  150.0 45.3 %collective-permute-start.45 = (bf16[512,1024]{1,0:T(8,128)(2,1)}, bf16[512,1024]{1,0:T(8,128)(2,1)S(1)}, u32[]{:S(2)}, u32[]{:S(2)}) collective-permute-start(bf16[512,1024]{1,0:T(8,128)(2,1)} %collective-permute-done.44.refs_6_), channel_id=1, source_target_pairs={{0,1},{1,0},{2,3},{3,2},{4,5},{5,4},{6,7},{7,6},{8,9},{9,8},{10,11... | collective-permute-start | bytes 3145736 | tf_op jit(solution)/shard_map/ppermute | solution.py:19
  223.5 27.2 %collective-permute-start.46 = (bf16[256,512]{1,0:T(8,128)(2,1)}, bf16[256,512]{1,0:T(8,128)(2,1)}, u32[]{:S(2)}, u32[]{:S(2)}) collective-permute-start(bf16[256,512]{1,0:T(8,128)(2,1)} %slice.1219), channel_id=1, source_target_pairs={{0,4},{4,0},{8,12},{12,8},{16,20},{20,16},{24,28},{28,24},{1,5},{5... | collective-permute-start | bytes 786440 | tf_op jit(solution)/shard_map/ppermute | solution.py:19
  224.9 17.6 %collective-permute-start.53 = (bf16[512,1152]{1,0:T(8,128)(2,1)}, bf16[512,1152]{1,0:T(8,128)(2,1)S(1)}, u32[]{:S(2)}, u32[]{:S(2)}) collective-permute-start(bf16[512,1152]{1,0:T(8,128)(2,1)} %get-tuple-element.87), channel_id=1, source_target_pairs={{0,1},{1,0},{2,3},{3,2},{4,5},{5,4},{6,7},{7,6},{8,9},{9,8},{10,11... | collective-permute-start | bytes 3538952 | tf_op jit(solution)/shard_map/ppermute | solution.py:19
  224.9 144.1 %collective-permute-start.87 = (bf16[512,1152]{1,0:T(8,128)(2,1)}, bf16[512,1152]{1,0:T(8,128)(2,1)}, u32[]{:S(2)}, u32[]{:S(2)}) collective-permute-start(bf16[512,1152]{1,0:T(8,128)(2,1)} %get-tuple-element.133), channel_id=1, source_target_pairs={{0,1},{1,0},{2,3},{3,2},{4,5},{5,4},{6,7},{7,6},{8,9},{9,8},{10,11... | collective-permute-start | bytes 3538952 | tf_op jit(solution)/shard_map/ppermute | solution.py:19
  249.6 52.1 %collective-permute-start.82 = (bf16[512,384]{1,0:T(8,128)(2,1)}, bf16[512,384]{1,0:T(8,128)(2,1)S(1)}, u32[]{:S(2)}, u32[]{:S(2)}) collective-permute-start(bf16[512,384]{1,0:T(8,128)(2,1)} %get-tuple-element.131), channel_id=1, source_target_pairs={{0,1},{1,0},{2,3},{3,2},{4,5},{5,4},{6,7},{7,6},{8,9},{9,8},{10,11... | collective-permute-start | bytes 1179656 | tf_op jit(solution)/shard_map/ppermute | solution.py:19
  252.5 117.0 %collective-permute-start.88 = (bf16[512,1152]{1,0:T(8,128)(2,1)S(1)}, bf16[512,1152]{1,0:T(8,128)(2,1)S(1)}, u32[]{:S(2)}, u32[]{:S(2)}) collective-permute-start(bf16[512,1152]{1,0:T(8,128)(2,1)S(1)} %add_convert_fusion.2), channel_id=1, source_target_pairs={{0,2},{1,3},{2,0},{3,1},{4,6},{5,7},{6,4},{7,5},{8,10},{9,11},{10,... | collective-permute-start | bytes 3538952 | tf_op jit(solution)/shard_map/ppermute | solution.py:19
  253.6 49.8 %collective-permute-start.80 = (bf16[512,384]{1,0:T(8,128)(2,1)}, bf16[512,384]{1,0:T(8,128)(2,1)}, u32[]{:S(2)}, u32[]{:S(2)}) collective-permute-start(bf16[512,384]{1,0:T(8,128)(2,1)} %get-tuple-element.129), channel_id=1, source_target_pairs={{0,1},{1,0},{2,3},{3,2},{4,5},{5,4},{6,7},{7,6},{8,9},{9,8},{10,11... | collective-permute-start | bytes 1179656 | tf_op jit(solution)/shard_map/ppermute | solution.py:19
  327.2 21.1 %collective-permute-start.59 = (bf16[2,512,256]{2,1,0:T(8,128)(2,1)S(1)}, bf16[2,512,256]{2,1,0:T(8,128)(2,1)S(1)}, u32[]{:S(2)}, u32[]{:S(2)}) collective-permute-start(bf16[2,512,256]{2,1,0:T(8,128)(2,1)S(1)} %add_convert_fusion.12), channel_id=1, source_target_pairs={{0,2},{1,3},{2,0},{3,1},{4,6},{5,7},{6,4},{7,5},{8,10},{9,11},{10,... | collective-permute-start | bytes 1572872 | tf_op jit(solution)/shard_map/ppermute | solution.py:19
  368.4 37.4 %collective-permute-start.63 = (bf16[512,512]{1,0:T(8,128)(2,1)}, bf16[512,512]{1,0:T(8,128)(2,1)S(1)}, u32[]{:S(2)}, u32[]{:S(2)}) collective-permute-start(bf16[512,512]{1,0:T(8,128)(2,1)} %get-tuple-element.119), channel_id=1, source_target_pairs={{0,1},{1,0},{2,3},{3,2},{4,5},{5,4},{6,7},{7,6},{8,9},{9,8},{10,11... | collective-permute-start | bytes 1572872 | tf_op jit(solution)/shard_map/ppermute | solution.py:19
  368.9 39.5 %collective-permute-start.74 = (bf16[512,512]{1,0:T(8,128)(2,1)}, bf16[512,512]{1,0:T(8,128)(2,1)S(1)}, u32[]{:S(2)}, u32[]{:S(2)}) collective-permute-start(bf16[512,512]{1,0:T(8,128)(2,1)} %get-tuple-element.125), channel_id=1, source_target_pairs={{0,1},{1,0},{2,3},{3,2},{4,5},{5,4},{6,7},{7,6},{8,9},{9,8},{10,11... | collective-permute-start | bytes 1572872 | tf_op jit(solution)/shard_map/ppermute | solution.py:19
  373.7 33.0 %collective-permute-start.65 = (bf16[512,512]{1,0:T(8,128)(2,1)S(1)}, bf16[512,512]{1,0:T(8,128)(2,1)S(1)}, u32[]{:S(2)}, u32[]{:S(2)}) collective-permute-start(bf16[512,512]{1,0:T(8,128)(2,1)S(1)} %add_convert_fusion.10), channel_id=1, source_target_pairs={{0,2},{1,3},{2,0},{3,1},{4,6},{5,7},{6,4},{7,5},{8,10},{9,11},{10,... | collective-permute-start | bytes 1572872 | tf_op jit(solution)/shard_map/ppermute | solution.py:19
  374.8 34.9 %collective-permute-start.76 = (bf16[512,512]{1,0:T(8,128)(2,1)S(1)}, bf16[512,512]{1,0:T(8,128)(2,1)S(1)}, u32[]{:S(2)}, u32[]{:S(2)}) collective-permute-start(bf16[512,512]{1,0:T(8,128)(2,1)S(1)} %add_convert_fusion.7), channel_id=1, source_target_pairs={{0,2},{1,3},{2,0},{3,1},{4,6},{5,7},{6,4},{7,5},{8,10},{9,11},{10,... | collective-permute-start | bytes 1572872 | tf_op jit(solution)/shard_map/ppermute | solution.py:19
  405.2 25.4 %collective-permute-start.70 = (bf16[256,640]{1,0:T(8,128)(2,1)S(1)}, bf16[256,640]{1,0:T(8,128)(2,1)S(1)}, u32[]{:S(2)}, u32[]{:S(2)}) collective-permute-start(bf16[256,640]{1,0:T(8,128)(2,1)S(1)} %slice.1332), channel_id=1, source_target_pairs={{0,4},{4,0},{8,12},{12,8},{16,20},{20,16},{24,28},{28,24},{1,5},{5... | collective-permute-start | bytes 983048 | tf_op jit(solution)/shard_map/ppermute | solution.py:19
  405.8 24.7 %collective-permute-start.71 = (bf16[256,640]{1,0:T(8,128)(2,1)S(1)}, bf16[256,640]{1,0:T(8,128)(2,1)S(1)}, u32[]{:S(2)}, u32[]{:S(2)}) collective-permute-start(bf16[256,640]{1,0:T(8,128)(2,1)S(1)} %add_convert_fusion.18), channel_id=1, source_target_pairs={{0,2},{1,3},{2,0},{3,1},{4,6},{5,7},{6,4},{7,5},{8,10},{9,11},{10,... | collective-permute-start | bytes 983048 | tf_op jit(solution)/shard_map/ppermute | solution.py:19
  (177 other events, 1477.0 us)
